TPU v7x, 32 devices: a whole 2x2x4 slice. The times are simulated.
32 devices in a mesh: narrow: 4 (over y, x), wide: 8 (over z, core).
Axes of the slice: x: 2, y: 2, z: 4, core: 2. Of those that a mesh axis runs over, the one named last changes fastest.
Arguments:
- tokens: bfloat16 [8192, 1024], P(('narrow', 'wide')), may hold values from -6 to 6
- attn_gain: float32 [1024], replicated, may hold values from 0.5 to 1.5
- qkv_weights: float32 [3, 1024, 1024], P(None, 'narrow', 'wide'), may hold values from -0.1875 to 0.1875
- out_weight: float32 [1024, 1024], P('narrow', 'wide'), may hold values from -1.75 to 1.75
- rel_bias: float32 [32, 16], replicated, may hold values from -6 to 6
- moe_gain: float32 [1024], replicated, may hold values from 0.5 to 1.5
- router: float32 [1024, 8], P('narrow', 'wide'), may hold values from -0.125 to 0.125
- gate_weight: float32 [4, 8, 1024, 704], P('narrow', 'wide'), may hold values from -0.1875 to 0.1875
- up_weight: float32 [4, 8, 1024, 704], P('narrow', 'wide'), may hold values from -0.1875 to 0.1875
- down_weight: float32 [4, 8, 704, 1024], P('narrow', 'wide'), may hold values from -0.21875 to 0.21875
- expert_ids: int32 [8192, 2], P(('narrow', 'wide')), may hold values from 0 to 7, as said below
- expert_slots: int32 [8192, 2], P(('narrow', 'wide')), may hold values from -1 to 79, as said below
- buckets: int32 [511], replicated, may hold values from 0 to 31, as said below
- upstream: bfloat16 [8192, 1024], P(('narrow', 'wide')), may hold values from -6 to 6
Outputs:
- block_out: bfloat16 [8192, 1024], P(('narrow', 'wide'))
- tokens_grad: bfloat16 [8192, 1024], P(('narrow', 'wide'))
- attn_gain_grad: float32 [1024], replicated
- qkv_grad: float32 [3, 1024, 1024], replicated
- out_weight_grad: float32 [1024, 1024], replicated
- rel_bias_grad: float32 [32, 16], replicated
- moe_gain_grad: float32 [1024], replicated
- router_grad: float32 [1024, 8], replicated
- gate_grad: float32 [4, 8, 1024, 704], P('narrow', 'wide')
- up_grad: float32 [4, 8, 1024, 704], P('narrow', 'wide')
- down_grad: float32 [4, 8, 704, 1024], P('narrow', 'wide')
- qkv_new: float32 [3, 1024, 1024], P(None, 'narrow', 'wide')
- out_weight_step: float32 [1024, 1024], P('narrow', 'wide')
- router_new: float32 [1024, 8], P('narrow', 'wide')
- gate_new: float32 [4, 8, 1024, 704], P('narrow', 'wide')
- up_new: float32 [4, 8, 1024, 704], P('narrow', 'wide')
- down_new: float32 [4, 8, 704, 1024], P('narrow', 'wide')
- qkv_stats: float32 [2, 3, 1024], replicated
- out_stats: float32 [2, 1024], replicated
- router_rows: float32 [1024], replicated
- router_cols: float32 [8], replicated
- expert_sum_stats: float32 [4, 8, 3, 1024], P('narrow', 'wide')
- expert_part_stats: float32 [4, 8, 3, 704], P('narrow', 'wide')
Inputs may be any that keep to these rules, and one draw needn't show every extreme that they name: `expert_ids`: each token names two different experts. `expert_slots`: among the pairs of one device's 256 tokens, taken in order of token and then choice, those naming the same expert hold slots 0, 1, 2 and so on; a pair whose slot would be 80 or more holds -1. `buckets`: entry j - i + 255 is the bucket of offset j - i: 0 at offset 0, never falling with the offset's size on either side, under 32 // 2 for offsets of 0 or less and 16 or more for positive ones.
All inputs are finite; a program needn't handle non-finite values.
Results may differ from a plain program's by a relative error of at most 0.02.
Values may be sent and summed in bfloat16 or wider, within the bound.
No kernel may reach another device: no remote copies, remote signals or barrier semaphores. Data moves between devices by JAX's collectives and lax.ppermute only.
A program may use at most 256 MiB of HBM per device.

v0:
```python
import jax
import jax.numpy as jnp
from jax import lax
from jax.sharding import PartitionSpec as P

NORM_EPS = 1e-06
STAT_EPS = 1e-06
STEP_RATE = 0.01


def from_partner(value, axis, stride):
    mask = 2**stride
    pairs = [(source, source ^ mask) for source in range(lax.axis_size(axis))]
    return lax.ppermute(value, axis, pairs)


def norm_apply(values, gain):
    factor = lax.rsqrt(jnp.mean(values * values, axis=-1, keepdims=True) + NORM_EPS)
    return values * factor * gain


def gelu_tanh(values):
    return jax.nn.gelu(values, approximate=True)


def adafactor_step(gradient, row_stats, col_stats, mean_rows):
    return (
        STEP_RATE
        * gradient
        / jnp.sqrt(row_stats[..., :, None] * col_stats[..., None, :] / mean_rows[..., None, None])
    )


def factored(weight, gradient, row_stats, col_stats, mean_rows):
    return weight - adafactor_step(gradient, row_stats, col_stats, mean_rows)


def on_device(
    tokens,
    attn_gain,
    qkv_weights,
    out_weight,
    rel_bias,
    moe_gain,
    router,
    gate_weight,
    up_weight,
    down_weight,
    expert_ids,
    expert_slots,
    buckets,
    upstream,
):
    length, features = tokens.shape
    bucket_count, head_count = rel_bias.shape
    head_dim = features // head_count
    score_scale = head_dim ** (-0.5)
    groups = lax.axis_size("narrow")
    wide_count = lax.axis_size("wide")
    part_width = gate_weight.shape[3]
    qkv_low = qkv_weights.astype(jnp.bfloat16)
    out_low = out_weight.astype(jnp.bfloat16)
    router_low = router.astype(jnp.bfloat16)
    qkv_cols, out_cols, router_cols_low = (
        lax.all_gather(qkv_low, "wide", axis=2, tiled=True),
        lax.all_gather(out_low, "wide", axis=1, tiled=True),
        lax.all_gather(router_low, "wide", axis=1, tiled=True),
    )
    full_qkv, full_out, full_router = (
        lax.all_gather(qkv_cols, "narrow", axis=1, tiled=True),
        lax.all_gather(out_cols, "narrow", axis=0, tiled=True),
        lax.all_gather(router_cols_low, "narrow", axis=0, tiled=True),
    )
    experts = full_router.shape[1]
    places = experts // groups
    split_parts = wide_count // places
    capacity = (10 * length // experts + 3) // 4
    slot_total = experts * capacity
    inputs = tokens.astype(jnp.float32)
    normed, attn_norm_back = jax.vjp(norm_apply, inputs, attn_gain)
    normed_in = normed.astype(jnp.bfloat16)
    projected = jnp.einsum(
        "td,kde->kte", normed_in, full_qkv, preferred_element_type=jnp.float32
    ).astype(jnp.bfloat16)
    query_heads = projected[0].reshape(length, head_count, head_dim)
    key_heads = projected[1].reshape(length, head_count, head_dim)
    value_heads = projected[2].reshape(length, head_count, head_dim)
    table_hot = (buckets[:, None] == jnp.arange(bucket_count)[None, :]).astype(jnp.float32)
    bias_table = jnp.dot(table_hot, rel_bias, precision=lax.Precision.HIGHEST).T
    block_rows = min(512, length)
    block_count = length // block_rows
    key_positions = jnp.arange(length, dtype=jnp.int32)
    bucket_ids = jnp.arange(bucket_count, dtype=jnp.int32)

    def offsets(first_row):
        return (
            key_positions[None, :]
            - (first_row + jnp.arange(block_rows, dtype=jnp.int32))[:, None]
            + length
            - 1
        )

    def block_scores(first_row):
        raw_scores = jnp.einsum(
            "qhd,khd->hqk", query_heads, key_heads, preferred_element_type=jnp.float32
        )
        return (
            query_heads,
            raw_scores * score_scale + jnp.take(bias_table, offsets(first_row), axis=1),
        )

    def forward_block(state_carry, step_index):
        row_heads, scores = block_scores(step_index * block_rows)
        row_max = jnp.max(scores, axis=-1, keepdims=True)
        totals = jnp.log(jnp.sum(jnp.exp(scores - row_max), axis=-1, keepdims=True)) + row_max
        probs_low = jnp.exp(scores - totals).astype(jnp.bfloat16)
        mixed_heads = jnp.einsum(
            "hqk,khd->qhd", probs_low, value_heads, preferred_element_type=jnp.float32
        )
        return (
            state_carry,
            (mixed_heads.reshape(block_rows, features).astype(jnp.bfloat16), totals),
        )

    unused, (attended, log_totals) = lax.scan(
        forward_block, jnp.int32(0), jnp.arange(block_count, dtype=jnp.int32)
    )
    attended = attended.reshape(length, features)
    hidden_x1 = inputs + jnp.dot(attended, full_out, preferred_element_type=jnp.float32)
    moe_normed, moe_norm_back = jax.vjp(norm_apply, hidden_x1, moe_gain)
    moe_input = moe_normed.astype(jnp.bfloat16)
    logits = jnp.dot(moe_input, full_router, preferred_element_type=jnp.float32)
    pick_mask = expert_ids[:, :, None] == jnp.arange(experts, dtype=jnp.int32)[None, None, :]
    picked = jnp.sum(jnp.where(pick_mask, logits[:, None, :], 0.0), axis=2)
    gate_values = jax.nn.softmax(picked, axis=1)
    kept_pairs = expert_slots >= 0
    keep_float = kept_pairs.astype(jnp.float32)
    owner_slot = expert_ids % groups * places + expert_ids // groups
    row_ids = jnp.where(kept_pairs, owner_slot * capacity + expert_slots, -1)
    route_hot = (
        jnp.arange(slot_total, dtype=jnp.int32)[:, None, None] == row_ids.T[None, :, :]
    ).astype(jnp.bfloat16)
    safe_rows = jnp.maximum(row_ids, 0)

    def spread(buffer):
        shaped = buffer.reshape(groups, places, 1, capacity, features)
        return jnp.broadcast_to(shaped, (groups, places, split_parts, capacity, features)).reshape(
            groups, wide_count, capacity, features
        )

    def gather_parts(received):
        return (
            received.reshape(groups, places, split_parts, capacity, features)
            .astype(jnp.float32)
            .sum(axis=2)
            .reshape(slot_total, features)
        )

    joined = jnp.concatenate([gate_weight[0, 0], up_weight[0, 0]], axis=1).astype(jnp.bfloat16)
    down_low = down_weight[0, 0].astype(jnp.bfloat16)
    slot_rows = jnp.einsum(
        "scl,ld->sd", route_hot, moe_input, preferred_element_type=jnp.float32
    ).astype(jnp.bfloat16)
    expert_rows = lax.all_to_all(
        spread(slot_rows).reshape(groups * wide_count, capacity, features),
        ("narrow", "wide"),
        split_axis=0,
        concat_axis=0,
        tiled=True,
    ).reshape(-1, features)
    gate_up = jnp.dot(expert_rows, joined, preferred_element_type=jnp.float32)
    gate_pre = gate_up[:, :part_width]
    up_pre = gate_up[:, part_width:]
    activated, gelu_back = jax.vjp(gelu_tanh, gate_pre)
    hidden = (activated * up_pre).astype(jnp.bfloat16)
    produced = jnp.dot(hidden, down_low, preferred_element_type=jnp.float32).astype(jnp.bfloat16)
    summed = gather_parts(
        lax.all_to_all(
            produced.reshape(groups * wide_count, capacity, features),
            ("narrow", "wide"),
            split_axis=0,
            concat_axis=0,
            tiled=True,
        )
    )
    first_rows = jnp.take(summed, safe_rows[:, 0], axis=0) * keep_float[:, 0:1]
    second_rows = jnp.take(summed, safe_rows[:, 1], axis=0) * keep_float[:, 1:2]
    moe_sum = gate_values[:, 0:1] * first_rows + gate_values[:, 1:2] * second_rows
    block_out = (hidden_x1 + moe_sum).astype(jnp.bfloat16)
    cotangent = upstream.astype(jnp.float32)
    pair_grad = jnp.stack(
        [jnp.sum(cotangent * first_rows, axis=1), jnp.sum(cotangent * second_rows, axis=1)], axis=1
    )
    logit_pair = gate_values * (pair_grad - jnp.sum(gate_values * pair_grad, axis=1, keepdims=True))
    logit_grad = jnp.sum(jnp.where(pick_mask, logit_pair[:, :, None], 0.0), axis=1).astype(
        jnp.bfloat16
    )
    scaled_grad = jnp.stack(
        [gate_values[:, 0:1] * cotangent, gate_values[:, 1:2] * cotangent], axis=0
    ).astype(jnp.bfloat16)
    slot_grads = jnp.einsum(
        "scl,cld->sd", route_hot, scaled_grad, preferred_element_type=jnp.float32
    ).astype(jnp.bfloat16)
    output_rows_grad = lax.all_to_all(
        spread(slot_grads).reshape(groups * wide_count, capacity, features),
        ("narrow", "wide"),
        split_axis=0,
        concat_axis=0,
        tiled=True,
    ).reshape(-1, features)
    hidden_grad = jnp.einsum(
        "rd,fd->rf", output_rows_grad, down_low, preferred_element_type=jnp.float32
    )
    down_local = jnp.einsum(
        "rf,rd->fd", hidden, output_rows_grad, preferred_element_type=jnp.float32
    )
    gate_pre_grad = gelu_back(hidden_grad * up_pre)[0]
    up_pre_grad = hidden_grad * activated
    pre_grad = jnp.concatenate([gate_pre_grad, up_pre_grad], axis=1).astype(jnp.bfloat16)
    joined_grad = jnp.einsum("rd,rf->df", expert_rows, pre_grad, preferred_element_type=jnp.float32)
    rows_grad = jnp.einsum(
        "rf,df->rd", pre_grad, joined, preferred_element_type=jnp.float32
    ).astype(jnp.bfloat16)
    accumulated_derivative = gather_parts(
        lax.all_to_all(
            rows_grad.reshape(groups * wide_count, capacity, features),
            ("narrow", "wide"),
            split_axis=0,
            concat_axis=0,
            tiled=True,
        )
    )
    moe_input_grad = jnp.take(accumulated_derivative, safe_rows[:, 0], axis=0) * keep_float[:, 0:1]
    moe_input_grad = (
        moe_input_grad
        + jnp.take(accumulated_derivative, safe_rows[:, 1], axis=0) * keep_float[:, 1:2]
    )
    moe_input_grad = moe_input_grad + jnp.einsum(
        "te,de->td", logit_grad, full_router, preferred_element_type=jnp.float32
    )
    router_local = jnp.einsum(
        "td,te->de", moe_input, logit_grad, preferred_element_type=jnp.float32
    )
    x1_part, moe_gain_local = moe_norm_back(moe_input_grad)
    x1_grad = cotangent + x1_part
    branch_grad = x1_grad.astype(jnp.bfloat16)
    out_local = jnp.einsum("td,te->de", attended, branch_grad, preferred_element_type=jnp.float32)
    attended_grad = (
        jnp.einsum("te,de->td", branch_grad, full_out, preferred_element_type=jnp.float32)
        .astype(jnp.bfloat16)
        .reshape(length, head_count, head_dim)
    )

    def backward_block(state_carry, step_index):
        key_acc, value_acc, bias_acc = state_carry
        first_row = step_index * block_rows
        row_heads, scores = block_scores(first_row)
        attn_probs = jnp.exp(scores - log_totals[step_index])
        probs_low = attn_probs.astype(jnp.bfloat16)
        prob_grad = jnp.einsum(
            "qhd,khd->hqk", attended_grad, value_heads, preferred_element_type=jnp.float32
        )
        scores_gradient = (
            attn_probs * (prob_grad - jnp.sum(attn_probs * prob_grad, axis=-1, keepdims=True))
        ).astype(jnp.bfloat16)
        query_grad = (
            jnp.einsum(
                "hqk,khd->qhd", scores_gradient, key_heads, preferred_element_type=jnp.float32
            )
            * score_scale
        ).astype(jnp.bfloat16)
        key_acc = (
            key_acc
            + jnp.einsum(
                "hqk,qhd->khd", scores_gradient, row_heads, preferred_element_type=jnp.float32
            )
            * score_scale
        )
        value_acc = value_acc + jnp.einsum(
            "hqk,qhd->khd", probs_low, attended_grad, preferred_element_type=jnp.float32
        )
        bucket_onehot_mask = (
            bucket_ids[:, None, None] == jnp.take(buckets, offsets(first_row))[None]
        ).astype(jnp.bfloat16)
        bias_acc = bias_acc + jnp.einsum(
            "cue,tue->tc", scores_gradient, bucket_onehot_mask, preferred_element_type=jnp.float32
        )
        return ((key_acc, value_acc, bias_acc), query_grad.reshape(block_rows, features))

    start_state = (
        jnp.zeros((length, head_count, head_dim), jnp.float32),
        jnp.zeros((length, head_count, head_dim), jnp.float32),
        jnp.zeros((bucket_count, head_count), jnp.float32),
    )
    (key_acc, value_acc, bias_local), query_grads = lax.scan(
        backward_block, start_state, jnp.arange(block_count, dtype=jnp.int32)
    )
    projected_grad = jnp.stack(
        [
            query_grads.reshape(length, features),
            key_acc.astype(jnp.bfloat16).reshape(length, features),
            value_acc.astype(jnp.bfloat16).reshape(length, features),
        ],
        axis=0,
    )
    qkv_local = jnp.einsum(
        "td,kte->kde", normed_in, projected_grad, preferred_element_type=jnp.float32
    )
    normed_grad = jnp.einsum(
        "kte,kde->td", projected_grad, full_qkv, preferred_element_type=jnp.float32
    )
    inputs_part, attn_gain_local = attn_norm_back(normed_grad)
    tokens_grad = (x1_grad + inputs_part).astype(jnp.bfloat16)
    gate_local = joined_grad[:, :part_width]
    up_local = joined_grad[:, part_width:]
    local_sums = jnp.stack(
        [
            jnp.sum(gate_local * gate_local, axis=1),
            jnp.sum(up_local * up_local, axis=1),
            jnp.sum(down_local * down_local, axis=0),
        ],
        axis=0,
    )
    part_stats = (
        jnp.stack(
            [
                jnp.mean(gate_local * gate_local, axis=0),
                jnp.mean(up_local * up_local, axis=0),
                jnp.mean(down_local * down_local, axis=1),
            ],
            axis=0,
        )
        + STAT_EPS
    )
    wide_sums = local_sums
    for bit_number in range(split_parts.bit_length() - 1):
        wide_sums = wide_sums + from_partner(wide_sums, "wide", bit_number)
    qkv_total, out_total, router_total, gain_a_total, gain_m_total, bias_total = lax.psum(
        (qkv_local, out_local, router_local, attn_gain_local, moe_gain_local, bias_local),
        ("narrow", "wide"),
    )
    wide_stats = wide_sums / (part_width * split_parts) + STAT_EPS
    gate_new = factored(
        gate_weight[0, 0], gate_local, wide_stats[0], part_stats[0], jnp.mean(wide_stats[0])
    )
    up_new = factored(
        up_weight[0, 0], up_local, wide_stats[1], part_stats[1], jnp.mean(wide_stats[1])
    )
    down_new = factored(
        down_weight[0, 0], down_local, part_stats[2], wide_stats[2], jnp.mean(wide_stats[2])
    )
    attn_all = jnp.concatenate([qkv_total, out_total[None]], axis=0)
    focus_squared_mean = attn_all * attn_all
    attn_rows = jnp.mean(focus_squared_mean, axis=2) + STAT_EPS
    attn_cols = jnp.mean(focus_squared_mean, axis=1) + STAT_EPS
    attn_means = jnp.mean(attn_rows, axis=1)
    row_count = qkv_weights.shape[1]
    col_count = qkv_weights.shape[2]
    row_first = lax.axis_index("narrow") * row_count
    col_first = lax.axis_index("wide") * col_count
    rows_mine = lax.dynamic_slice_in_dim(attn_rows, row_first, row_count, 1)
    cols_mine = lax.dynamic_slice_in_dim(attn_cols, col_first, col_count, 1)
    attn_block = lax.dynamic_slice_in_dim(
        lax.dynamic_slice_in_dim(attn_all, row_first, row_count, 1), col_first, col_count, 2
    )
    qkv_new = factored(qkv_weights, attn_block[:3], rows_mine[:3], cols_mine[:3], attn_means[:3])
    out_step = adafactor_step(attn_block[3], rows_mine[3], cols_mine[3], attn_means[3])
    qkv_stats = jnp.stack([attn_rows[:3], attn_cols[:3]], axis=0)
    out_stats = jnp.stack([attn_rows[3], attn_cols[3]], axis=0)
    router_sq = router_total * router_total
    router_rows = jnp.mean(router_sq, axis=1) + STAT_EPS
    router_cols = jnp.mean(router_sq, axis=0) + STAT_EPS
    router_row_count = router.shape[0]
    router_col_count = router.shape[1]
    router_row_first = lax.axis_index("narrow") * router_row_count
    router_col_first = lax.axis_index("wide") * router_col_count
    router_block = lax.dynamic_slice_in_dim(
        lax.dynamic_slice_in_dim(router_total, router_row_first, router_row_count, 0),
        router_col_first,
        router_col_count,
        1,
    )
    router_new = factored(
        router,
        router_block,
        lax.dynamic_slice_in_dim(router_rows, router_row_first, router_row_count, 0),
        lax.dynamic_slice_in_dim(router_cols, router_col_first, router_col_count, 0),
        jnp.mean(router_rows),
    )
    return (
        block_out,
        tokens_grad,
        gain_a_total,
        qkv_total,
        out_total,
        bias_total,
        gain_m_total,
        router_total,
        gate_local[None, None],
        up_local[None, None],
        down_local[None, None],
        qkv_new,
        out_step,
        router_new,
        gate_new[None, None],
        up_new[None, None],
        down_new[None, None],
        qkv_stats,
        out_stats,
        router_rows,
        router_cols,
        wide_stats[None, None],
        part_stats[None, None],
    )


def solution(mesh):
    in_specs = (
        P(("narrow", "wide"), None),
        P(),
        P(None, "narrow", "wide"),
        P("narrow", "wide"),
        P(),
        P(),
        P("narrow", "wide"),
        P("narrow", "wide", None, None),
        P("narrow", "wide", None, None),
        P("narrow", "wide", None, None),
        P(("narrow", "wide"), None),
        P(("narrow", "wide"), None),
        P(),
        P(("narrow", "wide"), None),
    )
    out_specs = (
        P(("narrow", "wide"), None),
        P(("narrow", "wide"), None),
        P(),
        P(),
        P(),
        P(),
        P(),
        P(),
        P("narrow", "wide", None, None),
        P("narrow", "wide", None, None),
        P("narrow", "wide", None, None),
        P(None, "narrow", "wide"),
        P("narrow", "wide"),
        P("narrow", "wide"),
        P("narrow", "wide", None, None),
        P("narrow", "wide", None, None),
        P("narrow", "wide", None, None),
        P(),
        P(),
        P(),
        P(),
        P("narrow", "wide", None, None),
        P("narrow", "wide", None, None),
    )
    return jax.shard_map(
        on_device, mesh=mesh, in_specs=in_specs, out_specs=out_specs, check_vma=False
    )
```

profile of v0, /device:TPU:0, one launch (start us, length us, event | category | flops | bytes accessed | tf_op | source)
XLA Modules:
  0.0 1517.5 jit_solution(16019908768874178970)
XLA Ops:
  9.0 31.1 %all-gather.5.cloned.1.call-done = bf16[3,256,1024]{2,1,0:T(8,128)(2,1)} async-done(((bf16[3,256,128]{2,1,0:T(8,128)(2,1)}), bf16[3,256,1024]{2,1,0:T(8,128)(2,1)}) %all-gather.5.cloned.1.call-update) | async-done | bytes 1572880 | tf_op jit(solution)/shard_map/all_gather | solution.py:65
  41.1 15.1 all_gather.20
  56.9 215.9 %gather_fusion.1 = f32[65536,16]{1,0:T(8,128)} fusion(f32[16,511]{0,1:T(8,128)S(1)} %copy.142, s32[65536]{0:T(1024)S(1)} %broadcast_clamp_fusion.1), kind=kCustom, calls=%fused_computation.clone | custom fusion | bytes 8650752 | tf_op jit(solution)/shard_map/while/body/eval_jaxpr/jit(_take)/gather | solution.py:109
  272.8 20.1 %copy.144 = f32[256,256,16]{0,1,2:T(8,128)} copy(f32[256,256,16]{2,1,0:T(8,128)} %bitcast.177) | data formatting | bytes 8388608 | tf_op jit(solution)/shard_map/while/body/eval_jaxpr/jit(_take)/gather | solution.py:109
  293.7 4.7 fusion.19
  313.4 3.8 all-to-all-start
  319.6 4.6 copy.147
  324.1 4.1 bitcast_convert_fusion
  328.2 106.5 %all-to-all-done = bf16[32,80,1024]{2,1,0:T(8,128)(2,1)} async-done(((bf16[32,80,1024]{2,1,0:T(8,128)(2,1)}), bf16[32,80,1024]{2,1,0:T(8,128)(2,1)}, u32[]{:S(2)}, u32[]{:S(2)}) %all-to-all-start) | async-done | bytes 5242912 | tf_op jit(solution)/shard_map/all_to_all | solution.py:164
  434.7 12.8 fusion.18
  453.3 6.1 fusion.98
  463.2 92.1 %all-gather = bf16[8,1,256]{2,1,0:T(2,128)(2,1)S(1)} all-gather(bf16[1,1,256]{2,1,0:T(2,128)(2,1)S(1)} %convert_bitcast_fusion), channel_id=1, replica_groups=mesh['narrow'=4,'wide'=8] {'wide'}, dimensions={0}, use_global_device_ids=true | all-gather | bytes 4608 | tf_op jit(solution)/shard_map/all_gather | solution.py:67
  555.3 8.3 all_gather.23
  564.1 16.7 %all-to-all-done.1 = bf16[32,80,1024]{2,1,0:T(8,128)(2,1)} async-done(((bf16[32,80,1024]{2,1,0:T(8,128)(2,1)}), bf16[32,80,1024]{2,1,0:T(8,128)(2,1)}, u32[]{:S(2)}, u32[]{:S(2)}) %all-to-all-start.1) | async-done | bytes 5242912 | tf_op jit(solution)/shard_map/all_to_all | solution.py:178
  580.8 4.1 convert_reduce_fusion.1
  594.2 130.7 %all_to_all.20 = bf16[32,80,1024]{2,1,0:T(8,128)(2,1)} all-to-all(bf16[32,80,1024]{2,1,0:T(8,128)(2,1)S(1)} %bitcast.181), channel_id=1, replica_groups=mesh['narrow'=4,'wide'=8] {'narrow','wide'}, dimensions={0} | all-to-all | bytes 10485760 | tf_op jit(solution)/shard_map/all_to_all | solution.py:204
  725.0 12.3 fusion.10
  737.3 15.1 convolution_convert_fusion.1
  752.4 3.8 all-to-all-start.3
  757.4 409.5 %gather_fusion = s32[65536]{0:T(1024)S(1)} fusion(s32[511]{0:T(512)S(1)} %copy-done.2, s32[65536]{0:T(1024)S(1)} %broadcast_clamp_fusion), kind=kCustom, calls=%fused_computation.5 | custom fusion | bytes 786432 | tf_op jit(solution)/shard_map/while/body/eval_jaxpr/jit(_take)/gather | solution.py:283
  1167.4 4.1 convert_reduce_fusion
  1191.0 6.7 convolution_bitcast_fusion
  1197.8 9.4 multiply_reduce_fusion.5
  1207.2 10.4 fusion.11
  1230.4 7.7 fusion.14
  1250.3 5.2 fusion.16
  1257.6 5.2 fusion.32
  1262.9 42.5 %all-reduce = (f32[1024]{0:T(1024)}, f32[32,16]{0,1:T(8,128)}, f32[1024]{0:T(1024)}, f32[1024,8]{0,1:T(8,128)S(1)}) all-reduce(f32[1024]{0:T(1024)S(1)} %get-tuple-element.193, f32[32,16]{0,1:T(8,128)S(1)} %fusion.28, f32[1024]{0:T(1024)S(1)} %get-tuple-element.191, ...), channel_id=1, replica_groups=mesh['narrow'=4,'wide'=8] {'narrow','wide'}, use_global_device_ids=true, to_apply=%region_18.21 | all-reduce | flops 10752 | bytes 86016 | tf_op jit(solution)/shard_map/psum | solution.py:338
  1309.9 169.6 %all-reduce.4.cloned.1.call-done = (f32[3,1024,1024]{1,2,0:T(8,128)}, f32[1024,1024]{0,1:T(8,128)}) async-done(((f32[3,1024,1024]{1,2,0:T(8,128)}, f32[1024,1024]{0,1:T(8,128)}), (f32[3,1024,1024]{1,2,0:T(8,128)}, f32[1024,1024]{0,1:T(8,128)})) %all-reduce.4.cloned.1.call-update) | async-done | bytes 16777232 | tf_op jit(solution)/shard_map/psum | solution.py:338
  1479.4 7.0 fusion.1
  1486.7 12.6 copy.160
  1499.3 5.3 copy.161
  (287 shorter events, 96.3 us)
Async XLA Ops:
  7.2 49.2 %copy-start = (f32[32,16]{0,1:T(8,128)S(1)}, f32[32,16]{0,1:T(8,128)}, u32[]{:S(2)}) copy-start(f32[32,16]{0,1:T(8,128)} %param.22) | copy-start | bytes 6148
  7.2 49.2 %copy-start.2 = (s32[511]{0:T(512)S(1)}, s32[511]{0:T(512)}, u32[]{:S(2)}) copy-start(s32[511]{0:T(512)} %param.30) | copy-start | bytes 6136
  7.2 32.9 %all-gather.5.cloned.1.call-start = ((), (), s32[]{:S(2)}) async-start(), calls=%async_computation.4 | async-start | bytes 1769472 | tf_op jit(solution)/shard_map/all_gather | solution.py:65
  9.0 284.7 %all-gather.7.cloned.1.call-start = ((), (), s32[]{:S(2)}) async-start(), calls=%async_computation.5 | async-start | bytes 7864320 | tf_op jit(solution)/shard_map/all_gather | solution.py:70
  40.1 265.2 %all-gather.9.cloned.1.call-start = ((), (), s32[]{:S(2)}) async-start(), calls=%async_computation.6 | async-start | bytes 2621440 | tf_op jit(solution)/shard_map/all_gather | solution.py:71
  272.8 20.3 %copy-start.50 = (s32[256,2]{0,1:T(2,128)S(1)}, s32[256,2]{0,1:T(2,128)}, u32[]{:S(2)}) copy-start(s32[256,2]{0,1:T(2,128)} %param.28) | copy-start | bytes 6148
  272.8 20.3 %copy-start.61 = (s32[256,2]{0,1:T(2,128)S(1)}, s32[256,2]{0,1:T(2,128)}, u32[]{:S(2)}) copy-start(s32[256,2]{0,1:T(2,128)} %param.29) | copy-start | bytes 6148
  272.8 20.6 %copy-start.20 = (bf16[256,1024]{1,0:T(8,128)(2,1)S(1)}, bf16[256,1024]{1,0:T(8,128)(2,1)}, u32[]{:S(2)}) copy-start(bf16[256,1024]{1,0:T(8,128)(2,1)} %param.18) | copy-start | bytes 1572868
  272.8 20.8 %copy-start.51 = (f32[1024]{0:T(1024)S(1)}, f32[1024]{0:T(1024)}, u32[]{:S(2)}) copy-start(f32[1024]{0:T(1024)} %param.19) | copy-start | bytes 12292
  305.3 8.1 copy-start.25
  313.4 121.3 %all-to-all-start = ((bf16[32,80,1024]{2,1,0:T(8,128)(2,1)}), bf16[32,80,1024]{2,1,0:T(8,128)(2,1)}, u32[]{:S(2)}, u32[]{:S(2)}) async-start(bf16[32,80,1024]{2,1,0:T(8,128)(2,1)} %bitcast.180), calls=%async_computation | async-start | bytes 10485760 | tf_op jit(solution)/shard_map/all_to_all | solution.py:164
  319.6 8.7 copy-start.5
  459.5 104.3 %copy-start.24 = (bf16[256,1024]{1,0:T(8,128)(2,1)S(1)}, bf16[256,1024]{1,0:T(8,128)(2,1)}, u32[]{:S(2)}) copy-start(bf16[256,1024]{1,0:T(8,128)(2,1)} %copy-done.23) | copy-start | bytes 1572868
  459.5 121.3 %all-to-all-start.1 = ((bf16[32,80,1024]{2,1,0:T(8,128)(2,1)}), bf16[32,80,1024]{2,1,0:T(8,128)(2,1)}, u32[]{:S(2)}, u32[]{:S(2)}) async-start(bf16[32,80,1024]{2,1,0:T(8,128)(2,1)} %bitcast.189), calls=%async_computation.1 | async-start | bytes 10485760 | tf_op jit(solution)/shard_map/all_to_all | solution.py:178
  588.9 136.0 %slice-start = ((s8[14417920]{0:T(1024)(128)(4,1)}), s8[4194304]{0:T(1024)(128)(4,1)S(1)}, s32[]{:S(2)}) async-start(s8[14417920]{0:T(1024)(128)(4,1)} %bitcast.182), calls=%async_computation.8 | async-start | bytes 8388608
  592.6 132.3 %slice-start.1 = ((s8[14417920]{0:T(1024)(128)(4,1)}), s8[4194304]{0:T(1024)(128)(4,1)S(1)}, s32[]{:S(2)}) async-start(s8[14417920]{0:T(1024)(128)(4,1)} %bitcast.182), calls=%async_computation.9 | async-start | bytes 8388608
  593.5 131.4 %slice-start.2 = ((s8[14417920]{0:T(1024)(128)(4,1)}), s8[4194304]{0:T(1024)(128)(4,1)S(1)}, s32[]{:S(2)}) async-start(s8[14417920]{0:T(1024)(128)(4,1)} %bitcast.182), calls=%async_computation.10 | async-start | bytes 8388608
  594.2 130.7 %slice-start.3 = ((s8[14417920]{0:T(1024)(128)(4,1)}), s8[1835008]{0:T(1024)(128)(4,1)S(1)}, s32[]{:S(2)}) async-start(s8[14417920]{0:T(1024)(128)(4,1)} %bitcast.182), calls=%async_computation.11 | async-start | bytes 3670016
  594.2 130.7 %copy-start.36 = (f32[1,1,704,1024]{3,2,1,0:T(8,128)S(1)}, f32[1,1,704,1024]{3,2,1,0:T(8,128)}, u32[]{:S(2)}) copy-start(f32[1,1,704,1024]{3,2,1,0:T(8,128)} %param.27) | copy-start | bytes 8650756
  752.4 415.0 %all-to-all-start.3 = ((bf16[32,80,1024]{2,1,0:T(8,128)(2,1)}), bf16[32,80,1024]{2,1,0:T(8,128)(2,1)}, u32[]{:S(2)}, u32[]{:S(2)}) async-start(bf16[32,80,1024]{2,1,0:T(8,128)(2,1)} %bitcast.188), calls=%async_computation.3 | async-start | bytes 10485760 | tf_op jit(solution)/shard_map/all_to_all | solution.py:225
  756.2 723.2 %all-reduce.4.cloned.1.call-start = ((), (), s32[]{:S(2)}) async-start(), calls=%async_computation.7 | async-start | bytes 33554432 | tf_op jit(solution)/shard_map/psum | solution.py:338
  1197.8 9.4 copy-start.66
  1197.8 9.4 copy-start.67
  1220.1 10.4 copy-start.6
  1221.7 1.2 collective-permute-start
  1222.9 4.3 collective-permute-start.1
  1257.6 50.5 %copy-start.58 = (f32[256]{0:T(256)S(1)}, f32[256]{0:T(256)}, u32[]{:S(2)}) copy-start(f32[256]{0:T(256)} %copy-done.57) | copy-start | bytes 3076
  1257.6 50.5 %copy-start.64 = (f32[256,1]{0,1:T(1,128)S(1)}, f32[256,1]{0,1:T(1,128)}, u32[]{:S(2)}) copy-start(f32[256,1]{0,1:T(1,128)} %param.24) | copy-start | bytes 3076
  1257.6 51.2 %copy-start.13 = (f32[256,1024]{1,0:T(8,128)S(1)}, f32[256,1024]{1,0:T(8,128)}, u32[]{:S(2)}) copy-start(f32[256,1024]{1,0:T(8,128)} %copy-done.12) | copy-start | bytes 3145732
  1305.4 181.1 %copy-start.49 = (f32[1024,8]{0,1:T(8,128)}, f32[1024,8]{0,1:T(8,128)S(1)}, u32[]{:S(2)}) copy-start(f32[1024,8]{0,1:T(8,128)S(1)} %get-tuple-element.208) | copy-start | bytes 98308
  1305.5 180.9 %copy-start.65 = (f32[8]{0:T(128)}, f32[8]{0:T(128)S(1)}, u32[]{:S(2)}) copy-start(f32[8]{0:T(128)S(1)} %multiply_add_fusion.6) | copy-start | bytes 100
  1306.7 179.7 %copy-start.62 = (f32[1024]{0:T(1024)}, f32[1024]{0:T(1024)S(1)}, u32[]{:S(2)}) copy-start(f32[1024]{0:T(1024)S(1)} %get-tuple-element.212) | copy-start | bytes 12292
  (49 other events, 161.7 us)
Sparse Core Ops, SparseCore 0:
  10.2 29.8 all-gather.4
  42.0 69.2 all-gather.6
  113.2 35.3 all-gather.8
  1197.9 281.4 all-reduce.3
where the time goes:
time: 1530 us; the launch traced here: 1520 us
  local copies, waits for them, and re-layouts  711 us (46%)
  waiting for transfers between devices  327 us (21%)
  blocking collectives  289 us (19%)
  matrix products  105 us (7%)
  other arithmetic  54 us (4%)
  between operations  18.1 us (1%)
    gather x2, local copies, waits for them, and re-layouts, backward_block(): jnp.take(buckets, offsets(first_row))[None]  410 us
    gather x2, local copies, waits for them, and re-layouts, block_scores(): jnp.take(bias_table, offsets(first_row), axis=1)  236 us
    psum x1, waiting for transfers between devices, on_device(): lax.psum((qkv_local, out_local, router_local, attn_gain_local, moe_gain_l...  170 us
    all_to_all x1, blocking collectives, on_device(): lax.all_to_all(spread(slot_grads).reshape(groups * wide_count, capacity,...  131 us
    all_to_all x1, waiting for transfers between devices, on_device(): lax.all_to_all(spread(slot_rows).reshape(groups * wide_count, capacity, f...  106 us
    all_gather x1, blocking collectives, on_device(): lax.all_gather(router_low, 'wide', axis=1, tiled=True)  92.1 us
    unnamed x159, local copies, waits for them, and re-layouts  50 us
    psum x1, blocking collectives, on_device(): lax.psum((qkv_local, out_local, router_local, attn_gain_local, moe_gain_l...  42.5 us
  transfers between devices with their start and end apart: 9, of which 6 were waited for; matrix products, arithmetic and copies ran while one was open for 48% of the time, Pallas kernels for 0%

commit v1 on v0

v1 whole, which is shorter than its diff:
```python
import functools

import jax
import jax.numpy as jnp
from jax import lax
from jax.experimental import pallas as pl
from jax.experimental.pallas import tpu as pltpu
from jax.sharding import PartitionSpec as P

NORM_EPS = 1e-06
STAT_EPS = 1e-06
STEP_RATE = 0.01
LANES = 128
GELU_C = 0.7978845608028654
GELU_A = 0.044715
BF = jnp.bfloat16
F32 = jnp.float32
VMEM_LIMIT = 60 * 1024 * 1024
NN = (((1,), (0,)), ((), ()))
NT = (((1,), (1,)), ((), ()))
TN = (((0,), (0,)), ((), ()))


def mm(a, b, dims=NN):
    return lax.dot_general(a, b, dims, preferred_element_type=F32)


def from_partner(value, hop):
    axis, bit = hop
    mask = 2**bit
    pairs = [(source, source ^ mask) for source in range(lax.axis_size(axis))]
    return lax.ppermute(value, axis, pairs)


def hop_orders(groups, wide_count):
    narrow = [("narrow", b) for b in range(groups.bit_length() - 1)]
    wide = [("wide", b) for b in range(1, wide_count.bit_length() - 1)]
    far, near = wide[1:][::-1], wide[:1]
    core = [("wide", 0)]
    return (
        far + narrow + near + core,
        far + near + narrow + core,
        far + narrow[1:] + near + narrow[:1] + core,
    )


def block_slots(order, groups, wide_count):
    n_ids = jnp.arange(groups, dtype=jnp.int32)[:, None]
    w_ids = 2 * jnp.arange(wide_count // 2, dtype=jnp.int32)[None, :]
    slots = jnp.zeros((groups, wide_count // 2), jnp.int32)
    for stage, (axis, bit) in enumerate(order[:-1]):
        ids = n_ids if axis == "narrow" else w_ids
        differs = ((ids ^ lax.axis_index(axis)) >> bit) & 1
        slots = slots | (differs << stage)
    return slots


def gather_blocks(block, order):
    blocks = block[None]
    for hop in order[:-1]:
        blocks = jnp.concatenate([blocks, from_partner(blocks, hop)], axis=0)
    return blocks, from_partner(blocks, order[-1])


def scatter_sum(keep, send, order):
    total = keep + from_partner(send, order[-1]).astype(F32)
    for hop in order[:-1][::-1]:
        half = total.shape[0] // 2
        total = total[:half] + from_partner(total[half:].astype(BF), hop).astype(F32)
    return total[0]


def cube_sum(value, hops):
    for hop in hops:
        value = value + from_partner(value, hop)
    return value


def as_matrix(own, other, slots, my_core):
    groups, half_wide = slots.shape
    both = jnp.stack([jnp.where(my_core == 0, own, other), jnp.where(my_core == 0, other, own)], 1)
    picked = jnp.take(both, slots.reshape(-1), axis=0)
    rows, cols = own.shape[1:]
    picked = picked.reshape(groups, half_wide, 2, rows, cols)
    return jnp.transpose(picked, (0, 3, 1, 2, 4)).reshape(groups * rows, half_wide * 2 * cols)


def from_matrix(matrix, groups, half_wide):
    lead = matrix.shape[:-2]
    rows, cols = matrix.shape[-2] // groups, matrix.shape[-1] // (2 * half_wide)
    shaped = matrix.reshape(lead + (groups, rows, half_wide, 2, cols))
    k = len(lead)
    order = tuple(range(k)) + (k, k + 2, k + 3, k + 1, k + 4)
    return jnp.transpose(shaped, order)


def gelu_tanh(values):
    return jax.nn.gelu(values, approximate=True)


def adafactor_step(gradient, row_stats, col_stats, mean_rows):
    return (
        STEP_RATE
        * gradient
        / jnp.sqrt(row_stats[..., :, None] * col_stats[..., None, :] / mean_rows[..., None, None])
    )


def factored(weight, gradient, row_stats, col_stats, mean_rows):
    return weight - adafactor_step(gradient, row_stats, col_stats, mean_rows)


def vmem():
    return pl.BlockSpec(memory_space=pltpu.VMEM)


def smem():
    return pl.BlockSpec(memory_space=pltpu.SMEM)


def params():
    return pltpu.CompilerParams(vmem_limit_bytes=VMEM_LIMIT)


def lane_masks(head_dim):
    heads = LANES // head_dim
    ids = lax.broadcasted_iota(jnp.int32, (1, LANES), 1) // head_dim
    return [ids == i for i in range(heads)]


def attend_body(
    table_ref, tokens_ref, gain_ref, bias_ref,
    own_q, own_k, own_v, far_q, far_k, far_v,
    normed_ref, heads_ref, probs_ref, attended_ref,
    *, groups, pairs, head_dim,
):
    length, features = tokens_ref.shape
    rows = features // groups
    x = tokens_ref[...].astype(F32)
    factor = lax.rsqrt(jnp.mean(x * x, axis=-1, keepdims=True) + NORM_EPS)
    normed_ref[...] = (x * factor * gain_ref[...]).astype(BF)
    core = table_ref[0]

    def project(w2, carry):
        for m, (own, far) in enumerate(((own_q, far_q), (own_k, far_k), (own_v, far_v))):
            total = None
            for n in range(groups):
                at = table_ref[1 + (m * groups + n) * pairs + w2]
                block = jnp.concatenate([own[at], far[at]], axis=1)
                part = mm(normed_ref[:, n * rows : (n + 1) * rows], block)
                total = part if total is None else total + part
            total = total.astype(BF)
            heads_ref[m, 2 * w2 + core] = total[:, :LANES]
            heads_ref[m, 2 * w2 + 1 - core] = total[:, LANES:]
        return carry

    lax.fori_loop(0, pairs, project, 0)
    masks = lane_masks(head_dim)
    scale = head_dim**-0.5

    def attend(w, carry):
        q, k, v = heads_ref[0, w], heads_ref[1, w], heads_ref[2, w]
        mixed = jnp.zeros((length, LANES), F32)
        for i, mask in enumerate(masks):
            head = w * len(masks) + i
            raw = mm(jnp.where(mask, q, jnp.zeros_like(q)), k, NT)
            line = jnp.broadcast_to(bias_ref[pl.ds(head, 1), :], (length, 2 * length))
            bias = pltpu.roll(line, length + 1, 1, stride=1, stride_axis=0)[:, :length]
            scores = raw * scale + bias
            top = jnp.max(scores, axis=-1, keepdims=True)
            grown = jnp.exp(scores - top)
            probs = grown / jnp.sum(grown, axis=-1, keepdims=True)
            probs_ref[head] = probs
            mixed = jnp.where(mask, mm(probs.astype(BF), v), mixed)
        attended_ref[w] = mixed.astype(BF)
        return carry

    lax.fori_loop(0, 2 * pairs, attend, 0)


def attend_call(table, tokens, gain, bias_table, gathered, groups, head_dim):
    length, features = tokens.shape
    pairs = features // (2 * LANES)
    head_count = features // head_dim
    owns = [g[0] for g in gathered]
    fars = [g[1] for g in gathered]
    body = functools.partial(attend_body, groups=groups, pairs=pairs, head_dim=head_dim)
    return pl.pallas_call(
        body,
        in_specs=[smem()] + [vmem()] * 9,
        out_specs=[vmem()] * 4,
        out_shape=[
            jax.ShapeDtypeStruct((length, features), BF),
            jax.ShapeDtypeStruct((3, 2 * pairs, length, LANES), BF),
            jax.ShapeDtypeStruct((head_count, length, length), F32),
            jax.ShapeDtypeStruct((2 * pairs, length, LANES), BF),
        ],
        compiler_params=params(),
        name="attend",
    )(table, tokens, gain.reshape(1, features), bias_table, *owns, *fars)


def attend_back_body(
    table_ref, normed_ref, heads_ref, probs_ref, grad_ref,
    keep_ref, send_ref, dheads_ref, diag_ref,
    *, groups, pairs, head_dim,
):
    length, features = normed_ref.shape
    rows = features // groups
    masks = lane_masks(head_dim)
    scale = head_dim**-0.5

    def back(w, carry):
        q, k, v = heads_ref[0, w], heads_ref[1, w], heads_ref[2, w]
        da = grad_ref[w]
        dq = jnp.zeros((length, LANES), F32)
        dk, dv = dq, dq
        for i, mask in enumerate(masks):
            head = w * len(masks) + i
            probs = probs_ref[head]
            dp = mm(jnp.where(mask, da, jnp.zeros_like(da)), v, NT)
            spread = jnp.sum(probs * dp, axis=-1, keepdims=True)
            ds = (probs * (dp - spread)).astype(BF)
            dq = jnp.where(mask, mm(ds, k), dq)
            dk = jnp.where(mask, mm(ds, q, TN), dk)
            dv = jnp.where(mask, mm(probs.astype(BF), da, TN), dv)
            wide_ds = jnp.concatenate([ds.astype(F32), jnp.zeros((length, length), F32)], axis=1)
            diag = jnp.zeros((8, 2 * length), F32)
            for g in range(length // 8):
                diag = diag + pltpu.roll(wide_ds[8 * g : 8 * g + 8], length - 1 - 8 * g, 1)
            diag_ref[head] = diag
        dheads_ref[0, w] = (dq * scale).astype(BF)
        dheads_ref[1, w] = (dk * scale).astype(BF)
        dheads_ref[2, w] = dv.astype(BF)
        return carry

    lax.fori_loop(0, 2 * pairs, back, 0)
    core = table_ref[0]

    def weigh(w2, carry):
        for m in range(3):
            both = jnp.concatenate(
                [dheads_ref[m, 2 * w2 + core], dheads_ref[m, 2 * w2 + 1 - core]], axis=1
            )
            for n in range(groups):
                at = table_ref[1 + (m * groups + n) * pairs + w2]
                block = mm(normed_ref[:, n * rows : (n + 1) * rows], both, TN)
                keep_ref[m, at] = block[:, :LANES]
                send_ref[m, at] = block[:, LANES:].astype(BF)
        return carry

    lax.fori_loop(0, pairs, weigh, 0)


def attend_back_call(table, normed, heads, probs, attended_grad, groups, head_dim):
    length, features = normed.shape
    pairs = features // (2 * LANES)
    head_count = features // head_dim
    rows = features // groups
    body = functools.partial(attend_back_body, groups=groups, pairs=pairs, head_dim=head_dim)
    return pl.pallas_call(
        body,
        in_specs=[smem()] + [vmem()] * 4,
        out_specs=[vmem()] * 4,
        out_shape=[
            jax.ShapeDtypeStruct((3, groups * pairs, rows, LANES), F32),
            jax.ShapeDtypeStruct((3, groups * pairs, rows, LANES), BF),
            jax.ShapeDtypeStruct((3, 2 * pairs, length, LANES), BF),
            jax.ShapeDtypeStruct((head_count, 8, 2 * length), F32),
        ],
        compiler_params=params(),
        name="attend_back",
    )(table, normed, heads, probs, attended_grad)


def tokens_back_body(
    table_ref, tokens_ref, gain_ref, x1_grad_ref, dheads_ref,
    own_q, own_k, own_v, far_q, far_k, far_v,
    out_ref, gain_out_ref, acc_ref,
    *, groups, pairs,
):
    length, features = tokens_ref.shape
    rows = features // groups
    core = table_ref[0]
    for n in range(groups):

        def step(w2, total):
            for m, (own, far) in enumerate(((own_q, far_q), (own_k, far_k), (own_v, far_v))):
                at = table_ref[1 + (m * groups + n) * pairs + w2]
                both = jnp.concatenate(
                    [dheads_ref[m, 2 * w2 + core], dheads_ref[m, 2 * w2 + 1 - core]], axis=1
                )
                total = total + mm(both, jnp.concatenate([own[at], far[at]], axis=1), NT)
            return total

        total = lax.fori_loop(0, pairs, step, jnp.zeros((length, rows), F32))
        acc_ref[:, n * rows : (n + 1) * rows] = total
    x = tokens_ref[...].astype(F32)
    factor = lax.rsqrt(jnp.mean(x * x, axis=-1, keepdims=True) + NORM_EPS)
    hat = x * factor
    grad = acc_ref[...]
    gain_out_ref[...] = jnp.sum(grad * hat, axis=0, keepdims=True)
    scaled = grad * gain_ref[...]
    inner = jnp.mean(scaled * hat, axis=-1, keepdims=True)
    out_ref[...] = (x1_grad_ref[...] + factor * (scaled - hat * inner)).astype(BF)


def tokens_back_call(table, tokens, gain, x1_grad, dheads, gathered, groups):
    length, features = tokens.shape
    pairs = features // (2 * LANES)
    owns = [g[0] for g in gathered]
    fars = [g[1] for g in gathered]
    return pl.pallas_call(
        functools.partial(tokens_back_body, groups=groups, pairs=pairs),
        in_specs=[smem()] + [vmem()] * 10,
        out_specs=[vmem()] * 2,
        out_shape=[
            jax.ShapeDtypeStruct((length, features), BF),
            jax.ShapeDtypeStruct((1, features), F32),
        ],
        scratch_shapes=[pltpu.VMEM((length, features), F32)],
        compiler_params=params(),
        name="tokens_back",
    )(table, tokens, gain.reshape(1, features), x1_grad, dheads, *owns, *fars)


def expert_body(
    expert_ref, x_ref, up_ref, router_ref, gate_w, up_w, down_w,
    y_ref, dx_ref, hidden_ref, dgate_ref, dup_ref, dy_ref,
):
    features = x_ref.shape[1]
    x = x_ref[...]
    logits = mm(x, router_ref[...])
    lane = lax.broadcasted_iota(jnp.int32, logits.shape, 1)
    other_id = up_ref[:, features : features + 1].astype(jnp.int32)
    mine = jnp.sum(jnp.where(lane == expert_ref[0], logits, 0.0), axis=1, keepdims=True)
    other = jnp.sum(jnp.where(lane == other_id, logits, 0.0), axis=1, keepdims=True)
    top = jnp.maximum(mine, other)
    mine_e = jnp.exp(mine - top)
    gate = mine_e / (mine_e + jnp.exp(other - top))
    dy = (gate * up_ref[:, :features].astype(F32)).astype(BF)
    dy_ref[...] = dy
    g = mm(x, gate_w[...])
    u = mm(x, up_w[...])
    t = jnp.tanh(GELU_C * (g + GELU_A * g * g * g))
    act = 0.5 * g * (1.0 + t)
    hidden = (act * u).astype(BF)
    hidden_ref[...] = hidden
    y_ref[...] = mm(hidden, down_w[...]).astype(BF)
    dh = mm(dy, down_w[...], NT)
    slope = 0.5 * (1.0 + t) + 0.5 * g * (1.0 - t * t) * (GELU_C * (1.0 + 3.0 * GELU_A * g * g))
    dg = (dh * u * slope).astype(BF)
    du = (dh * act).astype(BF)
    dgate_ref[...] = dg
    dup_ref[...] = du
    dx_ref[...] = (mm(dg, gate_w[...], NT) + mm(du, up_w[...], NT)).astype(BF)


def row_block(rows):
    for size in (256, 320, 160, 128, 64, 32, 16):
        if rows % size == 0:
            return size
    return rows


def expert_call(expert, x, upstream, router, gate_w, up_w, down_w):
    rows, features = x.shape
    size = row_block(rows)
    wide = gate_w.shape[1]

    def rows_spec(cols):
        return pl.BlockSpec((size, cols), lambda i, e: (i, 0))

    def whole(arr):
        return pl.BlockSpec(arr.shape, lambda i, e: (0, 0))

    return pl.pallas_call(
        expert_body,
        grid_spec=pltpu.PrefetchScalarGridSpec(
            num_scalar_prefetch=1,
            grid=(rows // size,),
            in_specs=[
                rows_spec(features), rows_spec(upstream.shape[1]),
                whole(router), whole(gate_w), whole(up_w), whole(down_w),
            ],
            out_specs=[
                rows_spec(features), rows_spec(features),
                rows_spec(wide), rows_spec(wide), rows_spec(wide), rows_spec(features),
            ],
        ),
        out_shape=[
            jax.ShapeDtypeStruct((rows, features), BF),
            jax.ShapeDtypeStruct((rows, features), BF),
            jax.ShapeDtypeStruct((rows, wide), BF),
            jax.ShapeDtypeStruct((rows, wide), BF),
            jax.ShapeDtypeStruct((rows, wide), BF),
            jax.ShapeDtypeStruct((rows, features), BF),
        ],
        compiler_params=params(),
        name="expert",
    )(expert, x, upstream, router, gate_w, up_w, down_w)


def expert_grad_body(xa, xb, dya, dyb, ha, hb, ga, gb, ua, ub, gate_ref, up_ref, down_ref):
    width = gate_ref.shape[1]
    gate_ref[...] = (mm(xa[...], ga[...], TN) + mm(xb[...], gb[...], TN))[:, :width]
    up_ref[...] = (mm(xa[...], ua[...], TN) + mm(xb[...], ub[...], TN))[:, :width]
    down_ref[...] = (mm(ha[...], dya[...], TN) + mm(hb[...], dyb[...], TN))[:width]


def expert_grad_call(xs, dys, hs, gs, us, width):
    rows, features = xs[0].shape
    padded = hs[0].shape[1]
    size = 256
    cols = pl.BlockSpec((rows, size), lambda i: (0, i))
    whole = pl.BlockSpec((rows, padded), lambda i: (0, 0))
    return pl.pallas_call(
        expert_grad_body,
        grid=(features // size,),
        in_specs=[cols] * 4 + [whole] * 6,
        out_specs=[
            pl.BlockSpec((size, width), lambda i: (i, 0)),
            pl.BlockSpec((size, width), lambda i: (i, 0)),
            pl.BlockSpec((width, size), lambda i: (0, i)),
        ],
        out_shape=[
            jax.ShapeDtypeStruct((features, width), F32),
            jax.ShapeDtypeStruct((features, width), F32),
            jax.ShapeDtypeStruct((width, features), F32),
        ],
        compiler_params=params(),
        name="expert_grad",
    )(*xs, *dys, *hs, *gs, *us)


def spread_body(table_ref, *refs, groups, pairs, count):
    owns, fars = refs[:count], refs[count : 2 * count]
    grads, row_ref, col_ref = refs[2 * count : 3 * count], refs[3 * count], refs[3 * count + 1]
    core = table_ref[0]
    rows = owns[0].shape[1]
    row_ref[...] = jnp.zeros_like(row_ref)
    for m in range(count):

        def column(w2, carry, m=m):
            for j, source in enumerate((owns[m], fars[m])):
                w = 2 * w2 + (core if j == 0 else 1 - core)
                total = jnp.zeros((1, LANES), F32)
                for n in range(groups):
                    at = table_ref[1 + (m * groups + n) * pairs + w2]
                    block = source[at].astype(F32)
                    place = pl.multiple_of(w * LANES, LANES)
                    grads[m][n * rows : (n + 1) * rows, pl.ds(place, LANES)] = block
                    square = block * block
                    total = total + jnp.sum(square, axis=0, keepdims=True)
                    row_ref[m, n * rows : (n + 1) * rows, :] += square
                col_ref[m, w] = total
            return carry

        lax.fori_loop(0, pairs, column, 0)


def spread_call(table, gathered, groups, features):
    pairs = features // (2 * LANES)
    count = len(gathered)
    owns = [g[0] for g in gathered]
    fars = [g[1] for g in gathered]
    out = pl.pallas_call(
        functools.partial(spread_body, groups=groups, pairs=pairs, count=count),
        in_specs=[smem()] + [vmem()] * (2 * count),
        out_specs=[vmem()] * (count + 2),
        out_shape=[jax.ShapeDtypeStruct((features, features), F32)] * count
        + [
            jax.ShapeDtypeStruct((count, features, LANES), F32),
            jax.ShapeDtypeStruct((count, 2 * pairs, 1, LANES), F32),
        ],
        compiler_params=params(),
        name="spread",
    )(table, *owns, *fars)
    row_sums = jnp.sum(out[count], axis=2)
    col_sums = out[count + 1].reshape(count, features)
    return out[:count], row_sums, col_sums


def on_device(
    tokens,
    attn_gain,
    qkv_weights,
    out_weight,
    rel_bias,
    moe_gain,
    router,
    gate_weight,
    up_weight,
    down_weight,
    expert_ids,
    expert_slots,
    buckets,
    upstream,
):
    length, features = tokens.shape
    bucket_count, head_count = rel_bias.shape
    head_dim = features // head_count
    groups = lax.axis_size("narrow")
    wide_count = lax.axis_size("wide")
    my_narrow = lax.axis_index("narrow")
    my_wide = lax.axis_index("wide")
    my_core = my_wide % 2
    part_width = gate_weight.shape[3]
    experts = router.shape[1] * wide_count
    places = experts // groups
    split_parts = wide_count // places
    capacity = (10 * length // experts + 3) // 4
    half_cap = capacity // 2
    slot_total = experts * capacity
    row_count, col_count = qkv_weights.shape[1:]
    half_wide = wide_count // 2
    orders = hop_orders(groups, wide_count)
    all_hops = orders[0]
    slots = [block_slots(order, groups, wide_count) for order in orders]
    direct = col_count % LANES == 0
    pairs = features // (2 * LANES)
    if direct:
        core_entry, tables = my_core, slots
    else:
        core_entry = jnp.int32(0)
        tables = [jnp.arange(groups * pairs, dtype=jnp.int32)] * 3

    def table_of(items):
        return jnp.concatenate(
            [jnp.reshape(core_entry, (1,)).astype(jnp.int32)] + [t.reshape(-1) for t in items]
        )

    qkv_table = table_of(tables)

    def gather_matrix(block, order, slot):
        gathered = gather_blocks(block, order)
        if direct:
            return gathered
        blocks = from_matrix(as_matrix(*gathered, slot, my_core), groups, pairs)
        blocks = blocks.reshape((groups * pairs,) + blocks.shape[2:])
        return blocks[:, 0], blocks[:, 1]

    def reduce_matrix(keep, send, order, slot):
        if direct:
            return scatter_sum(keep, send, order)
        both = jnp.stack([keep, send.astype(F32)], axis=1).reshape(
            groups, pairs, 2, features // groups, LANES
        )
        matrix = jnp.transpose(both, (0, 3, 1, 2, 4)).reshape(features, features)
        parts = from_matrix(matrix, groups, half_wide)
        placed = jnp.zeros((groups * half_wide,) + parts.shape[2:], F32)
        placed = placed.at[slot.reshape(-1)].set(parts.reshape(placed.shape))
        mine = jnp.where(my_core == 0, placed[:, 0], placed[:, 1])
        theirs = jnp.where(my_core == 0, placed[:, 1], placed[:, 0])
        return scatter_sum(mine, theirs.astype(BF), order)

    qkv_low = qkv_weights.astype(BF)
    qkv_parts = [gather_matrix(qkv_low[m], orders[m], slots[m]) for m in range(3)]
    table_hot = (
        jnp.pad(buckets, (0, 1), constant_values=-1)[:, None]
        == jnp.arange(bucket_count, dtype=jnp.int32)[None, :]
    ).astype(F32)
    bias_table = jnp.dot(table_hot, rel_bias, precision=lax.Precision.HIGHEST).T

    owner_slot = expert_ids % groups * places + expert_ids // groups
    kept_pairs = expert_slots >= 0
    row_ids = jnp.where(kept_pairs, owner_slot * capacity + expert_slots, -1)
    slot_ids = jnp.arange(slot_total, dtype=jnp.int32)
    route = [(slot_ids[:, None] == row_ids[:, c][None, :]).astype(BF) for c in range(2)]
    both_route = route[0] + route[1]

    def dispatch(slot_rows):
        width = slot_rows.shape[-1]
        shaped = slot_rows.reshape(groups, places, 1, 2, half_cap, width)
        copies = jnp.broadcast_to(
            shaped, (groups, places, split_parts // 2, 2, half_cap, width)
        ).reshape(groups * wide_count, half_cap, width)
        mine = lax.all_to_all(copies, ("narrow", "wide"), split_axis=0, concat_axis=0, tiled=True)
        return mine.reshape(-1, width), from_partner(mine, ("wide", 0)).reshape(-1, width)

    def collect(partials):
        mine = (
            partials[0].astype(F32) + from_partner(partials[1], ("wide", 0)).astype(F32)
        ).astype(BF)
        back = lax.all_to_all(
            mine.reshape(groups * wide_count, half_cap, features),
            ("narrow", "wide"),
            split_axis=0,
            concat_axis=0,
            tiled=True,
        ).reshape(groups, places, split_parts // 2, 2, half_cap, features)
        return jnp.transpose(back, (2, 0, 1, 3, 4, 5)).reshape(
            split_parts // 2 * slot_total, features
        )

    id_lanes = jnp.broadcast_to(
        expert_ids.astype(BF)[:, ::-1, None], (length, 2, LANES)
    )
    upstream_rows = jnp.concatenate(
        [
            mm(both_route, upstream),
            mm(route[0], id_lanes[:, 0]) + mm(route[1], id_lanes[:, 1]),
        ],
        axis=1,
    ).astype(BF)
    upstream_rows, _ = lax.optimization_barrier((upstream_rows, qkv_parts))
    upstream_got = dispatch(upstream_rows)

    normed_in, heads, probs, attended = attend_call(
        qkv_table, tokens, attn_gain, bias_table, qkv_parts, groups, head_dim
    )
    out_block = jnp.concatenate([out_weight.astype(BF), router.astype(BF)], axis=1)
    gathered_out = gather_blocks(out_block, orders[0])
    matrix_out = as_matrix(*gathered_out, slots[0], my_core).reshape(
        features, wide_count, col_count + router.shape[1]
    )
    full_out = matrix_out[:, :, :col_count].reshape(features, features)
    full_router = matrix_out[:, :, col_count:].reshape(features, experts)
    attended_rows = jnp.transpose(attended, (1, 0, 2)).reshape(length, features)
    inputs = tokens.astype(F32)
    hidden_x1 = inputs + mm(attended_rows, full_out)
    moe_factor = lax.rsqrt(jnp.mean(hidden_x1 * hidden_x1, axis=-1, keepdims=True) + NORM_EPS)
    moe_input = (hidden_x1 * moe_factor * moe_gain).astype(BF)
    expert_rows = dispatch(mm(both_route, moe_input).astype(BF))

    logits = mm(moe_input, full_router)
    pick_mask = expert_ids[:, :, None] == jnp.arange(experts, dtype=jnp.int32)[None, None, :]
    picked = jnp.sum(jnp.where(pick_mask, logits[:, None, :], 0.0), axis=2)
    gate_values = jax.nn.softmax(picked, axis=1)

    pad_width = -part_width % (2 * LANES)
    gate_low = jnp.pad(gate_weight[0, 0].astype(BF), ((0, 0), (0, pad_width)))
    up_low = jnp.pad(up_weight[0, 0].astype(BF), ((0, 0), (0, pad_width)))
    down_low = jnp.pad(down_weight[0, 0].astype(BF), ((0, pad_width), (0, 0)))
    router_wide = jnp.pad(full_router, ((0, 0), (0, -experts % LANES)))
    my_expert = (my_narrow + groups * (my_wide // split_parts)).reshape(1).astype(jnp.int32)
    done = [
        expert_call(my_expert, x, u, router_wide, gate_low, up_low, down_low)
        for x, u in zip(expert_rows, upstream_got)
    ]
    outputs_back = collect([d[0] for d in done])
    inputs_back = collect([d[1] for d in done])
    gate_local, up_local, down_local = expert_grad_call(
        expert_rows,
        [d[5] for d in done],
        [d[2] for d in done],
        [d[3] for d in done],
        [d[4] for d in done],
        part_width,
    )

    def pick(routes, rows):
        return sum(
            mm(routes, rows[h * slot_total : (h + 1) * slot_total], TN)
            for h in range(split_parts // 2)
        )

    first_rows = pick(route[0], outputs_back)
    second_rows = pick(route[1], outputs_back)
    moe_sum = gate_values[:, 0:1] * first_rows + gate_values[:, 1:2] * second_rows
    block_out = (hidden_x1 + moe_sum).astype(BF)
    cotangent = upstream.astype(F32)
    pair_grad = jnp.stack(
        [jnp.sum(cotangent * first_rows, axis=1), jnp.sum(cotangent * second_rows, axis=1)], axis=1
    )
    logit_pair = gate_values * (pair_grad - jnp.sum(gate_values * pair_grad, axis=1, keepdims=True))
    logit_grad = jnp.sum(jnp.where(pick_mask, logit_pair[:, :, None], 0.0), axis=1).astype(BF)
    router_local = mm(moe_input, logit_grad, TN)
    moe_input_grad = pick(both_route, inputs_back) + mm(logit_grad, full_router, NT)
    hat = hidden_x1 * moe_factor
    moe_gain_local = jnp.sum(moe_input_grad * hat, axis=0)
    scaled = moe_input_grad * moe_gain
    inner = jnp.mean(scaled * hat, axis=-1, keepdims=True)
    x1_grad = cotangent + moe_factor * (scaled - hat * inner)
    branch_grad = x1_grad.astype(BF)
    out_local = mm(attended_rows, branch_grad, TN)
    attended_grad = mm(branch_grad, full_out, NT).astype(BF)
    attended_grad = jnp.transpose(attended_grad.reshape(length, 2 * pairs, LANES), (1, 0, 2))

    out_parts = from_matrix(out_local, groups, half_wide).reshape(
        groups * half_wide, 2, row_count, col_count
    )
    back_slots = jnp.argsort(slots[0].reshape(-1))
    out_parts = jnp.take(out_parts, back_slots, axis=0)
    out_keep = jnp.where(my_core == 0, out_parts[:, 0], out_parts[:, 1])
    out_send = jnp.where(my_core == 0, out_parts[:, 1], out_parts[:, 0]).astype(BF)
    out_mine = scatter_sum(out_keep, out_send, orders[0])
    out_total_parts = gather_matrix(out_mine.astype(BF), orders[0], slots[0])

    keeps, sends, dheads, diag = attend_back_call(
        qkv_table, normed_in, heads, probs, attended_grad, groups, head_dim
    )
    qkv_mine = [reduce_matrix(keeps[m], sends[m], orders[m], slots[m]) for m in range(3)]
    qkv_total_parts = [
        gather_matrix(qkv_mine[m].astype(BF), orders[m], slots[m]) for m in range(3)
    ]
    tokens_grad, attn_gain_local = tokens_back_call(
        qkv_table, tokens, attn_gain, x1_grad, dheads, qkv_parts, groups
    )
    tail = jnp.pad(diag, ((0, 0), (0, 0), (0, 8)))
    line = sum(tail[:, s, s : s + 2 * length] for s in range(8))
    bias_local = jnp.dot(line, table_hot, precision=lax.Precision.HIGHEST).T

    small = jnp.concatenate(
        [
            attn_gain_local.reshape(-1),
            moe_gain_local,
            bias_local.reshape(-1),
            router_local.reshape(-1),
        ]
    )
    small = cube_sum(small.reshape(-1, LANES), all_hops).reshape(-1)
    gain_a_total = small[:features]
    gain_m_total = small[features : 2 * features]
    bias_size = bucket_count * head_count
    bias_total = small[2 * features : 2 * features + bias_size].reshape(bucket_count, head_count)
    router_total = small[2 * features + bias_size :].reshape(features, experts)

    local_sums = jnp.stack(
        [
            jnp.sum(gate_local * gate_local, axis=1),
            jnp.sum(up_local * up_local, axis=1),
            jnp.sum(down_local * down_local, axis=0),
        ],
        axis=0,
    )
    part_stats = (
        jnp.stack(
            [
                jnp.mean(gate_local * gate_local, axis=0),
                jnp.mean(up_local * up_local, axis=0),
                jnp.mean(down_local * down_local, axis=1),
            ],
            axis=0,
        )
        + STAT_EPS
    )
    wide_sums = cube_sum(
        local_sums, [("wide", bit) for bit in range(split_parts.bit_length() - 1)]
    )
    wide_stats = wide_sums / (part_width * split_parts) + STAT_EPS
    gate_new = factored(
        gate_weight[0, 0], gate_local, wide_stats[0], part_stats[0], jnp.mean(wide_stats[0])
    )
    up_new = factored(
        up_weight[0, 0], up_local, wide_stats[1], part_stats[1], jnp.mean(wide_stats[1])
    )
    down_new = factored(
        down_weight[0, 0], down_local, part_stats[2], wide_stats[2], jnp.mean(wide_stats[2])
    )

    grads, row_sums, col_sums = spread_call(
        table_of(tables + [tables[0]]), qkv_total_parts + [out_total_parts], groups, features
    )
    qkv_total = jnp.stack(grads[:3], axis=0)
    out_total = grads[3]
    attn_rows = row_sums / features + STAT_EPS
    attn_cols = col_sums / features + STAT_EPS
    attn_means = jnp.mean(attn_rows, axis=1)
    rows_mine = lax.dynamic_slice_in_dim(attn_rows, my_narrow * row_count, row_count, 1)
    cols_mine = lax.dynamic_slice_in_dim(attn_cols, my_wide * col_count, col_count, 1)
    attn_block = jnp.stack(qkv_mine + [out_mine], axis=0)
    qkv_new = factored(qkv_weights, attn_block[:3], rows_mine[:3], cols_mine[:3], attn_means[:3])
    out_step = adafactor_step(attn_block[3], rows_mine[3], cols_mine[3], attn_means[3])
    qkv_stats = jnp.stack([attn_rows[:3], attn_cols[:3]], axis=0)
    out_stats = jnp.stack([attn_rows[3], attn_cols[3]], axis=0)
    router_sq = router_total * router_total
    router_rows = jnp.mean(router_sq, axis=1) + STAT_EPS
    router_cols = jnp.mean(router_sq, axis=0) + STAT_EPS
    router_row_count, router_col_count = router.shape
    router_row_first = my_narrow * router_row_count
    router_col_first = my_wide * router_col_count
    router_block = lax.dynamic_slice(
        router_total, (router_row_first, router_col_first), (router_row_count, router_col_count)
    )
    router_new = factored(
        router,
        router_block,
        lax.dynamic_slice_in_dim(router_rows, router_row_first, router_row_count, 0),
        lax.dynamic_slice_in_dim(router_cols, router_col_first, router_col_count, 0),
        jnp.mean(router_rows),
    )
    return (
        block_out,
        tokens_grad,
        gain_a_total,
        qkv_total,
        out_total,
        bias_total,
        gain_m_total,
        router_total,
        gate_local[None, None],
        up_local[None, None],
        down_local[None, None],
        qkv_new,
        out_step,
        router_new,
        gate_new[None, None],
        up_new[None, None],
        down_new[None, None],
        qkv_stats,
        out_stats,
        router_rows,
        router_cols,
        wide_stats[None, None],
        part_stats[None, None],
    )


def solution(mesh):
    in_specs = (
        P(("narrow", "wide"), None),
        P(),
        P(None, "narrow", "wide"),
        P("narrow", "wide"),
        P(),
        P(),
        P("narrow", "wide"),
        P("narrow", "wide", None, None),
        P("narrow", "wide", None, None),
        P("narrow", "wide", None, None),
        P(("narrow", "wide"), None),
        P(("narrow", "wide"), None),
        P(),
        P(("narrow", "wide"), None),
    )
    out_specs = (
        P(("narrow", "wide"), None),
        P(("narrow", "wide"), None),
        P(),
        P(),
        P(),
        P(),
        P(),
        P(),
        P("narrow", "wide", None, None),
        P("narrow", "wide", None, None),
        P("narrow", "wide", None, None),
        P(None, "narrow", "wide"),
        P("narrow", "wide"),
        P("narrow", "wide"),
        P("narrow", "wide", None, None),
        P("narrow", "wide", None, None),
        P("narrow", "wide", None, None),
        P(),
        P(),
        P(),
        P(),
        P("narrow", "wide", None, None),
        P("narrow", "wide", None, None),
    )
    return jax.shard_map(
        on_device, mesh=mesh, in_specs=in_specs, out_specs=out_specs, check_vma=False
    )
```

time: 1530 us -> 674 us (0.44)
  local copies, waits for them, and re-layouts: 711 us -> 86.3 us
  blocking collectives: 289 us -> 0 us
  Pallas kernels: 0 us -> 120 us
  matrix products: 105 us -> 13.5 us
  starting transfers between devices: 13.2 us -> 86.2 us
  waiting for transfers between devices: 327 us -> 268 us
  other arithmetic: 54 us -> 87.6 us
    gather x8 -> x2, local copies, waits for them, and re-layouts: 654 us -> 11.5 us  [the longest x1 6.34 us: as_matrix(): picked = jnp.take(both, slots.reshape(-1), axis=0)]
    psum x1 -> x0, waiting for transfers between devices: 170 us -> none  [on_device(): lax.psum((qkv_local, out_local, router_local, attn_gain_local, moe_gain_l...]
    ppermute x2 -> x71, waiting for transfers between devices: 3.08 us -> 152 us  [from_partner(): return lax.ppermute(value, axis, pairs)]
    all_to_all x1 -> x0, blocking collectives: 131 us -> none  [on_device(): lax.all_to_all(spread(slot_grads).reshape(groups * wide_count, capacity,...]
    pallas_call x0 -> x7, Pallas kernels: none -> 120 us  [the longest x2 43.7 us: expert_call(): pl.pallas_call(expert_body, grid_spec=pltpu.PrefetchScalarGridSpec(num_sc...]
    all_gather x3 -> x0, blocking collectives: 115 us -> none  [the longest x1 92.1 us: on_device(): lax.all_gather(router_low, 'wide', axis=1, tiled=True)]
    dot_general x24 -> x17, matrix products: 105 us -> 12.6 us  [the longest x16 12.2 us: mm(): return lax.dot_general(a, b, dims, preferred_element_type=F32)]
    ppermute x2 -> x71, starting transfers between devices: 1.79 us -> 68.4 us  [from_partner(): return lax.ppermute(value, axis, pairs)]
  transfers between devices with their start and end apart: 9 -> 75, of which waited for: 6 -> 35; matrix products, arithmetic and copies ran while one was open for 48% -> 21% of each run, Pallas kernels for 0% -> 9%
where the time goes in v1:
time: 674 us; the launch traced here: 668 us
  waiting for transfers between devices  268 us (40%)
  Pallas kernels  120 us (18%)
  other arithmetic  87.6 us (13%)
  local copies, waits for them, and re-layouts  86.3 us (13%)
  starting transfers between devices  86.2 us (13%)
  matrix products  13.5 us (2%)
    ppermute x71, waiting for transfers between devices, from_partner(): return lax.ppermute(value, axis, pairs)  152 us
    ppermute x71, starting transfers between devices, from_partner(): return lax.ppermute(value, axis, pairs)  68.4 us
    all_to_all x2, waiting for transfers between devices, dispatch(): lax.all_to_all(copies, ('narrow', 'wide'), split_axis=0, concat_axis=0, t...  61.1 us
    all_to_all x2, waiting for transfers between devices, collect(): lax.all_to_all(mine.reshape(groups * wide_count, half_cap, features), ('n...  54.7 us
    pallas_call x2, Pallas kernels, expert_call(): pl.pallas_call(expert_body, grid_spec=pltpu.PrefetchScalarGridSpec(num_sc...  43.7 us
    unnamed x166, local copies, waits for them, and re-layouts  33.7 us
    pallas_call x1, Pallas kernels, expert_grad_call(): pl.pallas_call(expert_grad_body, grid=(features // size,), in_specs=[cols...  19.4 us
    pallas_call x1, Pallas kernels, attend_back_call(): pl.pallas_call(body, in_specs=[smem()] + [vmem()] * 4, out_specs=[vmem()]...  17.1 us
  transfers between devices with their start and end apart: 75, of which 35 were waited for; matrix products, arithmetic and copies ran while one was open for 21% of the time, Pallas kernels for 9%

profile of v1, /device:TPU:0, one launch (start us, length us, event | category | flops | bytes accessed | tf_op | source)
XLA Modules:
  0.0 667.7 jit_solution(6101856517689711664)
XLA Ops:
  1.8 4.1 collective-permute-start
  30.4 8.9 %collective-permute-done.3 = bf16[8,256,128]{2,1,0:T(8,128)(2,1)S(1)} collective-permute-done((bf16[8,256,128]{2,1,0:T(8,128)(2,1)S(1)}, bf16[8,256,128]{2,1,0:T(8,128)(2,1)S(1)}, u32[]{:S(2)}, u32[]{:S(2)}) %collective-permute-start.3) | collective-permute-done | bytes 524320 | tf_op jit(solution)/shard_map/ppermute | solution.py:32
  47.9 5.8 all-to-all-start.1
  56.6 67.4 %collective-permute-done.15 = bf16[1,256,129]{1,2,0:T(8,128)(2,1)S(1)} collective-permute-done((bf16[1,256,129]{1,2,0:T(8,128)(2,1)S(1)}, bf16[1,256,129]{1,2,0:T(8,128)(2,1)S(1)}, u32[]{:S(2)}, u32[]{:S(2)}) %collective-permute-start.15) | collective-permute-done | bytes 66080 | tf_op jit(solution)/shard_map/ppermute | solution.py:32
  125.2 4.1 collective-permute-done.16
  131.0 5.9 collective-permute-done.17
  137.9 11.1 %collective-permute-done.18 = bf16[8,256,129]{1,0,2:T(8,128)(2,1)S(1)} collective-permute-done((bf16[8,256,129]{1,0,2:T(8,128)(2,1)S(1)}, bf16[8,256,129]{1,0,2:T(8,128)(2,1)S(1)}, u32[]{:S(2)}, u32[]{:S(2)}) %collective-permute-start.18) | collective-permute-done | bytes 528416 | tf_op jit(solution)/shard_map/ppermute | solution.py:32
  153.7 15.9 %attend.1 = (bf16[256,1024]{1,0:T(8,128)(2,1)}, bf16[3,8,256,128]{3,2,1,0:T(8,128)(2,1)}, f32[16,256,256]{2,1,0:T(8,128)}, bf16[8,256,128]{2,1,0:T(8,128)(2,1)}) custom-call(s32[49]{0:T(128)} %pad_add_fusion.table_ref, bf16[256,1024]{1,0:T(8,128)(2,1)} %tokens_ref.3, f32[1,1024]{1,0:T(1,128)} %bitcast.233, f32[16,512]{1,0:T(8,128)} %convolution_bitcast_fusion.bias_ref, ...), custom_call_target="tpu_custom_call" | custom-call | tf_op jit(solution)/shard_map/attend/pallas_call | solution.py:188
  175.7 4.8 pad_maximum_fusion.1
  180.5 6.3 gather_fusion
  186.9 4.0 fusion.3
  190.9 3.9 reshape_reshape.3
  201.6 4.5 all-to-all-start
  206.4 61.1 %all-to-all-done = bf16[32,40,1024]{2,1,0:T(8,128)(2,1)} async-done(((bf16[32,40,1024]{2,1,0:T(8,128)(2,1)}), bf16[32,40,1024]{2,1,0:T(8,128)(2,1)}, u32[]{:S(2)}, u32[]{:S(2)}) %all-to-all-start) | async-done | bytes 2621472 | tf_op jit(solution)/shard_map/all_to_all | solution.py:578
  280.6 21.8 %expert.3 = (bf16[1280,1024]{1,0:T(8,128)(2,1)}, bf16[1280,1024]{1,0:T(8,128)(2,1)}, bf16[1280,768]{1,0:T(8,128)(2,1)}, bf16[1280,768]{1,0:T(8,128)(2,1)}, bf16[...) custom-call(s32[1]{0:T(128)} %bitcast.15.expert_ref, bf16[1280,1024]{1,0:T(8,128)(2,1)} %bitcast.26.x_ref.xb, ...), custom_call_target="tpu_custom_call" | custom-call | tf_op jit(solution)/shard_map/expert/pallas_call | solution.py:377
  303.0 21.8 %expert.2 = (bf16[1280,1024]{1,0:T(8,128)(2,1)}, bf16[1280,1024]{1,0:T(8,128)(2,1)}, bf16[1280,768]{1,0:T(8,128)(2,1)}, bf16[1280,768]{1,0:T(8,128)(2,1)}, bf16[...) custom-call(s32[1]{0:T(128)} %bitcast.15.expert_ref, bf16[1280,1024]{1,0:T(8,128)(2,1)} %bitcast.19.x_ref.xa, ...), custom_call_target="tpu_custom_call" | custom-call | tf_op jit(solution)/shard_map/expert/pallas_call | solution.py:377
  324.8 5.3 add_convert_fusion.1
  339.1 5.3 add_convert_fusion
  344.4 50.8 %all-to-all-done.2 = bf16[32,40,1024]{2,1,0:T(8,128)(2,1)} async-done(((bf16[32,40,1024]{2,1,0:T(8,128)(2,1)}), bf16[32,40,1024]{2,1,0:T(8,128)(2,1)}, u32[]{:S(2)}, u32[]{:S(2)}) %all-to-all-start.2) | async-done | bytes 2621472 | tf_op jit(solution)/shard_map/all_to_all | solution.py:585
  401.0 19.4 %expert_grad.1 = (f32[1024,704]{1,0:T(8,128)}, f32[1024,704]{1,0:T(8,128)}, f32[704,1024]{1,0:T(8,128)}) custom-call(bf16[1280,1024]{1,0:T(8,128)(2,1)} %bitcast.19.x_ref.xa, bf16[1280,1024]{1,0:T(8,128)(2,1)} %bitcast.26.x_ref.xb, bf16[1280,1024]{1,0:T(8,128)(2,1)} %get-tuple-element.76.dya, bf16[1280,1024]{1,0:T(8,128)(2,1)} %get-tuple-element.77.dyb, ...), custom_call_target="tpu_custom_call" | custom-call | tf_op jit(solution)/shard_map/expert_grad/pallas_call | solution.py:417
  436.1 6.1 collective-permute-done.70
  445.4 5.4 fusion.1
  456.4 3.9 all-to-all-done.3
  471.1 17.1 %attend_back.1 = (f32[3,16,256,128]{3,2,1,0:T(8,128)}, bf16[3,16,256,128]{3,2,1,0:T(8,128)(2,1)}, bf16[3,8,256,128]{3,2,1,0:T(8,128)(2,1)}, f32[16,8,512]{2,1,0:T(8,128)}) custom-call(s32[49]{0:T(128)} %pad_add_fusion.table_ref, bf16[256,1024]{1,0:T(8,128)(2,1)} %get-tuple-element.62.normed_ref, bf16[3,8,256,128]{3,2,1,0:T(8,128)(2,1)} %get-tuple-element.63.heads_ref, ...), custom_call_target="tpu_custom_call" | custom-call | tf_op jit(solution)/shard_map/attend_back/pallas_call | solution.py:261
  491.5 10.4 %tokens_back.1 = (bf16[256,1024]{1,0:T(8,128)(2,1)}, f32[1,1024]{1,0:T(1,128)}) custom-call(s32[49]{0:T(128)} %pad_add_fusion.table_ref, bf16[256,1024]{1,0:T(8,128)(2,1)} %tokens_ref.3, f32[1,1024]{1,0:T(1,128)} %bitcast.234, f32[256,1024]{1,0:T(8,128)} %copy-done.13, bf16[3,8,256,128]{3,2,1,0:T(8,128)(2,1)} %get-tuple-element.65.dheads_ref, ...), custom_call_target="tpu_custom_call" | custom-call | tf_op jit(solution)/shard_map/tokens_back/pallas_call | solution.py:313
  512.1 5.1 gather_fusion.1
  526.1 5.1 bitcast_add_fusion.1
  551.8 5.6 collective-permute-done.39
  614.9 6.6 collective-permute-done.37
  624.0 4.4 collective-permute-done.64
  635.1 14.1 %spread.1 = (f32[1024,1024]{1,0:T(8,128)}, f32[1024,1024]{1,0:T(8,128)}, f32[1024,1024]{1,0:T(8,128)}, f32[1024,1024]{1,0:T(8,128)}, f32[4,1024,128]{2,1,0:T(8,128)}, /*index=5*/f32[4,8,1,128]{3,2,1,0:T(1,128)}) custom-call(s32[65]{0:T(128)} %concatenate.167.table_ref, bf16[16,256,128]{2,1,0:T(8,128)(2,1)} %copy-done.35, ...), custom_call_target="tpu_custom_call" | custom-call | tf_op jit(solution)/shard_map/spread/pallas_call | solution.py:467
  654.3 10.7 %pad_maximum_fusion = f32[3,1024,1024]{2,1,0:T(8,128)} fusion(f32[1,1024,1024]{2,1,0:T(8,128)} %bitcast.197, f32[1,1024,1024]{2,1,0:T(8,128)} %bitcast.196, f32[1,1024,1024]{2,1,0:T(8,128)} %bitcast.195), kind=kLoop, calls=%fused_computation.2 | loop fusion | flops 6291456 | bytes 25165824 | tf_op jit(solution)/shard_map/stack | solution.py:755
  (518 shorter events, 235.4 us)
Async XLA Ops:
  26.1 13.2 %collective-permute-start.3 = (bf16[8,256,128]{2,1,0:T(8,128)(2,1)S(1)}, bf16[8,256,128]{2,1,0:T(8,128)(2,1)S(1)}, u32[]{:S(2)}, u32[]{:S(2)}) collective-permute-start(bf16[8,256,128]{2,1,0:T(8,128)(2,1)S(1)} %pad_maximum_fusion.4), channel_id=1, source_target_pairs={{0,2},{1,3},{2,0},{3,1},{4,6},{5,7},{6,4},{7,5},{8,10},{9,11},{10,... | collective-permute-start | bytes 1572872 | tf_op jit(solution)/shard_map/ppermute | solution.py:32
  27.1 12.4 %collective-permute-start.7 = (bf16[8,256,128]{2,1,0:T(8,128)(2,1)S(1)}, bf16[8,256,128]{2,1,0:T(8,128)(2,1)S(1)}, u32[]{:S(2)}, u32[]{:S(2)}) collective-permute-start(bf16[8,256,128]{2,1,0:T(8,128)(2,1)S(1)} %pad_maximum_fusion.5), channel_id=1, source_target_pairs={{0,16},{8,24},{16,0},{24,8},{1,17},{9,25},{17,1},{25,9},{2,18},{10... | collective-permute-start | bytes 1572872 | tf_op jit(solution)/shard_map/ppermute | solution.py:32
  28.7 12.0 %collective-permute-start.11 = (bf16[8,256,128]{2,1,0:T(8,128)(2,1)S(1)}, bf16[8,256,128]{2,1,0:T(8,128)(2,1)S(1)}, u32[]{:S(2)}, u32[]{:S(2)}) collective-permute-start(bf16[8,256,128]{2,1,0:T(8,128)(2,1)S(1)} %pad_maximum_fusion.6), channel_id=1, source_target_pairs={{0,8},{8,0},{16,24},{24,16},{1,9},{9,1},{17,25},{25,17},{2,10},{10... | collective-permute-start | bytes 1572872 | tf_op jit(solution)/shard_map/ppermute | solution.py:32
  47.9 151.9 %all-to-all-start.1 = ((bf16[32,40,1152]{2,1,0:T(8,128)(2,1)}), bf16[32,40,1152]{2,1,0:T(8,128)(2,1)}, u32[]{:S(2)}, u32[]{:S(2)}) async-start(bf16[32,40,1152]{2,1,0:T(8,128)(2,1)} %bitcast.21), calls=%async_computation.1 | async-start | bytes 5898240 | tf_op jit(solution)/shard_map/all_to_all | solution.py:578
  53.9 70.1 %collective-permute-start.15 = (bf16[1,256,129]{1,2,0:T(8,128)(2,1)S(1)}, bf16[1,256,129]{1,2,0:T(8,128)(2,1)S(1)}, u32[]{:S(2)}, u32[]{:S(2)}) collective-permute-start(bf16[1,256,129]{1,2,0:T(8,128)(2,1)S(1)} %maximum_bitcast_fusion), channel_id=1, source_target_pairs={{0,4},{1,5},{2,6},{3,7},{4,0},{5,1},{6,2},{7,3},{8,12},{9,13},{10,... | collective-permute-start | bytes 198152 | tf_op jit(solution)/shard_map/ppermute | solution.py:32
  137.1 11.9 %collective-permute-start.18 = (bf16[8,256,129]{1,0,2:T(8,128)(2,1)S(1)}, bf16[8,256,129]{1,0,2:T(8,128)(2,1)S(1)}, u32[]{:S(2)}, u32[]{:S(2)}) collective-permute-start(bf16[8,256,129]{1,0,2:T(8,128)(2,1)S(1)} %copy.241), channel_id=1, source_target_pairs={{0,2},{1,3},{2,0},{3,1},{4,6},{5,7},{6,4},{7,5},{8,10},{9,11},{10,... | collective-permute-start | bytes 1585160 | tf_op jit(solution)/shard_map/ppermute | solution.py:32
  151.7 19.2 %collective-permute-start.19 = (bf16[16,256,129]{1,0,2:T(8,128)(2,1)S(1)}, bf16[16,256,129]{1,0,2:T(8,128)(2,1)}, u32[]{:S(2)}, u32[]{:S(2)}) collective-permute-start(bf16[16,256,129]{1,0,2:T(8,128)(2,1)S(1)} %concatenate.164), channel_id=1, source_target_pairs={{0,1},{1,0},{2,3},{3,2},{4,5},{5,4},{6,7},{7,6},{8,9},{9,8},{10,11... | collective-permute-start | bytes 3170312 | tf_op jit(solution)/shard_map/ppermute | solution.py:32
  201.6 65.9 %all-to-all-start = ((bf16[32,40,1024]{2,1,0:T(8,128)(2,1)}), bf16[32,40,1024]{2,1,0:T(8,128)(2,1)}, u32[]{:S(2)}, u32[]{:S(2)}) async-start(bf16[32,40,1024]{2,1,0:T(8,128)(2,1)} %bitcast.18), calls=%async_computation | async-start | bytes 5242880 | tf_op jit(solution)/shard_map/all_to_all | solution.py:578
  206.2 74.4 %collective-permute-start.21 = (bf16[32,40,1152]{2,1,0:T(8,128)(2,1)}, bf16[32,40,1152]{2,1,0:T(8,128)(2,1)}, u32[]{:S(2)}, u32[]{:S(2)}) collective-permute-start(bf16[32,40,1152]{2,1,0:T(8,128)(2,1)} %all-to-all-done.1), channel_id=1, source_target_pairs={{0,1},{1,0},{2,3},{3,2},{4,5},{5,4},{6,7},{7,6},{8,9},{9,8},{10,11... | collective-permute-start | bytes 8847368 | tf_op jit(solution)/shard_map/ppermute | solution.py:32
  267.5 13.1 %collective-permute-start.20 = (bf16[32,40,1024]{2,1,0:T(8,128)(2,1)}, bf16[32,40,1024]{2,1,0:T(8,128)(2,1)}, u32[]{:S(2)}, u32[]{:S(2)}) collective-permute-start(bf16[32,40,1024]{2,1,0:T(8,128)(2,1)} %all-to-all-done), channel_id=1, source_target_pairs={{0,1},{1,0},{2,3},{3,2},{4,5},{5,4},{6,7},{7,6},{8,9},{9,8},{10,11... | collective-permute-start | bytes 7864328 | tf_op jit(solution)/shard_map/ppermute | solution.py:32
  302.4 22.4 %collective-permute-start.22 = (bf16[1280,1024]{1,0:T(8,128)(2,1)}, bf16[1280,1024]{1,0:T(8,128)(2,1)}, u32[]{:S(2)}, u32[]{:S(2)}) collective-permute-start(bf16[1280,1024]{1,0:T(8,128)(2,1)} %get-tuple-element.59), channel_id=1, source_target_pairs={{0,1},{1,0},{2,3},{3,2},{4,5},{5,4},{6,7},{7,6},{8,9},{9,8},{10,11... | collective-permute-start | bytes 7864328 | tf_op jit(solution)/shard_map/ppermute | solution.py:32
  330.1 65.0 %all-to-all-start.2 = ((bf16[32,40,1024]{2,1,0:T(8,128)(2,1)}), bf16[32,40,1024]{2,1,0:T(8,128)(2,1)}, u32[]{:S(2)}, u32[]{:S(2)}) async-start(bf16[32,40,1024]{2,1,0:T(8,128)(2,1)} %bitcast.186), calls=%async_computation.2 | async-start | bytes 5242880 | tf_op jit(solution)/shard_map/all_to_all | solution.py:585
  395.2 65.2 %all-to-all-start.3 = ((bf16[32,40,1024]{2,1,0:T(8,128)(2,1)}), bf16[32,40,1024]{2,1,0:T(8,128)(2,1)}, u32[]{:S(2)}, u32[]{:S(2)}) async-start(bf16[32,40,1024]{2,1,0:T(8,128)(2,1)} %bitcast.185), calls=%async_computation.3 | async-start | bytes 5242880 | tf_op jit(solution)/shard_map/all_to_all | solution.py:585
  426.7 15.4 %collective-permute-start.70 = (f32[3,1024]{1,0:T(4,128)S(1)}, f32[3,1024]{1,0:T(4,128)S(1)}, u32[]{:S(2)}, u32[]{:S(2)}) collective-permute-start(f32[3,1024]{1,0:T(4,128)S(1)} %fusion.67), channel_id=1, source_target_pairs={{0,2},{1,3},{2,0},{3,1},{4,6},{5,7},{6,4},{7,5},{8,10},{9,11},{10,... | collective-permute-start | bytes 36872 | tf_op jit(solution)/shard_map/ppermute | solution.py:32
  507.0 19.0 %collective-permute-start.47 = (bf16[16,256,128]{2,1,0:T(8,128)(2,1)}, bf16[16,256,128]{2,1,0:T(8,128)(2,1)}, u32[]{:S(2)}, u32[]{:S(2)}) collective-permute-start(bf16[16,256,128]{2,1,0:T(8,128)(2,1)} %get-tuple-element.313), channel_id=1, source_target_pairs={{0,1},{1,0},{2,3},{3,2},{4,5},{5,4},{6,7},{7,6},{8,9},{9,8},{10,11... | collective-permute-start | bytes 3145736 | tf_op jit(solution)/shard_map/ppermute | solution.py:32
  507.0 19.0 %collective-permute-start.38 = (bf16[16,256,128]{2,1,0:T(8,128)(2,1)}, bf16[16,256,128]{2,1,0:T(8,128)(2,1)}, u32[]{:S(2)}, u32[]{:S(2)}) collective-permute-start(bf16[16,256,128]{2,1,0:T(8,128)(2,1)} %get-tuple-element.314), channel_id=1, source_target_pairs={{0,1},{1,0},{2,3},{3,2},{4,5},{5,4},{6,7},{7,6},{8,9},{9,8},{10,11... | collective-permute-start | bytes 3145736 | tf_op jit(solution)/shard_map/ppermute | solution.py:32
  507.5 18.5 %collective-permute-start.29 = (bf16[16,256,128]{2,1,0:T(8,128)(2,1)S(1)}, bf16[16,256,128]{2,1,0:T(8,128)(2,1)}, u32[]{:S(2)}, u32[]{:S(2)}) collective-permute-start(bf16[16,256,128]{2,1,0:T(8,128)(2,1)S(1)} %get-tuple-element.315), channel_id=1, source_target_pairs={{0,1},{1,0},{2,3},{3,2},{4,5},{5,4},{6,7},{7,6},{8,9},{9,8},{10,11... | collective-permute-start | bytes 3145736 | tf_op jit(solution)/shard_map/ppermute | solution.py:32
  525.0 19.4 %collective-permute-start.56 = (bf16[16,256,128]{2,1,0:T(8,128)(2,1)}, bf16[16,256,128]{2,1,0:T(8,128)(2,1)}, u32[]{:S(2)}, u32[]{:S(2)}) collective-permute-start(bf16[16,256,128]{2,1,0:T(8,128)(2,1)} %fusion.7), channel_id=1, source_target_pairs={{0,1},{1,0},{2,3},{3,2},{4,5},{5,4},{6,7},{7,6},{8,9},{9,8},{10,11... | collective-permute-start | bytes 3145736 | tf_op jit(solution)/shard_map/ppermute | solution.py:32
  525.9 15.0 %collective-permute-start.28 = (f32[84,128]{1,0:T(8,128)S(1)}, f32[84,128]{1,0:T(8,128)S(1)}, u32[]{:S(2)}, u32[]{:S(2)}) collective-permute-start(f32[84,128]{1,0:T(8,128)S(1)} %add.293), channel_id=1, source_target_pairs={{0,1},{1,0},{2,3},{3,2},{4,5},{5,4},{6,7},{7,6},{8,9},{9,8},{10,11... | collective-permute-start | bytes 129032 | tf_op jit(solution)/shard_map/ppermute | solution.py:32
  532.2 17.3 %collective-permute-start.30 = (bf16[8,256,128]{2,1,0:T(8,128)(2,1)}, bf16[8,256,128]{2,1,0:T(8,128)(2,1)}, u32[]{:S(2)}, u32[]{:S(2)}) collective-permute-start(bf16[8,256,128]{2,1,0:T(8,128)(2,1)} %slice.569), channel_id=1, source_target_pairs={{0,2},{1,3},{2,0},{3,1},{4,6},{5,7},{6,4},{7,5},{8,10},{9,11},{10,... | collective-permute-start | bytes 1572872 | tf_op jit(solution)/shard_map/ppermute | solution.py:32
  542.6 14.8 %collective-permute-start.39 = (bf16[8,256,128]{2,1,0:T(8,128)(2,1)S(1)}, bf16[8,256,128]{2,1,0:T(8,128)(2,1)S(1)}, u32[]{:S(2)}, u32[]{:S(2)}) collective-permute-start(bf16[8,256,128]{2,1,0:T(8,128)(2,1)S(1)} %slice.568), channel_id=1, source_target_pairs={{0,16},{8,24},{16,0},{24,8},{1,17},{9,25},{17,1},{25,9},{2,18},{10... | collective-permute-start | bytes 1572872 | tf_op jit(solution)/shard_map/ppermute | solution.py:32
  543.8 14.4 %collective-permute-start.48 = (bf16[8,256,128]{2,1,0:T(8,128)(2,1)S(1)}, bf16[8,256,128]{2,1,0:T(8,128)(2,1)S(1)}, u32[]{:S(2)}, u32[]{:S(2)}) collective-permute-start(bf16[8,256,128]{2,1,0:T(8,128)(2,1)S(1)} %slice.567), channel_id=1, source_target_pairs={{0,8},{8,0},{16,24},{24,16},{1,9},{9,1},{17,25},{25,17},{2,10},{10... | collective-permute-start | bytes 1572872 | tf_op jit(solution)/shard_map/ppermute | solution.py:32
  547.4 14.8 %collective-permute-start.57 = (bf16[8,256,128]{2,1,0:T(8,128)(2,1)S(1)}, bf16[8,256,128]{2,1,0:T(8,128)(2,1)S(1)}, u32[]{:S(2)}, u32[]{:S(2)}) collective-permute-start(bf16[8,256,128]{2,1,0:T(8,128)(2,1)S(1)} %slice.566), channel_id=1, source_target_pairs={{0,2},{1,3},{2,0},{3,1},{4,6},{5,7},{6,4},{7,5},{8,10},{9,11},{10,... | collective-permute-start | bytes 1572872 | tf_op jit(solution)/shard_map/ppermute | solution.py:32
  550.7 12.8 %collective-permute-start.31 = (bf16[4,256,128]{2,1,0:T(8,128)(2,1)S(1)}, bf16[4,256,128]{2,1,0:T(8,128)(2,1)S(1)}, u32[]{:S(2)}, u32[]{:S(2)}) collective-permute-start(bf16[4,256,128]{2,1,0:T(8,128)(2,1)S(1)} %slice.573), channel_id=1, source_target_pairs={{0,16},{8,24},{16,0},{24,8},{1,17},{9,25},{17,1},{25,9},{2,18},{10... | collective-permute-start | bytes 786440 | tf_op jit(solution)/shard_map/ppermute | solution.py:32
  571.9 11.8 %collective-permute-start.42 = (bf16[1,256,128]{2,1,0:T(8,128)(2,1)S(1)}, bf16[1,256,128]{2,1,0:T(8,128)(2,1)S(1)}, u32[]{:S(2)}, u32[]{:S(2)}) collective-permute-start(bf16[1,256,128]{2,1,0:T(8,128)(2,1)S(1)} %slice.580), channel_id=1, source_target_pairs={{0,4},{1,5},{2,6},{3,7},{4,0},{5,1},{6,2},{7,3},{8,12},{9,13},{10,... | collective-permute-start | bytes 196616 | tf_op jit(solution)/shard_map/ppermute | solution.py:32
  575.1 12.9 %collective-permute-start.60 = (bf16[1,256,128]{2,1,0:T(8,128)(2,1)S(1)}, bf16[1,256,128]{2,1,0:T(8,128)(2,1)S(1)}, u32[]{:S(2)}, u32[]{:S(2)}) collective-permute-start(bf16[1,256,128]{2,1,0:T(8,128)(2,1)S(1)} %slice.578), channel_id=1, source_target_pairs={{0,4},{1,5},{2,6},{3,7},{4,0},{5,1},{6,2},{7,3},{8,12},{9,13},{10,... | collective-permute-start | bytes 196616 | tf_op jit(solution)/shard_map/ppermute | solution.py:32
  606.6 14.9 %collective-permute-start.37 = (bf16[8,256,128]{2,1,0:T(8,128)(2,1)S(1)}, bf16[8,256,128]{2,1,0:T(8,128)(2,1)S(1)}, u32[]{:S(2)}, u32[]{:S(2)}) collective-permute-start(bf16[8,256,128]{2,1,0:T(8,128)(2,1)S(1)} %pad_maximum_fusion.7), channel_id=1, source_target_pairs={{0,2},{1,3},{2,0},{3,1},{4,6},{5,7},{6,4},{7,5},{8,10},{9,11},{10,... | collective-permute-start | bytes 1572872 | tf_op jit(solution)/shard_map/ppermute | solution.py:32
  607.1 14.6 %collective-permute-start.46 = (bf16[8,256,128]{2,1,0:T(8,128)(2,1)S(1)}, bf16[8,256,128]{2,1,0:T(8,128)(2,1)S(1)}, u32[]{:S(2)}, u32[]{:S(2)}) collective-permute-start(bf16[8,256,128]{2,1,0:T(8,128)(2,1)S(1)} %pad_maximum_fusion.8), channel_id=1, source_target_pairs={{0,16},{8,24},{16,0},{24,8},{1,17},{9,25},{17,1},{25,9},{2,18},{10... | collective-permute-start | bytes 1572872 | tf_op jit(solution)/shard_map/ppermute | solution.py:32
  609.1 13.9 %collective-permute-start.55 = (bf16[8,256,128]{2,1,0:T(8,128)(2,1)S(1)}, bf16[8,256,128]{2,1,0:T(8,128)(2,1)S(1)}, u32[]{:S(2)}, u32[]{:S(2)}) collective-permute-start(bf16[8,256,128]{2,1,0:T(8,128)(2,1)S(1)} %pad_maximum_fusion.9), channel_id=1, source_target_pairs={{0,8},{8,0},{16,24},{24,16},{1,9},{9,1},{17,25},{25,17},{2,10},{10... | collective-permute-start | bytes 1572872 | tf_op jit(solution)/shard_map/ppermute | solution.py:32
  612.2 16.1 %collective-permute-start.64 = (bf16[8,256,128]{2,1,0:T(8,128)(2,1)S(1)}, bf16[8,256,128]{2,1,0:T(8,128)(2,1)S(1)}, u32[]{:S(2)}, u32[]{:S(2)}) collective-permute-start(bf16[8,256,128]{2,1,0:T(8,128)(2,1)S(1)} %pad_maximum_fusion.10), channel_id=1, source_target_pairs={{0,2},{1,3},{2,0},{3,1},{4,6},{5,7},{6,4},{7,5},{8,10},{9,11},{10,... | collective-permute-start | bytes 1572872 | tf_op jit(solution)/shard_map/ppermute | solution.py:32
  621.6 13.4 %collective-permute-start.65 = (bf16[16,256,128]{2,1,0:T(8,128)(2,1)S(1)}, bf16[16,256,128]{2,1,0:T(8,128)(2,1)}, u32[]{:S(2)}, u32[]{:S(2)}) collective-permute-start(bf16[16,256,128]{2,1,0:T(8,128)(2,1)S(1)} %constant_dynamic-update-slice_fusion.15.refs_0_), channel_id=1, source_target_pairs={{0,1},{1,0},{2,3},{3,2},{4,5},{5,4},{6,7},{7,6},{8,9},{9,8},{10,11... | collective-permute-start | bytes 3145736 | tf_op jit(solution)/shard_map/ppermute | solution.py:32
  622.6 12.4 %collective-permute-start.66 = (bf16[16,256,128]{2,1,0:T(8,128)(2,1)}, bf16[16,256,128]{2,1,0:T(8,128)(2,1)}, u32[]{:S(2)}, u32[]{:S(2)}) collective-permute-start(bf16[16,256,128]{2,1,0:T(8,128)(2,1)} %constant_dynamic-update-slice_fusion.20.refs_1_), channel_id=1, source_target_pairs={{0,1},{1,0},{2,3},{3,2},{4,5},{5,4},{6,7},{7,6},{8,9},{9,8},{10,11... | collective-permute-start | bytes 3145736 | tf_op jit(solution)/shard_map/ppermute | solution.py:32
  (111 other events, 1138.8 us)

commit v2 on v1

v2 whole, which is shorter than its diff:
```python
import functools

import jax
import jax.numpy as jnp
from jax import lax
from jax.experimental import pallas as pl
from jax.experimental.pallas import tpu as pltpu
from jax.sharding import PartitionSpec as P

NORM_EPS = 1e-06
STAT_EPS = 1e-06
STEP_RATE = 0.01
LANES = 128
GELU_C = 0.7978845608028654
GELU_A = 0.044715
BF = jnp.bfloat16
F32 = jnp.float32
VMEM_LIMIT = 60 * 1024 * 1024
NN = (((1,), (0,)), ((), ()))
NT = (((1,), (1,)), ((), ()))
TN = (((0,), (0,)), ((), ()))


def mm(a, b, dims=NN):
    return lax.dot_general(a, b, dims, preferred_element_type=F32)


def from_partner(value, hop):
    axis, bit = hop
    mask = 2**bit
    pairs = [(source, source ^ mask) for source in range(lax.axis_size(axis))]
    return lax.ppermute(value, axis, pairs)


def after(values, *others):
    return lax.optimization_barrier((values, others))[0]


def hop_orders(groups, wide_count):
    narrow = [("narrow", b) for b in range(groups.bit_length() - 1)]
    wide = [("wide", b) for b in range(1, wide_count.bit_length() - 1)]
    far, near = wide[1:][::-1], wide[:1]
    core = [("wide", 0)]
    return (
        far + narrow + near + core,
        far + near + narrow + core,
        far + narrow[1:] + near + narrow[:1] + core,
        far + narrow[:1] + near + narrow[1:] + core,
    )


def block_slots(order, groups, wide_count):
    n_ids = jnp.arange(groups, dtype=jnp.int32)[:, None]
    w_ids = 2 * jnp.arange(wide_count // 2, dtype=jnp.int32)[None, :]
    slots = jnp.zeros((groups, wide_count // 2), jnp.int32)
    for stage, (axis, bit) in enumerate(order[:-1]):
        ids = n_ids if axis == "narrow" else w_ids
        differs = ((ids ^ lax.axis_index(axis)) >> bit) & 1
        slots = slots | (differs << stage)
    return slots


def together(*values):
    return lax.optimization_barrier(values)


def shared_hops(orders):
    count = 0
    while len({order[count] for order in orders}) == 1 and count < len(orders[0]) - 1:
        count += 1
    return count


def grow(blocks, hop, axis=0):
    return jnp.concatenate([blocks, from_partner(blocks, hop)], axis=axis)


def gather_chains(blocks, orders):
    shared = shared_hops(orders)
    blocks = blocks[:, None]
    for hop in orders[0][:shared]:
        blocks = grow(blocks, hop, 1)
    chains = [blocks[i] for i in range(len(orders))]
    for stage in range(shared, len(orders[0]) - 1):
        chains = [grow(chain, order[stage]) for chain, order in zip(chains, orders)]
    return chains


def core_sum(keep, send, order):
    return keep + from_partner(send, order[-1]).astype(F32)


def halve(total, hop, axis=0):
    half = total.shape[axis] // 2
    mine = lax.slice_in_dim(total, 0, half, axis=axis)
    theirs = lax.slice_in_dim(total, half, 2 * half, axis=axis)
    return mine + from_partner(theirs.astype(BF), hop).astype(F32)


def send_step(state, hop):
    sources, places = state.shape[:2]
    split = state.reshape((sources, 2, places // 2) + state.shape[2:])
    return jnp.concatenate([split[:, 0], from_partner(split[:, 1], hop)], axis=0)


def return_step(state, hop):
    half = state.shape[0] // 2
    got = from_partner(state[half:], hop)
    return jnp.stack([state[:half], got], axis=1).reshape((half, -1) + state.shape[2:])


def row_slots(hops, groups, places, parts):
    n_ids = jnp.arange(groups, dtype=jnp.int32)[:, None]
    w_ids = parts * jnp.arange(places, dtype=jnp.int32)[None, :]
    slots = jnp.zeros((groups, places), jnp.int32)
    for axis, bit in hops:
        ids = n_ids if axis == "narrow" else w_ids
        slots = 2 * slots + (((ids ^ lax.axis_index(axis)) >> bit) & 1)
    return slots.reshape(-1)


def cube_sum(value, hops):
    for hop in hops:
        value = value + from_partner(value, hop)
    return value


def as_matrix(own, other, slots, my_core):
    groups, half_wide = slots.shape
    both = jnp.stack([jnp.where(my_core == 0, own, other), jnp.where(my_core == 0, other, own)], 1)
    picked = jnp.take(both, slots.reshape(-1), axis=0)
    rows, cols = own.shape[1:]
    picked = picked.reshape(groups, half_wide, 2, rows, cols)
    return jnp.transpose(picked, (0, 3, 1, 2, 4)).reshape(groups * rows, half_wide * 2 * cols)


def from_matrix(matrix, groups, half_wide):
    lead = matrix.shape[:-2]
    rows, cols = matrix.shape[-2] // groups, matrix.shape[-1] // (2 * half_wide)
    shaped = matrix.reshape(lead + (groups, rows, half_wide, 2, cols))
    k = len(lead)
    order = tuple(range(k)) + (k, k + 2, k + 3, k + 1, k + 4)
    return jnp.transpose(shaped, order)


def gelu_tanh(values):
    return jax.nn.gelu(values, approximate=True)


def adafactor_step(gradient, row_stats, col_stats, mean_rows):
    return (
        STEP_RATE
        * gradient
        / jnp.sqrt(row_stats[..., :, None] * col_stats[..., None, :] / mean_rows[..., None, None])
    )


def factored(weight, gradient, row_stats, col_stats, mean_rows):
    return weight - adafactor_step(gradient, row_stats, col_stats, mean_rows)


def vmem():
    return pl.BlockSpec(memory_space=pltpu.VMEM)


def smem():
    return pl.BlockSpec(memory_space=pltpu.SMEM)


def params():
    return pltpu.CompilerParams(vmem_limit_bytes=VMEM_LIMIT)


def lane_masks(head_dim):
    heads = LANES // head_dim
    ids = lax.broadcasted_iota(jnp.int32, (1, LANES), 1) // head_dim
    return [ids == i for i in range(heads)]


def attend_body(
    table_ref, tokens_ref, gain_ref, bias_ref,
    own_q, own_k, own_v, far_q, far_k, far_v,
    normed_ref, heads_ref, probs_ref, attended_ref,
    *, groups, pairs, head_dim,
):
    length, features = tokens_ref.shape
    rows = features // groups
    x = tokens_ref[...].astype(F32)
    factor = lax.rsqrt(jnp.mean(x * x, axis=-1, keepdims=True) + NORM_EPS)
    normed_ref[...] = (x * factor * gain_ref[...]).astype(BF)
    core = table_ref[0]

    def project(w2, carry):
        for m, (own, far) in enumerate(((own_q, far_q), (own_k, far_k), (own_v, far_v))):
            total = None
            for n in range(groups):
                at = table_ref[1 + (m * groups + n) * pairs + w2]
                block = jnp.concatenate([own[at], far[at]], axis=1)
                part = mm(normed_ref[:, n * rows : (n + 1) * rows], block)
                total = part if total is None else total + part
            total = total.astype(BF)
            heads_ref[m, 2 * w2 + core] = total[:, :LANES]
            heads_ref[m, 2 * w2 + 1 - core] = total[:, LANES:]
        return carry

    lax.fori_loop(0, pairs, project, 0)
    masks = lane_masks(head_dim)
    scale = head_dim**-0.5

    def attend(w, carry):
        q, k, v = heads_ref[0, w], heads_ref[1, w], heads_ref[2, w]
        mixed = jnp.zeros((length, LANES), F32)
        for i, mask in enumerate(masks):
            head = w * len(masks) + i
            raw = mm(jnp.where(mask, q, jnp.zeros_like(q)), k, NT)
            line = jnp.broadcast_to(bias_ref[pl.ds(head, 1), :], (length, 2 * length))
            bias = pltpu.roll(line, length + 1, 1, stride=1, stride_axis=0)[:, :length]
            scores = raw * scale + bias
            top = jnp.max(scores, axis=-1, keepdims=True)
            grown = jnp.exp(scores - top)
            probs = grown / jnp.sum(grown, axis=-1, keepdims=True)
            probs_ref[head] = probs
            mixed = jnp.where(mask, mm(probs.astype(BF), v), mixed)
        attended_ref[w] = mixed.astype(BF)
        return carry

    lax.fori_loop(0, 2 * pairs, attend, 0)


def attend_call(table, tokens, gain, bias_table, gathered, groups, head_dim):
    length, features = tokens.shape
    pairs = features // (2 * LANES)
    head_count = features // head_dim
    owns = [g[0] for g in gathered]
    fars = [g[1] for g in gathered]
    body = functools.partial(attend_body, groups=groups, pairs=pairs, head_dim=head_dim)
    return pl.pallas_call(
        body,
        in_specs=[smem()] + [vmem()] * 9,
        out_specs=[vmem()] * 4,
        out_shape=[
            jax.ShapeDtypeStruct((length, features), BF),
            jax.ShapeDtypeStruct((3, 2 * pairs, length, LANES), BF),
            jax.ShapeDtypeStruct((head_count, length, length), F32),
            jax.ShapeDtypeStruct((2 * pairs, length, LANES), BF),
        ],
        compiler_params=params(),
        name="attend",
    )(table, tokens, gain.reshape(1, features), bias_table, *owns, *fars)


def expert_hot(ids_ref, expert, cap, length):
    slot = lax.broadcasted_iota(jnp.int32, (cap, length), 0) + expert * cap
    return [slot == ids_ref[c : c + 1, :] for c in range(2)]


def spread_rows(values, ids_ref, slots_ref, sends, experts, cap):
    length, features = values.shape
    half = cap // 2
    for e in range(experts):
        first, second = expert_hot(ids_ref, e, cap, length)
        rows = mm(jnp.where(first | second, 1.0, 0.0).astype(BF), values)
        for chain, send in enumerate(sends):
            at = slots_ref[chain * experts + e]
            send[at, :, :features] = rows[chain * half : (chain + 1) * half].astype(BF)


def upstream_body(slots_ref, values_ref, ids_ref, others_ref, send_a, send_b, *, experts, cap):
    length, features = values_ref.shape
    half = cap // 2
    spread_rows(values_ref[...], ids_ref, slots_ref, (send_a, send_b), experts, cap)
    for e in range(experts):
        first, second = expert_hot(ids_ref, e, cap, length)
        other = jnp.where(first, others_ref[0:1, :], 0.0) + jnp.where(
            second, others_ref[1:2, :], 0.0
        )
        other = jnp.sum(other, axis=1, keepdims=True)
        other = jnp.broadcast_to(other, (cap, LANES))
        for chain, send in enumerate((send_a, send_b)):
            at = slots_ref[chain * experts + e]
            send[at, :, features:] = other[chain * half : (chain + 1) * half].astype(BF)


def upstream_call(row_table, upstream, row_ids, other_ids, experts, cap):
    features = upstream.shape[1]
    return pl.pallas_call(
        functools.partial(upstream_body, experts=experts, cap=cap),
        in_specs=[smem()] + [vmem()] * 3,
        out_specs=[vmem()] * 2,
        out_shape=[jax.ShapeDtypeStruct((experts, cap // 2, features + LANES), BF)] * 2,
        compiler_params=params(),
        name="upstream_rows",
    )(row_table, upstream, row_ids, other_ids)


def post_body(
    table_ref, slots_ref, tokens_ref, attended_ref, own, far, gain_ref, ids_ref,
    x1_ref, normed_ref, send_a, send_b,
    *, groups, experts, cap,
):
    length, features = tokens_ref.shape
    pairs = features // (2 * LANES)
    per_group = 2 * pairs // groups
    depth = features // groups
    core = table_ref[0]
    rows = [
        jnp.concatenate([attended_ref[n * per_group + i] for i in range(per_group)], axis=1)
        for n in range(groups)
    ]
    for w2 in range(pairs):
        total = None
        for n in range(groups):
            at = table_ref[1 + (3 * groups + n) * pairs + w2]
            block = jnp.concatenate([own[at, :depth], far[at, :depth]], axis=1)
            part = mm(rows[n], block)
            total = part if total is None else total + part
        for j in range(2):
            w = 2 * w2 + (core if j == 0 else 1 - core)
            place = pl.multiple_of(w * LANES, LANES)
            mine = total[:, j * LANES : (j + 1) * LANES]
            x1_ref[:, pl.ds(place, LANES)] = mine + tokens_ref[:, pl.ds(place, LANES)].astype(F32)
    x1 = x1_ref[...]
    factor = lax.rsqrt(jnp.mean(x1 * x1, axis=-1, keepdims=True) + NORM_EPS)
    normed = (x1 * factor * gain_ref[...]).astype(BF)
    normed_ref[...] = normed
    spread_rows(normed, ids_ref, slots_ref, (send_a, send_b), experts, cap)


def post_call(table, row_table, tokens, attended, out_halves, gain, row_ids, groups, experts, cap):
    length, features = tokens.shape
    return pl.pallas_call(
        functools.partial(post_body, groups=groups, experts=experts, cap=cap),
        in_specs=[smem()] * 2 + [vmem()] * 6,
        out_specs=[vmem()] * 4,
        out_shape=[
            jax.ShapeDtypeStruct((length, features), F32),
            jax.ShapeDtypeStruct((length, features), BF),
            jax.ShapeDtypeStruct((experts, cap // 2, features), BF),
            jax.ShapeDtypeStruct((experts, cap // 2, features), BF),
        ],
        compiler_params=params(),
        name="post",
    )(table, row_table, tokens, attended, *out_halves, gain.reshape(1, features), row_ids)


def mid_body(
    table_ref, slots_ref, x1_ref, gain_ref, normed_ref, upstream_ref, back_a, back_b,
    ids_ref, choice_ref, router_ref, attended_ref, own, far,
    x1_grad_ref, gates_ref, gain_out_ref, router_out_ref, keep_ref, send_ref, att_grad_ref,
    *, groups, experts, cap,
):
    length, features = x1_ref.shape
    pairs = features // (2 * LANES)
    per_group = 2 * pairs // groups
    rows = features // groups
    half = cap // 2
    core = table_ref[0]
    dmoe = jnp.zeros((length, features), F32)
    dots = [jnp.zeros((length, LANES), F32)] * 2
    for e in range(experts):
        hots = expert_hot(ids_ref, e, cap, length)
        hots = [jnp.where(hot, 1.0, 0.0).astype(BF) for hot in hots]
        both = hots[0] + hots[1]
        for chain, back in enumerate((back_a, back_b)):
            at = slots_ref[chain * experts + e]
            part = slice(chain * half, (chain + 1) * half)
            got = back[at]
            dmoe = dmoe + mm(both[part], got[:, :features], TN)
            for c in range(2):
                dots[c] = dots[c] + mm(hots[c][part], got[:, features:], TN)
    normed = normed_ref[...]
    logits = mm(normed, router_ref[...])
    lane = lax.broadcasted_iota(jnp.int32, logits.shape, 1)
    picks = [lane == choice_ref[:, c : c + 1] for c in range(2)]
    picked = [jnp.sum(jnp.where(pick, logits, 0.0), axis=1, keepdims=True) for pick in picks]
    top = jnp.maximum(picked[0], picked[1])
    grown = [jnp.exp(value - top) for value in picked]
    gates = [value / (grown[0] + grown[1]) for value in grown]
    gates_ref[...] = jnp.where(lane == 0, gates[0], jnp.where(lane == 1, gates[1], 0.0))
    dgates = [dot[:, 0:1] for dot in dots]
    inner = gates[0] * dgates[0] + gates[1] * dgates[1]
    dlogits = jnp.where(picks[0], gates[0] * (dgates[0] - inner), 0.0) + jnp.where(
        picks[1], gates[1] * (dgates[1] - inner), 0.0
    )
    dlogits = dlogits.astype(BF)
    router_out_ref[...] = mm(normed, dlogits, TN)
    dmoe = dmoe + mm(dlogits, router_ref[...], NT)
    x1 = x1_ref[...]
    factor = lax.rsqrt(jnp.mean(x1 * x1, axis=-1, keepdims=True) + NORM_EPS)
    hat = x1 * factor
    gain_out_ref[...] = jnp.sum(dmoe * hat, axis=0, keepdims=True)
    scaled = dmoe * gain_ref[...]
    inner = jnp.mean(scaled * hat, axis=-1, keepdims=True)
    x1_grad_ref[...] = upstream_ref[...].astype(F32) + factor * (scaled - hat * inner)
    branches = []
    for w2 in range(pairs):
        both = []
        for j in range(2):
            w = 2 * w2 + (core if j == 0 else 1 - core)
            both.append(x1_grad_ref[:, pl.ds(pl.multiple_of(w * LANES, LANES), LANES)].astype(BF))
        branches.append(jnp.concatenate(both, axis=1))
    for n in range(groups):
        att = jnp.concatenate(
            [attended_ref[n * per_group + i] for i in range(per_group)], axis=1
        )
        total = None
        for w2 in range(pairs):
            at = table_ref[1 + (3 * groups + n) * pairs + w2]
            block = mm(att, branches[w2], TN)
            keep_ref[at] = block[:, :LANES]
            send_ref[at] = block[:, LANES:].astype(BF)
            block = jnp.concatenate([own[at, :rows], far[at, :rows]], axis=1)
            part = mm(branches[w2], block, NT)
            total = part if total is None else total + part
        for i in range(per_group):
            att_grad_ref[n * per_group + i] = total[:, i * LANES : (i + 1) * LANES].astype(BF)


def mid_call(
    table, row_table, x1, gain, normed, upstream, backs, row_ids, choices, router, attended,
    out_halves, groups, experts, cap,
):
    length, features = x1.shape
    pairs = features // (2 * LANES)
    rows = features // groups
    return pl.pallas_call(
        functools.partial(mid_body, groups=groups, experts=experts, cap=cap),
        in_specs=[smem()] * 2 + [vmem()] * 12,
        out_specs=[vmem()] * 7,
        out_shape=[
            jax.ShapeDtypeStruct((length, features), F32),
            jax.ShapeDtypeStruct((length, LANES), F32),
            jax.ShapeDtypeStruct((1, features), F32),
            jax.ShapeDtypeStruct((features, LANES), F32),
            jax.ShapeDtypeStruct((groups * pairs, rows, LANES), F32),
            jax.ShapeDtypeStruct((groups * pairs, rows, LANES), BF),
            jax.ShapeDtypeStruct((2 * pairs, length, LANES), BF),
        ],
        compiler_params=params(),
        name="mid",
    )(
        table, row_table, x1, gain.reshape(1, features), normed, upstream, *backs,
        row_ids, choices, router, attended, *out_halves,
    )


def block_out_body(
    slots_ref, x1_ref, gates_ref, back_a, back_b, ids_ref, out_ref, *, experts, cap
):
    length, features = x1_ref.shape
    half = cap // 2
    sums = [jnp.zeros((length, features), F32)] * 2
    for e in range(experts):
        hots = [
            jnp.where(hot, 1.0, 0.0).astype(BF) for hot in expert_hot(ids_ref, e, cap, length)
        ]
        for chain, back in enumerate((back_a, back_b)):
            got = back[slots_ref[chain * experts + e]]
            part = slice(chain * half, (chain + 1) * half)
            sums = [total + mm(hot[part], got, TN) for total, hot in zip(sums, hots)]
    moe = gates_ref[:, 0:1] * sums[0] + gates_ref[:, 1:2] * sums[1]
    out_ref[...] = (x1_ref[...] + moe).astype(BF)


def block_out_call(row_table, x1, gates, backs, row_ids, experts, cap):
    return pl.pallas_call(
        functools.partial(block_out_body, experts=experts, cap=cap),
        in_specs=[smem()] + [vmem()] * 5,
        out_specs=vmem(),
        out_shape=jax.ShapeDtypeStruct(x1.shape, BF),
        compiler_params=params(),
        name="block_out",
    )(row_table, x1, gates, *backs, row_ids)


def attend_back_body(
    table_ref, normed_ref, heads_ref, probs_ref, grad_ref,
    keep_ref, send_ref, dheads_ref, diag_ref,
    *, groups, pairs, head_dim,
):
    length, features = normed_ref.shape
    rows = features // groups
    masks = lane_masks(head_dim)
    scale = head_dim**-0.5

    def back(w, carry):
        q, k, v = heads_ref[0, w], heads_ref[1, w], heads_ref[2, w]
        da = grad_ref[w]
        dq = jnp.zeros((length, LANES), F32)
        dk, dv = dq, dq
        for i, mask in enumerate(masks):
            head = w * len(masks) + i
            probs = probs_ref[head]
            dp = mm(jnp.where(mask, da, jnp.zeros_like(da)), v, NT)
            spread = jnp.sum(probs * dp, axis=-1, keepdims=True)
            ds = (probs * (dp - spread)).astype(BF)
            dq = jnp.where(mask, mm(ds, k), dq)
            dk = jnp.where(mask, mm(ds, q, TN), dk)
            dv = jnp.where(mask, mm(probs.astype(BF), da, TN), dv)
            wide_ds = jnp.concatenate([ds.astype(F32), jnp.zeros((length, length), F32)], axis=1)
            diag = jnp.zeros((8, 2 * length), F32)
            for g in range(length // 8):
                diag = diag + pltpu.roll(wide_ds[8 * g : 8 * g + 8], length - 1 - 8 * g, 1)
            diag_ref[head] = diag
        dheads_ref[0, w] = (dq * scale).astype(BF)
        dheads_ref[1, w] = (dk * scale).astype(BF)
        dheads_ref[2, w] = dv.astype(BF)
        return carry

    lax.fori_loop(0, 2 * pairs, back, 0)
    core = table_ref[0]

    def weigh(w2, carry):
        for m in range(3):
            both = jnp.concatenate(
                [dheads_ref[m, 2 * w2 + core], dheads_ref[m, 2 * w2 + 1 - core]], axis=1
            )
            for n in range(groups):
                at = table_ref[1 + (m * groups + n) * pairs + w2]
                block = mm(normed_ref[:, n * rows : (n + 1) * rows], both, TN)
                keep_ref[m, at] = block[:, :LANES]
                send_ref[m, at] = block[:, LANES:].astype(BF)
        return carry

    lax.fori_loop(0, pairs, weigh, 0)


def attend_back_call(table, normed, heads, probs, attended_grad, groups, head_dim):
    length, features = normed.shape
    pairs = features // (2 * LANES)
    head_count = features // head_dim
    rows = features // groups
    body = functools.partial(attend_back_body, groups=groups, pairs=pairs, head_dim=head_dim)
    return pl.pallas_call(
        body,
        in_specs=[smem()] + [vmem()] * 4,
        out_specs=[vmem()] * 4,
        out_shape=[
            jax.ShapeDtypeStruct((3, groups * pairs, rows, LANES), F32),
            jax.ShapeDtypeStruct((3, groups * pairs, rows, LANES), BF),
            jax.ShapeDtypeStruct((3, 2 * pairs, length, LANES), BF),
            jax.ShapeDtypeStruct((head_count, 8, 2 * length), F32),
        ],
        compiler_params=params(),
        name="attend_back",
    )(table, normed, heads, probs, attended_grad)


def tokens_back_body(
    table_ref, tokens_ref, gain_ref, x1_grad_ref, dheads_ref,
    own_q, own_k, own_v, far_q, far_k, far_v,
    out_ref, gain_out_ref, acc_ref,
    *, groups, pairs,
):
    length, features = tokens_ref.shape
    rows = features // groups
    core = table_ref[0]
    for n in range(groups):

        def step(w2, total):
            for m, (own, far) in enumerate(((own_q, far_q), (own_k, far_k), (own_v, far_v))):
                at = table_ref[1 + (m * groups + n) * pairs + w2]
                both = jnp.concatenate(
                    [dheads_ref[m, 2 * w2 + core], dheads_ref[m, 2 * w2 + 1 - core]], axis=1
                )
                total = total + mm(both, jnp.concatenate([own[at], far[at]], axis=1), NT)
            return total

        total = lax.fori_loop(0, pairs, step, jnp.zeros((length, rows), F32))
        acc_ref[:, n * rows : (n + 1) * rows] = total
    x = tokens_ref[...].astype(F32)
    factor = lax.rsqrt(jnp.mean(x * x, axis=-1, keepdims=True) + NORM_EPS)
    hat = x * factor
    grad = acc_ref[...]
    gain_out_ref[...] = jnp.sum(grad * hat, axis=0, keepdims=True)
    scaled = grad * gain_ref[...]
    inner = jnp.mean(scaled * hat, axis=-1, keepdims=True)
    out_ref[...] = (x1_grad_ref[...] + factor * (scaled - hat * inner)).astype(BF)


def tokens_back_call(table, tokens, gain, x1_grad, dheads, gathered, groups):
    length, features = tokens.shape
    pairs = features // (2 * LANES)
    owns = [g[0] for g in gathered]
    fars = [g[1] for g in gathered]
    return pl.pallas_call(
        functools.partial(tokens_back_body, groups=groups, pairs=pairs),
        in_specs=[smem()] + [vmem()] * 10,
        out_specs=[vmem()] * 2,
        out_shape=[
            jax.ShapeDtypeStruct((length, features), BF),
            jax.ShapeDtypeStruct((1, features), F32),
        ],
        scratch_shapes=[pltpu.VMEM((length, features), F32)],
        compiler_params=params(),
        name="tokens_back",
    )(table, tokens, gain.reshape(1, features), x1_grad, dheads, *owns, *fars)


def choose(refs, which):
    value = refs[0][...]
    for i in range(1, len(refs)):
        value = jnp.where(which == i, refs[i][...], value)
    return value


def expert_body(expert_ref, *refs, count):
    x_refs, up_refs, refs = refs[:count], refs[count : 2 * count], refs[2 * count :]
    router_ref, gate_w, up_w, down_w = refs[:4]
    y_refs, dx_refs = refs[-2 * count - 5 : -count - 5], refs[-count - 5 : -5]
    x_out, dy_ref, hidden_ref, dgate_ref, dup_ref = refs[-5:]
    piece = pl.program_id(0)
    x = choose(x_refs, piece)
    up = choose(up_refs, piece)
    x_out[...] = x
    features = x.shape[1]
    logits = mm(x, router_ref[...])
    lane = lax.broadcasted_iota(jnp.int32, logits.shape, 1)
    other_id = up[:, features : features + 1].astype(jnp.int32)
    mine = jnp.sum(jnp.where(lane == expert_ref[0], logits, 0.0), axis=1, keepdims=True)
    other = jnp.sum(jnp.where(lane == other_id, logits, 0.0), axis=1, keepdims=True)
    top = jnp.maximum(mine, other)
    mine_e = jnp.exp(mine - top)
    gate = mine_e / (mine_e + jnp.exp(other - top))
    grad = up[:, :features].astype(F32)
    dy = (gate * grad).astype(BF)
    dy_ref[...] = dy
    y, dx = None, None
    step = 2 * LANES
    width = gate_w.shape[0]
    for f in range(0, width, step):
        chunk = slice(f, min(f + step, width))
        gate_f, up_f, down_f = gate_w[chunk, :], up_w[chunk, :], down_w[chunk, :]
        g = mm(x, gate_f, NT)
        u = mm(x, up_f, NT)
        dh = mm(dy, down_f, NT)
        t = jnp.tanh(g * (GELU_C + (GELU_C * GELU_A) * (g * g)))
        half_t = 0.5 + 0.5 * t
        act = g * half_t
        hidden = (act * u).astype(BF)
        slope = half_t + act * (1.0 - t) * (GELU_C + (3.0 * GELU_C * GELU_A) * (g * g))
        dg = (dh * u * slope).astype(BF)
        du = (dh * act).astype(BF)
        hidden_ref[:, chunk] = hidden
        dgate_ref[:, chunk] = dg
        dup_ref[:, chunk] = du
        y_f = mm(hidden, down_f)
        dx_f = mm(dg, gate_f) + mm(du, up_f)
        y = y_f if y is None else y + y_f
        dx = dx_f if dx is None else dx + dx_f
    y = y.astype(BF)
    dot = jnp.sum(grad * y.astype(F32), axis=1, keepdims=True)
    dx = dx.astype(BF)
    dot = jnp.broadcast_to(dot, (x.shape[0], LANES)).astype(BF)
    for i in range(count):

        @pl.when(piece == i)
        def _(i=i):
            y_refs[i][...] = y
            dx_refs[i][:, :features] = dx
            dx_refs[i][:, features:] = dot


def expert_call(expert, xs, upstreams, router, gate_w, up_w, down_w, first, total, kept):
    rows, features = xs[0].shape
    width = gate_w.shape[0]
    count = len(xs)

    def whole(arr):
        return pl.BlockSpec(arr.shape, lambda i, e: (0, 0))

    def kept_spec(cols):
        return pl.BlockSpec((rows, cols), lambda i, e: (first + i, 0))

    kept_cols = (features, features, width, width, width)
    kept_in = [] if kept is None else list(kept)
    inputs = list(xs) + list(upstreams) + [router, gate_w, up_w, down_w]
    out = pl.pallas_call(
        functools.partial(expert_body, count=count),
        grid_spec=pltpu.PrefetchScalarGridSpec(
            num_scalar_prefetch=1,
            grid=(count,),
            in_specs=[whole(arr) for arr in inputs]
            + [pl.BlockSpec(memory_space=pl.ANY)] * len(kept_in),
            out_specs=[pl.BlockSpec((rows, features), lambda i, e: (0, 0))] * count
            + [pl.BlockSpec((rows, features + LANES), lambda i, e: (0, 0))] * count
            + [kept_spec(cols) for cols in kept_cols],
        ),
        out_shape=[jax.ShapeDtypeStruct((rows, features), BF)] * count
        + [jax.ShapeDtypeStruct((rows, features + LANES), BF)] * count
        + [jax.ShapeDtypeStruct((total, cols), BF) for cols in kept_cols],
        input_output_aliases={
            1 + len(inputs) + i: 2 * count + i for i in range(len(kept_in))
        },
        compiler_params=params(),
        name="expert",
    )(expert, *inputs, *kept_in)
    return out[:count], out[count : 2 * count], out[2 * count :]


def expert_grad_body(left_ref, right_ref, out_ref):
    out_ref[...] = mm(left_ref[...], right_ref[...], TN)


def expert_grad_call(left, right):
    rows, features = right.shape
    width = left.shape[1]
    size = 2 * LANES
    return pl.pallas_call(
        expert_grad_body,
        grid=(features // size,),
        in_specs=[
            pl.BlockSpec((rows, width), lambda i: (0, 0)),
            pl.BlockSpec((rows, size), lambda i: (0, i)),
        ],
        out_specs=pl.BlockSpec((width, size), lambda i: (0, i)),
        out_shape=jax.ShapeDtypeStruct((width, features), F32),
        compiler_params=params(),
        name="expert_grad",
    )(left, right)


def finish_body(table_ref, place_ref, *refs, groups, pairs, count, first, update, subtract):
    owns, fars, refs = refs[:count], refs[count : 2 * count], refs[2 * count :]
    if update:
        mine_ref, weight_ref, refs = refs[0], refs[1], refs[2:]
    grads_ref, rows_ref, cols_ref = refs[:3]
    new_ref = refs[3] if update else None
    acc_ref, line_ref = refs[-2:]
    core = table_ref[0]
    rows = owns[0].shape[1]
    features = acc_ref.shape[0]
    for m in range(count):
        acc_ref[...] = jnp.zeros_like(acc_ref)

        def column(w2, carry, m=m):
            for j, source in enumerate((owns[m], fars[m])):
                w = 2 * w2 + (core if j == 0 else 1 - core)
                place = pl.multiple_of(w * LANES, LANES)
                total = jnp.zeros((1, LANES), F32)
                for n in range(groups):
                    at = table_ref[1 + ((first + m) * groups + n) * pairs + w2]
                    block = source[at].astype(F32)
                    grads_ref[m, n * rows : (n + 1) * rows, pl.ds(place, LANES)] = block
                    square = block * block
                    total = total + jnp.sum(square, axis=0, keepdims=True)
                    acc_ref[n * rows : (n + 1) * rows, :] += square
                cols_ref[m, w] = total / features + STAT_EPS
            return carry

        lax.fori_loop(0, pairs, column, 0)
        squares = acc_ref[...]
        sums = lax.dot_general(
            jnp.ones((8, LANES), F32), squares, NT,
            precision=lax.Precision.HIGHEST, preferred_element_type=F32,
        )
        rows_ref[m] = sums / features + STAT_EPS
        if update:
            line = jnp.sum(squares, axis=1, keepdims=True) / features + STAT_EPS
            line_ref[...] = jnp.broadcast_to(line, line_ref.shape)
            mean = jnp.sum(line, axis=0, keepdims=True) / features
            my_rows = line_ref[pl.ds(pl.multiple_of(place_ref[0] * rows, rows), rows), :]
            my_cols = cols_ref[m, place_ref[1]]
            step = STEP_RATE * mine_ref[m] / jnp.sqrt(my_rows * my_cols / mean)
            new_ref[m] = weight_ref[m] - step if subtract else step


def finish_call(table, place, gathered, first, groups, features, mine, weights, subtract):
    pairs = features // (2 * LANES)
    count = len(gathered)
    rows = features // groups
    owns = [g[0] for g in gathered]
    fars = [g[1] for g in gathered]
    update = mine is not None
    extra = [mine, weights] if update else []
    shapes = [
        jax.ShapeDtypeStruct((count, features, features), F32),
        jax.ShapeDtypeStruct((count, 8, features), F32),
        jax.ShapeDtypeStruct((count, 2 * pairs, 1, LANES), F32),
    ]
    if update:
        shapes.append(jax.ShapeDtypeStruct((count, rows, LANES), F32))
    out = pl.pallas_call(
        functools.partial(
            finish_body, groups=groups, pairs=pairs, count=count, first=first,
            update=update, subtract=subtract,
        ),
        in_specs=[smem()] * 2 + [vmem()] * (2 * count + len(extra)),
        out_specs=[vmem()] * len(shapes),
        out_shape=shapes,
        scratch_shapes=[pltpu.VMEM((features, LANES), F32)] * 2,
        compiler_params=params(),
        name="finish",
    )(table, place, *owns, *fars, *extra)
    stats = (out[0], out[1][:, 0], out[2].reshape(count, features))
    return stats + (out[3] if update else None,)


def on_device(
    tokens,
    attn_gain,
    qkv_weights,
    out_weight,
    rel_bias,
    moe_gain,
    router,
    gate_weight,
    up_weight,
    down_weight,
    expert_ids,
    expert_slots,
    buckets,
    upstream,
):
    length, features = tokens.shape
    bucket_count, head_count = rel_bias.shape
    head_dim = features // head_count
    groups = lax.axis_size("narrow")
    wide_count = lax.axis_size("wide")
    my_narrow = lax.axis_index("narrow")
    my_wide = lax.axis_index("wide")
    my_core = my_wide % 2
    part_width = gate_weight.shape[3]
    experts = router.shape[1] * wide_count
    places = experts // groups
    split_parts = wide_count // places
    capacity = (10 * length // experts + 3) // 4
    half_cap = capacity // 2
    row_count, col_count = qkv_weights.shape[1:]
    half_wide = wide_count // 2
    core_hop = ("wide", 0)
    part_hop = ("wide", 1)
    orders = hop_orders(groups, wide_count)
    slots = [block_slots(order, groups, wide_count) for order in orders]
    direct = col_count == LANES
    pairs = features // (2 * LANES)
    if direct:
        core_entry, tables = my_core, slots
    else:
        core_entry = jnp.int32(0)
        tables = [jnp.arange(groups * pairs, dtype=jnp.int32)] * 4
    table = jnp.concatenate(
        [jnp.reshape(core_entry, (1,)).astype(jnp.int32)] + [t.reshape(-1) for t in tables]
    )
    place = jnp.stack([my_narrow, my_wide]).astype(jnp.int32)

    def as_pairs(matrix):
        blocks = from_matrix(matrix, groups, pairs)
        return blocks.reshape((groups * pairs,) + blocks.shape[2:])

    def as_halves(owns, fars, first):
        if direct:
            return list(zip(owns, fars))
        out = []
        for i, halves in enumerate(zip(owns, fars)):
            both = as_pairs(as_matrix(*halves, slots[first + i], my_core))
            out.append((both[:, 0], both[:, 1]))
        return out

    def halves_of(keep, send, which):
        if direct:
            return keep, send
        both = jnp.stack([keep, send.astype(F32)], axis=1).reshape(
            groups, pairs, 2, features // groups, LANES
        )
        matrix = jnp.transpose(both, (0, 3, 1, 2, 4)).reshape(features, features)
        parts = from_matrix(matrix, groups, half_wide)
        placed = jnp.zeros((groups * half_wide,) + parts.shape[2:], F32)
        placed = placed.at[slots[which].reshape(-1)].set(parts.reshape(placed.shape))
        mine = jnp.where(my_core == 0, placed[:, 0], placed[:, 1])
        theirs = jnp.where(my_core == 0, placed[:, 1], placed[:, 0])
        return mine, theirs.astype(BF)

    narrow_hops = [("narrow", b) for b in range(groups.bit_length() - 1)]
    place_hops = [
        ("wide", b) for b in range(split_parts.bit_length() - 1, wide_count.bit_length() - 1)
    ][::-1]
    chains = (
        narrow_hops[:1] + place_hops + narrow_hops[1:],
        place_hops + narrow_hops[1:] + narrow_hops[:1],
    )
    hop_count = len(chains[0])
    row_table = jnp.concatenate(
        [row_slots(hops, groups, places, split_parts) for hops in chains]
    )
    owner_slot = expert_ids % groups * places + expert_ids // groups
    row_ids = jnp.where(expert_slots >= 0, owner_slot * capacity + expert_slots, -1).T

    def flat(rows):
        return rows.reshape(-1, rows.shape[-1])

    def sends(states, step):
        return [send_step(state, hops[step]) for state, hops in zip(states, chains)]

    def to_core(values):
        return [from_partner(value, core_hop) for value in values]

    def to_part(values):
        return [from_partner(value, part_hop) for value in values]

    def add(a, b):
        return a.astype(F32) + b.astype(F32)

    def homeward(rows):
        return rows.astype(BF).reshape(-1, 1, half_cap, rows.shape[-1])

    def back_step(state, chain, step):
        return return_step(state, chains[chain][hop_count - 1 - step])

    def slots_first(state):
        return state.reshape((-1,) + state.shape[2:])

    router_tail = router.astype(BF).reshape(-1, col_count)
    tail_rows = router_tail.shape[0]
    out_low = jnp.concatenate(
        [
            out_weight.astype(BF),
            router_tail,
            jnp.zeros((-tail_rows % 16, col_count), BF),
        ],
        axis=0,
    )
    qkv_low = qkv_weights.astype(BF)
    upstream_a, upstream_b = upstream_call(
        row_table, upstream, row_ids, expert_ids.T[::-1].astype(F32), experts, capacity
    )
    qkv_chains = gather_chains(qkv_low, orders[:3])
    qkv_far = to_core(qkv_chains)
    out_chain = gather_chains(out_low[None], orders[3:])
    out_gathered = (out_chain[0], from_partner(out_chain[0], core_hop))
    qkv_parts = as_halves(qkv_chains, qkv_far, 0)
    tails = [half[:, row_count : row_count + tail_rows] for half in out_gathered]
    full_router = jnp.transpose(
        as_matrix(*tails, slots[3], my_core)
        .reshape(groups, tail_rows, wide_count, col_count)
        .transpose(0, 2, 1, 3)
        .reshape(groups, wide_count, row_count, router.shape[1]),
        (0, 2, 1, 3),
    ).reshape(features, experts)
    router_wide = jnp.pad(full_router, ((0, 0), (0, -experts % LANES)))
    out_halves = out_gathered
    if not direct:
        out_halves = [half[:, :row_count] for half in out_gathered]
        both = as_pairs(as_matrix(*out_halves, slots[3], my_core))
        out_halves = [both[:, 0], both[:, 1]]
    gate_low = gate_weight[0, 0].T.astype(BF)
    up_low = up_weight[0, 0].T.astype(BF)
    down_low = down_weight[0, 0].astype(BF)
    table_hot = (
        jnp.pad(buckets, (0, 1), constant_values=-1)[:, None]
        == jnp.arange(bucket_count, dtype=jnp.int32)[None, :]
    ).astype(F32)
    bias_table = jnp.dot(table_hot, rel_bias, precision=lax.Precision.HIGHEST).T
    (upstream_a, upstream_b), qkv_chains = together((upstream_a, upstream_b), qkv_chains)
    u_state = sends([upstream_a[None], upstream_b[None]], 0)
    normed_in, heads, probs, attended = attend_call(
        table, tokens, attn_gain, bias_table, qkv_parts, groups, head_dim
    )
    u_state, attended = together(u_state, attended)
    u_state = sends(u_state, 1)
    hidden_x1, moe_input, send_a, send_b = post_call(
        table, row_table, tokens, attended, out_halves, moe_gain, row_ids, groups, experts,
        capacity,
    )
    u_state, send_a, send_b = together(u_state, send_a, send_b)
    x_state = [send_a[None], send_b[None]]
    for step in range(hop_count):
        x_state = sends(x_state, step)
        if step + 2 < hop_count:
            u_state = sends(u_state, step + 2)
        elif step + 2 == hop_count:
            u_own = [flat(state) for state in u_state]
            u_core, u_part = to_core(u_own), to_part(u_own)
            x_state, u_core = together(x_state, u_core)
            continue
        if step + 1 < hop_count:
            x_state, u_state = together(x_state, u_state)
    x_state, u_part = together(x_state, u_part)
    x_own = [flat(state) for state in x_state]
    x_core, x_part = to_core(x_own), to_part(x_own)
    u_part_core = to_core(u_part)

    my_expert = (my_narrow + groups * (my_wide // split_parts)).reshape(1).astype(jnp.int32)
    row_total = 8 * x_own[0].shape[0]

    def run_expert(xs, us, first, kept):
        return expert_call(
            my_expert, xs, us, router_wide, gate_low, up_low, down_low, first, row_total, kept
        )

    y_near, dx_near, kept = run_expert(x_own + x_core, u_own + u_core, 0, None)
    x_part, u_part_core, dx_near = together(x_part, u_part_core, dx_near)
    x_part_core = to_core(x_part)
    dx_near_got = to_core(dx_near[2:])
    y_far, parts_back, far_sums = [], [], []
    for chain in range(2):
        xs = [x_part[chain], x_part_core[chain]]
        us = [u_part[chain], u_part_core[chain]]
        if chain:
            xs, far_sums = together(xs, far_sums)
        y_two, dx_two, kept = run_expert(xs, us, 4 + 2 * chain, kept)
        y_far.append(y_two)
        far_sums.append(add(dx_two[0], from_partner(dx_two[1], core_hop)).astype(BF))
        parts_back.append(from_partner(far_sums[chain], part_hop))
    near_sums = [add(mine, got) for mine, got in zip(dx_near[:2], dx_near_got)]
    near_sums, far_sums[1], kept = together(near_sums, far_sums[1], kept)
    y_near_got = to_core(y_near[2:])
    y_far_got = to_core([two[1] for two in y_far])

    x_all, dy_all, hidden_all, dgate_all, dup_all = kept
    backs = [homeward(add(near_sums[0], parts_back[0])), None]
    for step in range(hop_count + 1):
        if step < hop_count:
            backs[0] = back_step(backs[0], 0, step)
        if step == 1:
            backs[1] = homeward(add(near_sums[1], parts_back[1]))
        if step >= 1:
            backs[1] = back_step(backs[1], 1, step - 1)
        if step == 0:
            gate_local = expert_grad_call(dgate_all, x_all)
            up_local = expert_grad_call(dup_all, x_all)
            backs[0], parts_back[1], gate_local, up_local, hidden_all = together(
                backs[0], parts_back[1], gate_local, up_local, hidden_all
            )
        elif step == 1:
            down_local = expert_grad_call(hidden_all, dy_all)
            y_sums = [add(mine, got) for mine, got in zip(y_near[:2], y_near_got)]
            y_far_sums = [
                add(two[0], got).astype(BF) for two, got in zip(y_far, y_far_got)
            ]
            y_sums = [value.astype(BF) for value in y_sums]
            backs, down_local, y_sums, y_far_sums = together(
                backs, down_local, y_sums, y_far_sums
            )
        elif step == 2:
            y_part_got = to_part(y_far_sums)
            squares = [g * g for g in (gate_local, up_local, down_local)]
            local_sums = jnp.stack([jnp.sum(q, axis=0) for q in squares], axis=0)
            part_stats = jnp.stack([jnp.mean(q, axis=1) for q in squares], axis=0) + STAT_EPS
            wide_sums = cube_sum(local_sums, [core_hop])
            backs, wide_sums = together(backs, wide_sums)
        elif step == 3:
            wide_sums = cube_sum(wide_sums, [part_hop])
            wide_stats = wide_sums / (part_width * split_parts) + STAT_EPS
            gate_new = factored(
                gate_weight[0, 0].T, gate_local, part_stats[0], wide_stats[0],
                jnp.mean(wide_stats[0]),
            )
            up_new = factored(
                up_weight[0, 0].T, up_local, part_stats[1], wide_stats[1],
                jnp.mean(wide_stats[1]),
            )
            down_new = factored(
                down_weight[0, 0], down_local, part_stats[2], wide_stats[2],
                jnp.mean(wide_stats[2]),
            )
            backs, gate_new, up_new, down_new = together(backs, gate_new, up_new, down_new)
    inputs_back = [slots_first(state) for state in backs]

    x1_grad, gates, moe_gain_local, router_local, out_keep, out_send, attended_grad = mid_call(
        table, row_table, hidden_x1, moe_gain, moe_input, upstream, inputs_back, row_ids,
        expert_ids, router_wide, attended, out_halves, groups, experts, capacity,
    )
    y_part_got, attended_grad, out_send = together(y_part_got, attended_grad, out_send)
    y_backs = [homeward(add(near, got)) for near, got in zip(y_sums, y_part_got)]
    y_backs = [back_step(state, chain, 0) for chain, state in enumerate(y_backs)]
    out_keep, out_send = halves_of(out_keep, out_send, 3)
    out_half = core_sum(out_keep, out_send, orders[3])

    keeps, qkv_sends, dheads, diag = attend_back_call(
        table, normed_in, heads, probs, attended_grad, groups, head_dim
    )
    y_backs, out_half, qkv_sends = together(y_backs, out_half, qkv_sends)
    if direct:
        summed = core_sum(keeps, qkv_sends, orders[0])
        summed = [summed[m] for m in range(3)]
    else:
        summed = [
            core_sum(*halves_of(keeps[m], qkv_sends[m], m), orders[m]) for m in range(3)
        ]
    summed = summed + [out_half]
    y_backs = [back_step(state, chain, 1) for chain, state in enumerate(y_backs)]
    summed, y_backs = together(summed, y_backs)

    shared = shared_hops(orders)
    stages = range(shared, len(orders[0]) - 1)
    y_step = 2
    for count, stage in enumerate(stages[::-1]):
        summed = [halve(total, order[stage]) for total, order in zip(summed, orders)]
        if y_step < hop_count:
            y_backs = [back_step(state, c, y_step) for c, state in enumerate(y_backs)]
            y_step += 1
        if count == 0:
            tokens_grad, attn_gain_local = tokens_back_call(
                table, tokens, attn_gain, x1_grad, dheads, qkv_parts, groups
            )
            tail = jnp.pad(diag, ((0, 0), (0, 0), (0, 8)))
            line = sum(tail[:, i, i : i + 2 * length] for i in range(8))
            bias_local = jnp.dot(line, table_hot, precision=lax.Precision.HIGHEST).T
            small = jnp.concatenate(
                [
                    attn_gain_local.reshape(-1),
                    moe_gain_local.reshape(-1),
                    bias_local.reshape(-1),
                    router_local[:, :experts].reshape(-1),
                ]
            ).reshape(-1, LANES)
        summed, y_backs, small = together(summed, y_backs, small)
    while y_step < hop_count:
        y_backs = [back_step(state, c, y_step) for c, state in enumerate(y_backs)]
        y_step += 1
    block_out = block_out_call(
        row_table, hidden_x1, gates, [slots_first(state) for state in y_backs], row_ids,
        experts, capacity,
    )
    small_hops = list(orders[0])

    def small_step(value):
        return cube_sum(value, [small_hops.pop(0)]) if small_hops else value

    total = jnp.stack(summed)
    for hop in orders[0][:shared][::-1]:
        total = halve(total, hop, 1)
        small = small_step(small)
        total, small, block_out = together(total, small, block_out)
    dense_mine = total[:, 0]
    blocks = total.astype(BF)
    for hop in orders[0][:shared]:
        blocks = grow(blocks, hop, 1)
        small = small_step(small)
        blocks, small = together(blocks, small)
    dense = [blocks[i] for i in range(4)]
    for stage in stages:
        dense = [grow(chain, order[stage]) for chain, order in zip(dense, orders)]
        small = small_step(small)
        dense, small = together(dense, small)
    small = cube_sum(small, small_hops).reshape(-1)
    dense_parts = as_halves(dense, to_core(dense), 0)
    gain_a_total = small[:features]
    gain_m_total = small[features : 2 * features]
    bias_size = bucket_count * head_count
    bias_total = small[2 * features : 2 * features + bias_size].reshape(bucket_count, head_count)
    router_total = small[2 * features + bias_size :].reshape(features, experts)

    def finish(parts, first, mine, weights, subtract):
        mine_in = mine if direct else None
        grads, rows, cols, new = finish_call(
            table, place, parts, first, groups, features, mine_in, weights, subtract
        )
        if not direct:
            rows_mine = lax.dynamic_slice_in_dim(rows, my_narrow * row_count, row_count, 1)
            cols_mine = lax.dynamic_slice_in_dim(cols, my_wide * col_count, col_count, 1)
            step = adafactor_step(mine, rows_mine, cols_mine, jnp.mean(rows, axis=1))
            new = weights - step if subtract else step
        return grads, rows, cols, new

    out_total, out_rows, out_cols, out_step = finish(
        dense_parts[3:], 3, dense_mine[3:], out_weight[None], False
    )
    qkv_total, qkv_rows, qkv_cols, qkv_new = finish(
        dense_parts[:3], 0, dense_mine[:3], qkv_weights, True
    )
    qkv_stats = jnp.stack([qkv_rows, qkv_cols], axis=0)
    out_stats = jnp.concatenate([out_rows, out_cols], axis=0)
    router_sq = router_total * router_total
    router_rows = jnp.mean(router_sq, axis=1) + STAT_EPS
    router_cols = jnp.mean(router_sq, axis=0) + STAT_EPS
    router_row_count, router_col_count = router.shape
    router_row_first = my_narrow * router_row_count
    router_col_first = my_wide * router_col_count
    router_block = lax.dynamic_slice(
        router_total, (router_row_first, router_col_first), (router_row_count, router_col_count)
    )
    router_new = factored(
        router,
        router_block,
        lax.dynamic_slice_in_dim(router_rows, router_row_first, router_row_count, 0),
        lax.dynamic_slice_in_dim(router_cols, router_col_first, router_col_count, 0),
        jnp.mean(router_rows),
    )
    return (
        block_out,
        tokens_grad,
        gain_a_total,
        qkv_total,
        out_total[0],
        bias_total,
        gain_m_total,
        router_total,
        gate_local.T[None, None],
        up_local.T[None, None],
        down_local[None, None],
        qkv_new,
        out_step[0],
        router_new,
        gate_new.T[None, None],
        up_new.T[None, None],
        down_new[None, None],
        qkv_stats,
        out_stats,
        router_rows,
        router_cols,
        wide_stats[None, None],
        part_stats[None, None],
    )


def solution(mesh):
    in_specs = (
        P(("narrow", "wide"), None),
        P(),
        P(None, "narrow", "wide"),
        P("narrow", "wide"),
        P(),
        P(),
        P("narrow", "wide"),
        P("narrow", "wide", None, None),
        P("narrow", "wide", None, None),
        P("narrow", "wide", None, None),
        P(("narrow", "wide"), None),
        P(("narrow", "wide"), None),
        P(),
        P(("narrow", "wide"), None),
    )
    out_specs = (
        P(("narrow", "wide"), None),
        P(("narrow", "wide"), None),
        P(),
        P(),
        P(),
        P(),
        P(),
        P(),
        P("narrow", "wide", None, None),
        P("narrow", "wide", None, None),
        P("narrow", "wide", None, None),
        P(None, "narrow", "wide"),
        P("narrow", "wide"),
        P("narrow", "wide"),
        P("narrow", "wide", None, None),
        P("narrow", "wide", None, None),
        P("narrow", "wide", None, None),
        P(),
        P(),
        P(),
        P(),
        P("narrow", "wide", None, None),
        P("narrow", "wide", None, None),
    )
    return jax.shard_map(
        on_device, mesh=mesh, in_specs=in_specs, out_specs=out_specs, check_vma=False
    )
```

time: 674 us -> 604 us (0.90)
  Pallas kernels: 120 us -> 165 us
  local copies, waits for them, and re-layouts: 86.3 us -> 41.3 us
  waiting for transfers between devices: 268 us -> 230 us
  other arithmetic: 87.6 us -> 63.5 us
  matrix products: 13.5 us -> 1.3 us
    all_to_all x4 -> x0, waiting for transfers between devices: 116 us -> none  [the longest x2 61.1 us: dispatch(): lax.all_to_all(copies, ('narrow', 'wide'), split_axis=0, concat_axis=0, t...]
    ppermute x71 -> x105, waiting for transfers between devices: 152 us -> 230 us  [from_partner(): return lax.ppermute(value, axis, pairs)]
    pallas_call x4 -> x12, Pallas kernels: 77.1 us -> 122 us  [the longest x3 52.3 us: expert_call(): pl.pallas_call(functools.partial(expert_body, count=count), grid_spec=plt...]
    unnamed x166 -> x148, local copies, waits for them, and re-layouts: 33.7 us -> 13.3 us
    ppermute x71 -> x105, starting transfers between devices: 68.4 us -> 87.3 us  [from_partner(): return lax.ppermute(value, axis, pairs)]
    all_to_all x4 -> x0, starting transfers between devices: 17.8 us -> none  [the longest x2 10.3 us: dispatch(): lax.all_to_all(copies, ('narrow', 'wide'), split_axis=0, concat_axis=0, t...]
    dot_general x16 -> x0, matrix products: 12.2 us -> none  [mm(): return lax.dot_general(a, b, dims, preferred_element_type=F32)]
    broadcast_in_dim x4 -> x1, other arithmetic: 9.98 us -> 1.03 us  [gather_chains(): blocks = blocks[:, None]]
  transfers between devices with their start and end apart: 75 -> 105, of which waited for: 35 -> 49; matrix products, arithmetic and copies ran while one was open for 21% -> 13% of each run, Pallas kernels for 9% -> 26%
where the time goes in v2:
time: 604 us; the launch traced here: 594 us
  waiting for transfers between devices  230 us (38%)
  Pallas kernels  165 us (27%)
  starting transfers between devices  87.3 us (14%)
  other arithmetic  63.5 us (11%)
  local copies, waits for them, and re-layouts  41.3 us (7%)
    ppermute x105, waiting for transfers between devices, from_partner(): return lax.ppermute(value, axis, pairs)  230 us
    ppermute x105, starting transfers between devices, from_partner(): return lax.ppermute(value, axis, pairs)  87.3 us
    pallas_call x3, Pallas kernels, expert_call(): pl.pallas_call(functools.partial(expert_body, count=count), grid_spec=plt...  52.3 us
    pallas_call x3, Pallas kernels, expert_grad_call(): pl.pallas_call(expert_grad_body, grid=(features // size,), in_specs=[pl.B...  27.2 us
    pallas_call x1, Pallas kernels, attend_back_call(): pl.pallas_call(body, in_specs=[smem()] + [vmem()] * 4, out_specs=[vmem()]...  17.2 us
    pallas_call x2, Pallas kernels, finish_call(): pl.pallas_call(functools.partial(finish_body, groups=groups, pairs=pairs,...  16.8 us
    pallas_call x1, Pallas kernels, attend_call(): pl.pallas_call(body, in_specs=[smem()] + [vmem()] * 9, out_specs=[vmem()]...  15.9 us
    unnamed x148, local copies, waits for them, and re-layouts  13.3 us
  transfers between devices with their start and end apart: 105, of which 49 were waited for; matrix products, arithmetic and copies ran while one was open for 13% of the time, Pallas kernels for 26%

profile of v2, /device:TPU:0, one launch (start us, length us, event | category | flops | bytes accessed | tf_op | source)
XLA Modules:
  0.0 593.9 jit_solution(18142270609881046763)
XLA Ops:
  44.8 5.3 collective-permute-done.6
  59.2 11.2 %collective-permute-done.14 = bf16[1,4,40,1152]{3,2,1,0:T(8,128)(2,1)S(1)} collective-permute-done((bf16[1,4,40,1152]{3,2,1,0:T(8,128)(2,1)S(1)}, bf16[1,4,40,1152]{3,2,1,0:T(8,128)(2,1)S(1)}, u32[]{:S(2)}, u32[]{:S(2)}) %collective-permute-start.14) | collective-permute-done | bytes 368672 | tf_op jit(solution)/shard_map/ppermute | solution.py:32
  74.3 15.9 %attend.1 = (bf16[256,1024]{1,0:T(8,128)(2,1)}, bf16[3,8,256,128]{3,2,1,0:T(8,128)(2,1)}, f32[16,256,256]{2,1,0:T(8,128)}, bf16[8,256,128]{2,1,0:T(8,128)(2,1)}) custom-call(s32[65]{0:T(128)} %concatenate.148.table_ref, bf16[256,1024]{1,0:T(8,128)(2,1)} %tokens_ref.5, f32[1,1024]{1,0:T(1,128)} %bitcast.318, f32[16,512]{1,0:T(8,128)} %convolution_bitcast_fusion.bias_ref, ...), custom_call_target="tpu_custom_call" | custom-call | tf_op jit(solution)/shard_map/attend/pallas_call | solution.py:237
  93.6 4.9 post.1
  103.8 8.8 %collective-permute-done.15 = bf16[2,2,40,1152]{3,2,0,1:T(8,128)(2,1)} collective-permute-done((bf16[2,2,40,1152]{3,2,0,1:T(8,128)(2,1)}, bf16[2,2,40,1152]{3,2,0,1:T(8,128)(2,1)}, u32[]{:S(2)}, u32[]{:S(2)}) %collective-permute-start.15) | collective-permute-done | bytes 368672 | tf_op jit(solution)/shard_map/ppermute | solution.py:32
  117.9 12.3 %collective-permute-done.23 = bf16[1,4,40,1024]{3,2,1,0:T(8,128)(2,1)S(1)} collective-permute-done((bf16[1,4,40,1024]{3,2,1,0:T(8,128)(2,1)S(1)}, bf16[1,4,40,1024]{3,2,1,0:T(8,128)(2,1)S(1)}, u32[]{:S(2)}, u32[]{:S(2)}) %collective-permute-start.23) | collective-permute-done | bytes 327712 | tf_op jit(solution)/shard_map/ppermute | solution.py:32
  140.5 10.1 %collective-permute-done.26 = bf16[2,2,40,1024]{3,2,0,1:T(8,128)(2,1)S(1)} collective-permute-done((bf16[2,2,40,1024]{3,2,0,1:T(8,128)(2,1)S(1)}, bf16[2,2,40,1024]{3,2,0,1:T(8,128)(2,1)S(1)}, u32[]{:S(2)}, u32[]{:S(2)}) %collective-permute-start.26) | collective-permute-done | bytes 327712 | tf_op jit(solution)/shard_map/ppermute | solution.py:32
  153.0 7.4 %collective-permute-done.31 = bf16[4,1,40,1024]{3,2,0,1:T(8,128)(2,1)S(1)} collective-permute-done((bf16[4,1,40,1024]{3,2,0,1:T(8,128)(2,1)S(1)}, bf16[4,1,40,1024]{3,2,0,1:T(8,128)(2,1)S(1)}, u32[]{:S(2)}, u32[]{:S(2)}) %collective-permute-start.31) | collective-permute-done | bytes 327712 | tf_op jit(solution)/shard_map/ppermute | solution.py:32
  161.7 14.9 %collective-permute-done.33.refs_2_ = bf16[320,1152]{1,0:T(8,128)(2,1)} collective-permute-done((bf16[320,1152]{1,0:T(8,128)(2,1)S(1)}, bf16[320,1152]{1,0:T(8,128)(2,1)}, u32[]{:S(2)}, u32[]{:S(2)}) %collective-permute-start.33) | collective-permute-done | bytes 737312 | tf_op jit(solution)/shard_map/ppermute | solution.py:32
  184.8 24.3 %expert.3 = (bf16[320,1024]{1,0:T(8,128)(2,1)}, bf16[320,1024]{1,0:T(8,128)(2,1)}, bf16[320,1024]{1,0:T(8,128)(2,1)}, bf16[320,1024]{1,0:T(8,128)(2,1)}, bf16[32...) custom-call(s32[1]{0:T(128)} %bitcast.52.expert_ref, ...), custom_call_target="tpu_custom_call" | custom-call | tf_op jit(solution)/shard_map/expert/pallas_call | solution.py:678
  213.9 13.8 %expert.4 = (bf16[320,1024]{1,0:T(8,128)(2,1)}, bf16[320,1024]{1,0:T(8,128)(2,1)}, bf16[320,1152]{1,0:T(8,128)(2,1)}, bf16[320,1152]{1,0:T(8,128)(2,1)}, bf16[25...) custom-call(s32[1]{0:T(128)} %bitcast.52.expert_ref, ...), custom_call_target="tpu_custom_call", output_to_operand_aliasing={{4}: (9, {}), {5}: (10, {}), {6}: (11, {}), {7}: (12, {}), ... | custom-call | tf_op jit(solution)/shard_map/expert/pallas_call | solution.py:678
  235.5 14.2 %expert.5 = (bf16[320,1024]{1,0:T(8,128)(2,1)}, bf16[320,1024]{1,0:T(8,128)(2,1)}, bf16[320,1152]{1,0:T(8,128)(2,1)}, bf16[320,1152]{1,0:T(8,128)(2,1)}, bf16[25...) custom-call(s32[1]{0:T(128)} %bitcast.52.expert_ref, ...), custom_call_target="tpu_custom_call", output_to_operand_aliasing={{4}: (9, {}), {5}: (10, {}), {6}: (11, {}), {7}: (12, {}), ... | custom-call | tf_op jit(solution)/shard_map/expert/pallas_call | solution.py:678
  254.3 16.8 %collective-permute-done.46 = bf16[320,1152]{1,0:T(8,128)(2,1)S(1)} collective-permute-done((bf16[320,1152]{1,0:T(8,128)(2,1)S(1)}, bf16[320,1152]{1,0:T(8,128)(2,1)S(1)}, u32[]{:S(2)}, u32[]{:S(2)}) %collective-permute-start.46) | collective-permute-done | bytes 737312 | tf_op jit(solution)/shard_map/ppermute | solution.py:32
  275.7 9.0 %expert_grad.4 = f32[704,1024]{1,0:T(8,128)} custom-call(bf16[2560,704]{1,0:T(8,128)(2,1)} %get-tuple-element.263.left_ref, bf16[2560,1024]{1,0:T(8,128)(2,1)} %get-tuple-element.262.right_ref), custom_call_target="tpu_custom_call" | custom-call | tf_op jit(solution)/shard_map/expert_grad/pallas_call | solution.py:709
  284.7 9.0 %expert_grad.3 = f32[704,1024]{1,0:T(8,128)} custom-call(bf16[2560,704]{1,0:T(8,128)(2,1)} %get-tuple-element.261.left_ref, bf16[2560,1024]{1,0:T(8,128)(2,1)} %get-tuple-element.262.right_ref), custom_call_target="tpu_custom_call" | custom-call | tf_op jit(solution)/shard_map/expert_grad/pallas_call | solution.py:709
  300.1 9.2 %expert_grad.5 = f32[704,1024]{1,0:T(8,128)} custom-call(bf16[2560,704]{1,0:T(8,128)(2,1)} %get-tuple-element.268.left_ref, bf16[2560,1024]{1,0:T(8,128)(2,1)} %get-tuple-element.269.right_ref), custom_call_target="tpu_custom_call" | custom-call | tf_op jit(solution)/shard_map/expert_grad/pallas_call | solution.py:709
  309.3 6.2 %collective-permute-done.49 = bf16[2,2,40,1152]{3,2,0,1:T(8,128)(2,1)} collective-permute-done((bf16[2,2,40,1152]{3,2,0,1:T(8,128)(2,1)}, bf16[2,2,40,1152]{3,2,0,1:T(8,128)(2,1)}, u32[]{:S(2)}, u32[]{:S(2)}) %collective-permute-start.49) | collective-permute-done | bytes 368672 | tf_op jit(solution)/shard_map/ppermute | solution.py:32
  323.8 6.2 %collective-permute-done.58 = bf16[2,2,40,1152]{3,2,0,1:T(8,128)(2,1)S(1)} collective-permute-done((bf16[2,2,40,1152]{3,2,0,1:T(8,128)(2,1)S(1)}, bf16[2,2,40,1152]{3,2,0,1:T(8,128)(2,1)S(1)}, u32[]{:S(2)}, u32[]{:S(2)}) %collective-permute-start.58) | collective-permute-done | bytes 368672 | tf_op jit(solution)/shard_map/ppermute | solution.py:32
  336.0 24.8 %collective-permute-done.61 = f32[3,1024]{1,0:T(4,128)S(1)} collective-permute-done((f32[3,1024]{1,0:T(4,128)S(1)}, f32[3,1024]{1,0:T(4,128)S(1)}, u32[]{:S(2)}, u32[]{:S(2)}) %collective-permute-start.61) | collective-permute-done | bytes 12320 | tf_op jit(solution)/shard_map/ppermute | solution.py:32
  364.6 5.0 bitcast_subtract_fusion.2
  377.6 10.6 %mid.1 = (f32[256,1024]{1,0:T(8,128)}, f32[256,128]{1,0:T(8,128)}, f32[1,1024]{1,0:T(1,128)}, f32[1024,128]{1,0:T(8,128)}, f32[16,256,128]{2,1,0:T(8,128)}, /*in...) custom-call(s32[65]{0:T(128)} %concatenate.148.table_ref, s32[16]{0:T(128)} %pad_add_fusion.slots_ref, ...), custom_call_target="tpu_custom_call" | custom-call | tf_op jit(solution)/shard_map/mid/pallas_call | solution.py:426
  393.2 17.2 %attend_back.1 = (f32[3,16,256,128]{3,2,1,0:T(8,128)}, bf16[3,16,256,128]{3,2,1,0:T(8,128)(2,1)}, bf16[3,8,256,128]{3,2,1,0:T(8,128)(2,1)}, f32[16,8,512]{2,1,0:T(8,128)}) custom-call(s32[65]{0:T(128)} %concatenate.148.table_ref, bf16[256,1024]{1,0:T(8,128)(2,1)} %get-tuple-element.198.normed_ref, bf16[3,8,256,128]{3,2,1,0:T(8,128)(2,1)} %get-tuple-element.199.heads_ref, ...), custom_call_target="tpu_custom_call" | custom-call | tf_op jit(solution)/shard_map/attend_back/pallas_call | solution.py:534
  417.0 8.0 %collective-permute-done.67 = bf16[2,2,40,1024]{3,2,0,1:T(8,128)(2,1)S(1)} collective-permute-done((bf16[2,2,40,1024]{3,2,0,1:T(8,128)(2,1)S(1)}, bf16[2,2,40,1024]{3,2,0,1:T(8,128)(2,1)S(1)}, u32[]{:S(2)}, u32[]{:S(2)}) %collective-permute-start.67) | collective-permute-done | bytes 327712 | tf_op jit(solution)/shard_map/ppermute | solution.py:32
  425.1 8.1 %collective-permute-done.66 = bf16[2,2,40,1024]{3,2,0,1:T(8,128)(2,1)S(1)} collective-permute-done((bf16[2,2,40,1024]{3,2,0,1:T(8,128)(2,1)S(1)}, bf16[2,2,40,1024]{3,2,0,1:T(8,128)(2,1)S(1)}, u32[]{:S(2)}, u32[]{:S(2)}) %collective-permute-start.66) | collective-permute-done | bytes 327712 | tf_op jit(solution)/shard_map/ppermute | solution.py:32
  443.2 10.4 %tokens_back.1 = (bf16[256,1024]{1,0:T(8,128)(2,1)}, f32[1,1024]{1,0:T(1,128)}) custom-call(s32[65]{0:T(128)} %concatenate.148.table_ref, bf16[256,1024]{1,0:T(8,128)(2,1)} %tokens_ref.5, f32[1,1024]{1,0:T(1,128)} %bitcast.319, f32[256,1024]{1,0:T(8,128)} %get-tuple-element.313.x1_grad_ref, bf16[3,8,256,128]{3,2,1,0:T(8,128)(2,1)} %get-tuple-element.314.dheads_ref, ...), custom_call_target="tpu_custom_call" | custom-call | tf_op jit(solution)/shard_map/tokens_back/pallas_call | solution.py:586
  478.0 5.6 collective-permute-done.77
  497.6 7.0 %block_out.1 = bf16[256,1024]{1,0:T(8,128)(2,1)} custom-call(s32[16]{0:T(128)} %pad_add_fusion.slots_ref, f32[256,1024]{1,0:T(8,128)} %get-tuple-element.280.x1_ref, f32[256,128]{1,0:T(8,128)} %get-tuple-element.338.gates_ref, bf16[8,40,1024]{2,1,0:T(8,128)(2,1)} %bitcast.280, bf16[8,40,1024]{2,1,0:T(8,128)(2,1)} %bitcast.279, s32[2,256]{1,0:T(2,128)} %fusion.23.ids_ref), custom_call_target="tpu_custom_call" | custom-call | tf_op jit(solution)/shard_map/block_out/pallas_call | solution.py:466
  510.9 7.0 %collective-permute-done.84 = bf16[4,1,256,128]{3,2,1,0:T(8,128)(2,1)S(1)} collective-permute-done((bf16[4,1,256,128]{3,2,1,0:T(8,128)(2,1)S(1)}, bf16[4,1,256,128]{3,2,1,0:T(8,128)(2,1)S(1)}, u32[]{:S(2)}, u32[]{:S(2)}) %collective-permute-start.84) | collective-permute-done | bytes 262176 | tf_op jit(solution)/shard_map/ppermute | solution.py:32
  534.4 6.4 %collective-permute-done.95 = f32[84,128]{1,0:T(8,128)S(1)} collective-permute-done((f32[84,128]{1,0:T(8,128)S(1)}, f32[84,128]{1,0:T(8,128)S(1)}, u32[]{:S(2)}, u32[]{:S(2)}) %collective-permute-start.95) | collective-permute-done | bytes 43040 | tf_op jit(solution)/shard_map/ppermute | solution.py:32
  548.2 7.7 %collective-permute-done.99 = bf16[8,256,128]{2,1,0:T(8,128)(2,1)S(1)} collective-permute-done((bf16[8,256,128]{2,1,0:T(8,128)(2,1)S(1)}, bf16[8,256,128]{2,1,0:T(8,128)(2,1)S(1)}, u32[]{:S(2)}, u32[]{:S(2)}) %collective-permute-start.99) | collective-permute-done | bytes 524320 | tf_op jit(solution)/shard_map/ppermute | solution.py:32
  556.3 7.4 %collective-permute-done.97 = bf16[8,256,128]{2,1,0:T(8,128)(2,1)S(1)} collective-permute-done((bf16[8,256,128]{2,1,0:T(8,128)(2,1)S(1)}, bf16[8,256,128]{2,1,0:T(8,128)(2,1)S(1)}, u32[]{:S(2)}, u32[]{:S(2)}) %collective-permute-start.97) | collective-permute-done | bytes 524320 | tf_op jit(solution)/shard_map/ppermute | solution.py:32
  578.5 12.2 %finish.2 = (f32[3,1024,1024]{2,1,0:T(8,128)}, f32[3,8,1024]{2,1,0:T(8,128)}, f32[3,8,1,128]{3,2,1,0:T(1,128)}, f32[3,256,128]{2,1,0:T(8,128)}) custom-call(s32[65]{0:T(128)} %concatenate.148.table_ref, s32[2]{0:T(128)} %pad_add_fusion.1.place_ref, bf16[16,256,128]{2,1,0:T(8,128)(2,1)} %pad_maximum_fusion.4.refs_0_, ...), custom_call_target="tpu_custom_call" | custom-call | tf_op jit(solution)/shard_map/finish/pallas_call | solution.py:783
  (563 shorter events, 251.5 us)
Async XLA Ops:
  38.6 19.3 %collective-permute-start.20 = (bf16[1,8,272,128]{3,2,1,0:T(8,128)(2,1)S(1)}, bf16[1,8,272,128]{3,2,1,0:T(8,128)(2,1)S(1)}, u32[]{:S(2)}, u32[]{:S(2)}) collective-permute-start(bf16[1,8,272,128]{3,2,1,0:T(8,128)(2,1)S(1)} %pad_maximum_fusion.28), channel_id=1, source_target_pairs={{0,16},{8,24},{16,0},{24,8},{1,17},{9,25},{17,1},{25,9},{2,18},{10... | collective-permute-start | bytes 1671176 | tf_op jit(solution)/shard_map/ppermute | solution.py:32
  44.7 27.6 %collective-permute-start.12 = (bf16[16,256,128]{2,1,0:T(8,128)(2,1)S(1)}, bf16[16,256,128]{2,1,0:T(8,128)(2,1)S(1)}, u32[]{:S(2)}, u32[]{:S(2)}) collective-permute-start(bf16[16,256,128]{2,1,0:T(8,128)(2,1)S(1)} %pad_maximum_fusion.2.own_v), channel_id=1, source_target_pairs={{0,1},{1,0},{2,3},{3,2},{4,5},{5,4},{6,7},{7,6},{8,9},{9,8},{10,11... | collective-permute-start | bytes 3145736 | tf_op jit(solution)/shard_map/ppermute | solution.py:32
  50.2 22.1 %collective-permute-start.11 = (bf16[16,256,128]{2,1,0:T(8,128)(2,1)S(1)}, bf16[16,256,128]{2,1,0:T(8,128)(2,1)S(1)}, u32[]{:S(2)}, u32[]{:S(2)}) collective-permute-start(bf16[16,256,128]{2,1,0:T(8,128)(2,1)S(1)} %pad_maximum_fusion.1.own_k), channel_id=1, source_target_pairs={{0,1},{1,0},{2,3},{3,2},{4,5},{5,4},{6,7},{7,6},{8,9},{9,8},{10,11... | collective-permute-start | bytes 3145736 | tf_op jit(solution)/shard_map/ppermute | solution.py:32
  50.4 21.9 %collective-permute-start.10 = (bf16[16,256,128]{2,1,0:T(8,128)(2,1)S(1)}, bf16[16,256,128]{2,1,0:T(8,128)(2,1)S(1)}, u32[]{:S(2)}, u32[]{:S(2)}) collective-permute-start(bf16[16,256,128]{2,1,0:T(8,128)(2,1)S(1)} %pad_maximum_fusion.own_q), channel_id=1, source_target_pairs={{0,1},{1,0},{2,3},{3,2},{4,5},{5,4},{6,7},{7,6},{8,9},{9,8},{10,11... | collective-permute-start | bytes 3145736 | tf_op jit(solution)/shard_map/ppermute | solution.py:32
  51.0 19.4 %collective-permute-start.14 = (bf16[1,4,40,1152]{3,2,1,0:T(8,128)(2,1)S(1)}, bf16[1,4,40,1152]{3,2,1,0:T(8,128)(2,1)S(1)}, u32[]{:S(2)}, u32[]{:S(2)}) collective-permute-start(bf16[1,4,40,1152]{3,2,1,0:T(8,128)(2,1)S(1)} %get-tuple-element.461), channel_id=1, source_target_pairs={{0,4},{1,5},{2,6},{3,7},{4,0},{5,1},{6,2},{7,3},{8,12},{9,13},{10,... | collective-permute-start | bytes 1105928 | tf_op jit(solution)/shard_map/ppermute | solution.py:32
  70.4 22.2 %collective-permute-start.21 = (bf16[16,272,128]{2,1,0:T(8,128)(2,1)S(1)}, bf16[16,272,128]{2,1,0:T(8,128)(2,1)S(1)}, u32[]{:S(2)}, u32[]{:S(2)}) collective-permute-start(bf16[16,272,128]{2,1,0:T(8,128)(2,1)S(1)} %bitcast.246), channel_id=1, source_target_pairs={{0,1},{1,0},{2,3},{3,2},{4,5},{5,4},{6,7},{7,6},{8,9},{9,8},{10,11... | collective-permute-start | bytes 3342344 | tf_op jit(solution)/shard_map/ppermute | solution.py:32
  92.5 20.1 %collective-permute-start.15 = (bf16[2,2,40,1152]{3,2,0,1:T(8,128)(2,1)}, bf16[2,2,40,1152]{3,2,0,1:T(8,128)(2,1)}, u32[]{:S(2)}, u32[]{:S(2)}) collective-permute-start(bf16[2,2,40,1152]{3,2,0,1:T(8,128)(2,1)} %get-tuple-element.459), channel_id=1, source_target_pairs={{0,4},{1,5},{2,6},{3,7},{4,0},{5,1},{6,2},{7,3},{8,12},{9,13},{10,... | collective-permute-start | bytes 1105928 | tf_op jit(solution)/shard_map/ppermute | solution.py:32
  135.0 26.7 %collective-permute-start.32 = (bf16[320,1152]{1,0:T(8,128)(2,1)S(1)}, bf16[320,1152]{1,0:T(8,128)(2,1)}, u32[]{:S(2)}, u32[]{:S(2)}) collective-permute-start(bf16[320,1152]{1,0:T(8,128)(2,1)S(1)} %bitcast.256), channel_id=1, source_target_pairs={{0,2},{1,3},{2,0},{3,1},{4,6},{5,7},{6,4},{7,5},{8,10},{9,11},{10,... | collective-permute-start | bytes 2211848 | tf_op jit(solution)/shard_map/ppermute | solution.py:32
  140.4 36.2 %collective-permute-start.33 = (bf16[320,1152]{1,0:T(8,128)(2,1)S(1)}, bf16[320,1152]{1,0:T(8,128)(2,1)}, u32[]{:S(2)}, u32[]{:S(2)}) collective-permute-start(bf16[320,1152]{1,0:T(8,128)(2,1)S(1)} %bitcast.253), channel_id=1, source_target_pairs={{0,2},{1,3},{2,0},{3,1},{4,6},{5,7},{6,4},{7,5},{8,10},{9,11},{10,... | collective-permute-start | bytes 2211848 | tf_op jit(solution)/shard_map/ppermute | solution.py:32
  178.7 31.8 %collective-permute-start.36 = (bf16[320,1152]{1,0:T(8,128)(2,1)}, bf16[320,1152]{1,0:T(8,128)(2,1)}, u32[]{:S(2)}, u32[]{:S(2)}) collective-permute-start(bf16[320,1152]{1,0:T(8,128)(2,1)} %collective-permute-done.32.refs_2_), channel_id=1, source_target_pairs={{0,1},{1,0},{2,3},{3,2},{4,5},{5,4},{6,7},{7,6},{8,9},{9,8},{10,11... | collective-permute-start | bytes 2211848 | tf_op jit(solution)/shard_map/ppermute | solution.py:32
  179.2 31.3 %collective-permute-start.37 = (bf16[320,1152]{1,0:T(8,128)(2,1)}, bf16[320,1152]{1,0:T(8,128)(2,1)S(1)}, u32[]{:S(2)}, u32[]{:S(2)}) collective-permute-start(bf16[320,1152]{1,0:T(8,128)(2,1)} %collective-permute-done.33.refs_2_), channel_id=1, source_target_pairs={{0,1},{1,0},{2,3},{3,2},{4,5},{5,4},{6,7},{7,6},{8,9},{9,8},{10,11... | collective-permute-start | bytes 2211848 | tf_op jit(solution)/shard_map/ppermute | solution.py:32
  179.2 29.9 %collective-permute-start.34 = (bf16[320,1024]{1,0:T(8,128)(2,1)S(1)}, bf16[320,1024]{1,0:T(8,128)(2,1)}, u32[]{:S(2)}, u32[]{:S(2)}) collective-permute-start(bf16[320,1024]{1,0:T(8,128)(2,1)S(1)} %bitcast.271), channel_id=1, source_target_pairs={{0,2},{1,3},{2,0},{3,1},{4,6},{5,7},{6,4},{7,5},{8,10},{9,11},{10,... | collective-permute-start | bytes 1966088 | tf_op jit(solution)/shard_map/ppermute | solution.py:32
  179.8 30.7 %collective-permute-start.35 = (bf16[320,1024]{1,0:T(8,128)(2,1)S(1)}, bf16[320,1024]{1,0:T(8,128)(2,1)}, u32[]{:S(2)}, u32[]{:S(2)}) collective-permute-start(bf16[320,1024]{1,0:T(8,128)(2,1)S(1)} %bitcast.268), channel_id=1, source_target_pairs={{0,2},{1,3},{2,0},{3,1},{4,6},{5,7},{6,4},{7,5},{8,10},{9,11},{10,... | collective-permute-start | bytes 1966088 | tf_op jit(solution)/shard_map/ppermute | solution.py:32
  211.1 20.7 %collective-permute-start.51 = (bf16[320,1024]{1,0:T(8,128)(2,1)}, bf16[320,1024]{1,0:T(8,128)(2,1)}, u32[]{:S(2)}, u32[]{:S(2)}) collective-permute-start(bf16[320,1024]{1,0:T(8,128)(2,1)} %get-tuple-element.271), channel_id=1, source_target_pairs={{0,1},{1,0},{2,3},{3,2},{4,5},{5,4},{6,7},{7,6},{8,9},{9,8},{10,11... | collective-permute-start | bytes 1966088 | tf_op jit(solution)/shard_map/ppermute | solution.py:32
  229.1 21.0 %collective-permute-start.41 = (bf16[320,1152]{1,0:T(8,128)(2,1)}, bf16[320,1152]{1,0:T(8,128)(2,1)}, u32[]{:S(2)}, u32[]{:S(2)}) collective-permute-start(bf16[320,1152]{1,0:T(8,128)(2,1)} %get-tuple-element.234), channel_id=1, source_target_pairs={{0,1},{1,0},{2,3},{3,2},{4,5},{5,4},{6,7},{7,6},{8,9},{9,8},{10,11... | collective-permute-start | bytes 2211848 | tf_op jit(solution)/shard_map/ppermute | solution.py:32
  229.3 22.8 %collective-permute-start.40 = (bf16[320,1152]{1,0:T(8,128)(2,1)}, bf16[320,1152]{1,0:T(8,128)(2,1)S(1)}, u32[]{:S(2)}, u32[]{:S(2)}) collective-permute-start(bf16[320,1152]{1,0:T(8,128)(2,1)} %get-tuple-element.232), channel_id=1, source_target_pairs={{0,1},{1,0},{2,3},{3,2},{4,5},{5,4},{6,7},{7,6},{8,9},{9,8},{10,11... | collective-permute-start | bytes 2211848 | tf_op jit(solution)/shard_map/ppermute | solution.py:32
  233.4 39.1 %collective-permute-start.53 = (bf16[320,1024]{1,0:T(8,128)(2,1)}, bf16[320,1024]{1,0:T(8,128)(2,1)}, u32[]{:S(2)}, u32[]{:S(2)}) collective-permute-start(bf16[320,1024]{1,0:T(8,128)(2,1)} %get-tuple-element.275), channel_id=1, source_target_pairs={{0,1},{1,0},{2,3},{3,2},{4,5},{5,4},{6,7},{7,6},{8,9},{9,8},{10,11... | collective-permute-start | bytes 1966088 | tf_op jit(solution)/shard_map/ppermute | solution.py:32
  251.7 19.4 %collective-permute-start.46 = (bf16[320,1152]{1,0:T(8,128)(2,1)S(1)}, bf16[320,1152]{1,0:T(8,128)(2,1)S(1)}, u32[]{:S(2)}, u32[]{:S(2)}) collective-permute-start(bf16[320,1152]{1,0:T(8,128)(2,1)S(1)} %copy-done.39), channel_id=1, source_target_pairs={{0,2},{1,3},{2,0},{3,1},{4,6},{5,7},{6,4},{7,5},{8,10},{9,11},{10,... | collective-permute-start | bytes 2211848 | tf_op jit(solution)/shard_map/ppermute | solution.py:32
  252.2 22.3 %collective-permute-start.54 = (bf16[320,1024]{1,0:T(8,128)(2,1)S(1)}, bf16[320,1024]{1,0:T(8,128)(2,1)S(1)}, u32[]{:S(2)}, u32[]{:S(2)}) collective-permute-start(bf16[320,1024]{1,0:T(8,128)(2,1)S(1)} %copy-done.66), channel_id=1, source_target_pairs={{0,1},{1,0},{2,3},{3,2},{4,5},{5,4},{6,7},{7,6},{8,9},{9,8},{10,11... | collective-permute-start | bytes 1966088 | tf_op jit(solution)/shard_map/ppermute | solution.py:32
  252.5 42.3 %collective-permute-start.48 = (bf16[320,1152]{1,0:T(8,128)(2,1)S(1)}, bf16[320,1152]{1,0:T(8,128)(2,1)S(1)}, u32[]{:S(2)}, u32[]{:S(2)}) collective-permute-start(bf16[320,1152]{1,0:T(8,128)(2,1)S(1)} %add_convert_fusion.2), channel_id=1, source_target_pairs={{0,2},{1,3},{2,0},{3,1},{4,6},{5,7},{6,4},{7,5},{8,10},{9,11},{10,... | collective-permute-start | bytes 2211848 | tf_op jit(solution)/shard_map/ppermute | solution.py:32
  272.1 21.7 %collective-permute-start.47 = (bf16[4,1,40,1152]{3,2,0,1:T(8,128)(2,1)}, bf16[4,1,40,1152]{3,2,0,1:T(8,128)(2,1)}, u32[]{:S(2)}, u32[]{:S(2)}) collective-permute-start(bf16[4,1,40,1152]{3,2,0,1:T(8,128)(2,1)} %bitcast.69), channel_id=1, source_target_pairs={{0,16},{8,24},{16,0},{24,8},{1,17},{9,25},{17,1},{25,9},{2,18},{10... | collective-permute-start | bytes 1105928 | tf_op jit(solution)/shard_map/ppermute | solution.py:32
  295.8 20.9 %collective-permute-start.50 = (bf16[4,1,40,1152]{3,2,0,1:T(8,128)(2,1)}, bf16[4,1,40,1152]{3,2,0,1:T(8,128)(2,1)}, u32[]{:S(2)}, u32[]{:S(2)}) collective-permute-start(bf16[4,1,40,1152]{3,2,0,1:T(8,128)(2,1)} %bitcast.76), channel_id=1, source_target_pairs={{0,8},{8,0},{16,24},{24,16},{1,9},{9,1},{17,25},{25,17},{2,10},{10... | collective-permute-start | bytes 1105928 | tf_op jit(solution)/shard_map/ppermute | solution.py:32
  321.7 66.5 %collective-permute-start.55 = (bf16[320,1024]{1,0:T(8,128)(2,1)}, bf16[320,1024]{1,0:T(8,128)(2,1)}, u32[]{:S(2)}, u32[]{:S(2)}) collective-permute-start(bf16[320,1024]{1,0:T(8,128)(2,1)} %add_convert_fusion.7), channel_id=1, source_target_pairs={{0,2},{1,3},{2,0},{3,1},{4,6},{5,7},{6,4},{7,5},{8,10},{9,11},{10,... | collective-permute-start | bytes 1966088 | tf_op jit(solution)/shard_map/ppermute | solution.py:32
  321.7 66.5 %collective-permute-start.56 = (bf16[320,1024]{1,0:T(8,128)(2,1)}, bf16[320,1024]{1,0:T(8,128)(2,1)}, u32[]{:S(2)}, u32[]{:S(2)}) collective-permute-start(bf16[320,1024]{1,0:T(8,128)(2,1)} %add_convert_fusion.6), channel_id=1, source_target_pairs={{0,2},{1,3},{2,0},{3,1},{4,6},{5,7},{6,4},{7,5},{8,10},{9,11},{10,... | collective-permute-start | bytes 1966088 | tf_op jit(solution)/shard_map/ppermute | solution.py:32
  332.7 28.1 %collective-permute-start.61 = (f32[3,1024]{1,0:T(4,128)S(1)}, f32[3,1024]{1,0:T(4,128)S(1)}, u32[]{:S(2)}, u32[]{:S(2)}) collective-permute-start(f32[3,1024]{1,0:T(4,128)S(1)} %fusion.27), channel_id=1, source_target_pairs={{0,2},{1,3},{2,0},{3,1},{4,6},{5,7},{6,4},{7,5},{8,10},{9,11},{10,... | collective-permute-start | bytes 36872 | tf_op jit(solution)/shard_map/ppermute | solution.py:32
  333.6 42.0 %collective-permute-start.60 = (bf16[1,4,40,1152]{3,2,1,0:T(8,128)(2,1)}, bf16[1,4,40,1152]{3,2,1,0:T(8,128)(2,1)}, u32[]{:S(2)}, u32[]{:S(2)}) collective-permute-start(bf16[1,4,40,1152]{3,2,1,0:T(8,128)(2,1)} %get-tuple-element.441), channel_id=1, source_target_pairs={{0,4},{1,5},{2,6},{3,7},{4,0},{5,1},{6,2},{7,3},{8,12},{9,13},{10,... | collective-permute-start | bytes 1105928 | tf_op jit(solution)/shard_map/ppermute | solution.py:32
  388.2 22.4 %collective-permute-start.64 = (bf16[16,256,128]{2,1,0:T(8,128)(2,1)}, bf16[16,256,128]{2,1,0:T(8,128)(2,1)S(1)}, u32[]{:S(2)}, u32[]{:S(2)}) collective-permute-start(bf16[16,256,128]{2,1,0:T(8,128)(2,1)} %get-tuple-element.301), channel_id=1, source_target_pairs={{0,1},{1,0},{2,3},{3,2},{4,5},{5,4},{6,7},{7,6},{8,9},{9,8},{10,11... | collective-permute-start | bytes 3145736 | tf_op jit(solution)/shard_map/ppermute | solution.py:32
  389.7 20.8 %collective-permute-start.63 = (bf16[4,1,40,1024]{3,2,0,1:T(8,128)(2,1)S(1)}, bf16[4,1,40,1024]{3,2,0,1:T(8,128)(2,1)S(1)}, u32[]{:S(2)}, u32[]{:S(2)}) collective-permute-start(bf16[4,1,40,1024]{3,2,0,1:T(8,128)(2,1)S(1)} %bitcast.298), channel_id=1, source_target_pairs={{0,8},{8,0},{16,24},{24,16},{1,9},{9,1},{17,25},{25,17},{2,10},{10... | collective-permute-start | bytes 983048 | tf_op jit(solution)/shard_map/ppermute | solution.py:32
  414.7 18.7 %collective-permute-start.65 = (bf16[3,16,256,128]{3,2,1,0:T(8,128)(2,1)S(1)}, bf16[3,16,256,128]{3,2,1,0:T(8,128)(2,1)S(1)}, u32[]{:S(2)}, u32[]{:S(2)}) collective-permute-start(bf16[3,16,256,128]{3,2,1,0:T(8,128)(2,1)S(1)} %copy-done.65), channel_id=1, source_target_pairs={{0,1},{1,0},{2,3},{3,2},{4,5},{5,4},{6,7},{7,6},{8,9},{9,8},{10,11... | collective-permute-start | bytes 9437192 | tf_op jit(solution)/shard_map/ppermute | solution.py:32
  438.3 22.6 %collective-permute-start.73 = (bf16[1,4,40,1024]{3,2,1,0:T(8,128)(2,1)}, bf16[1,4,40,1024]{3,2,1,0:T(8,128)(2,1)}, u32[]{:S(2)}, u32[]{:S(2)}) collective-permute-start(bf16[1,4,40,1024]{3,2,1,0:T(8,128)(2,1)} %get-tuple-element.465), channel_id=1, source_target_pairs={{0,4},{1,5},{2,6},{3,7},{4,0},{5,1},{6,2},{7,3},{8,12},{9,13},{10,... | collective-permute-start | bytes 983048 | tf_op jit(solution)/shard_map/ppermute | solution.py:32
  439.1 26.4 %collective-permute-start.72 = (bf16[1,4,40,1024]{3,2,1,0:T(8,128)(2,1)}, bf16[1,4,40,1024]{3,2,1,0:T(8,128)(2,1)}, u32[]{:S(2)}, u32[]{:S(2)}) collective-permute-start(bf16[1,4,40,1024]{3,2,1,0:T(8,128)(2,1)} %get-tuple-element.467), channel_id=1, source_target_pairs={{0,8},{8,0},{16,24},{24,16},{1,9},{9,1},{17,25},{25,17},{2,10},{10... | collective-permute-start | bytes 983048 | tf_op jit(solution)/shard_map/ppermute | solution.py:32
  440.8 26.5 %collective-permute-start.71 = (bf16[8,256,128]{2,1,0:T(8,128)(2,1)}, bf16[8,256,128]{2,1,0:T(8,128)(2,1)S(1)}, u32[]{:S(2)}, u32[]{:S(2)}) collective-permute-start(bf16[8,256,128]{2,1,0:T(8,128)(2,1)} %slice.685), channel_id=1, source_target_pairs={{0,16},{8,24},{16,0},{24,8},{1,17},{9,25},{17,1},{25,9},{2,18},{10... | collective-permute-start | bytes 1572872 | tf_op jit(solution)/shard_map/ppermute | solution.py:32
  (143 other events, 1456.4 us)

commit v3 on v2

--- a/solution.py
+++ b/solution.py
@@ -15,7 +15,6 @@
 GELU_A = 0.044715
 BF = jnp.bfloat16
 F32 = jnp.float32
-VMEM_LIMIT = 60 * 1024 * 1024
 NN = (((1,), (0,)), ((), ()))
 NT = (((1,), (1,)), ((), ()))
 TN = (((0,), (0,)), ((), ()))
@@ -45,8 +44,12 @@
         far + narrow + near + core,
         far + near + narrow + core,
         far + narrow[1:] + near + narrow[:1] + core,
-        far + narrow[:1] + near + narrow[1:] + core,
-    )
+    )
+
+
+def row_cuts(count):
+    share = -(-count // 48) * 16
+    return [min(i * share, count) for i in range(4)]
 
 
 def block_slots(order, groups, wide_count):
@@ -71,42 +74,49 @@
     return count
 
 
-def grow(blocks, hop, axis=0):
-    return jnp.concatenate([blocks, from_partner(blocks, hop)], axis=axis)
-
-
-def gather_chains(blocks, orders):
-    shared = shared_hops(orders)
-    blocks = blocks[:, None]
-    for hop in orders[0][:shared]:
-        blocks = grow(blocks, hop, 1)
-    chains = [blocks[i] for i in range(len(orders))]
-    for stage in range(shared, len(orders[0]) - 1):
-        chains = [grow(chain, order[stage]) for chain, order in zip(chains, orders)]
-    return chains
-
-
-def core_sum(keep, send, order):
-    return keep + from_partner(send, order[-1]).astype(F32)
-
-
-def halve(total, hop, axis=0):
+def grow(blocks, got, axis=0):
+    return jnp.concatenate([blocks, got], axis=axis)
+
+
+def core_sum(keep, got):
+    return keep + got.astype(F32)
+
+
+def halve_send(total, hop, axis=0):
     half = total.shape[axis] // 2
-    mine = lax.slice_in_dim(total, 0, half, axis=axis)
-    theirs = lax.slice_in_dim(total, half, 2 * half, axis=axis)
-    return mine + from_partner(theirs.astype(BF), hop).astype(F32)
-
-
-def send_step(state, hop):
+    return from_partner(lax.slice_in_dim(total, half, 2 * half, axis=axis).astype(BF), hop)
+
+
+def halve_add(total, got, axis=0):
+    half = total.shape[axis] // 2
+    return lax.slice_in_dim(total, 0, half, axis=axis) + got.astype(F32)
+
+
+def row_send(state, hop):
     sources, places = state.shape[:2]
-    split = state.reshape((sources, 2, places // 2) + state.shape[2:])
-    return jnp.concatenate([split[:, 0], from_partner(split[:, 1], hop)], axis=0)
-
-
-def return_step(state, hop):
-    half = state.shape[0] // 2
-    got = from_partner(state[half:], hop)
-    return jnp.stack([state[:half], got], axis=1).reshape((half, -1) + state.shape[2:])
+    return from_partner(state.reshape((sources, 2, places // 2) + state.shape[2:])[:, 1], hop)
+
+
+def row_join(state, got):
+    sources, places = state.shape[:2]
+    kept = state.reshape((sources, 2, places // 2) + state.shape[2:])[:, 0]
+    return jnp.concatenate([kept, got], axis=0)
+
+
+def back_split(state, left, hop):
+    low = 2 ** left.index(hop)
+    split = state.reshape((-1, 2, low) + state.shape[1:])
+    return [split[:, i].reshape((-1,) + state.shape[1:]) for i in range(2)]
+
+
+def back_send(state, left, hop):
+    return from_partner(back_split(state, left, hop)[1], hop)
+
+
+def back_join(state, left, hop, got):
+    kept = back_split(state, left, hop)[0]
+    joined = jnp.stack([kept, got], axis=1).reshape((got.shape[0], -1) + state.shape[2:])
+    return joined, [other for other in left if other != hop]
 
 
 def row_slots(hops, groups, places, parts):
@@ -167,8 +177,14 @@
     return pl.BlockSpec(memory_space=pltpu.SMEM)
 
 
-def params():
-    return pltpu.CompilerParams(vmem_limit_bytes=VMEM_LIMIT)
+def params(mebibytes):
+    return pltpu.CompilerParams(vmem_limit_bytes=mebibytes * 1024 * 1024)
+
+
+def cost(micros):
+    return pl.CostEstimate(
+        flops=int(micros * 1153e6), transcendentals=0, bytes_accessed=int(micros * 3690e3)
+    )
 
 
 def lane_masks(head_dim):
@@ -195,7 +211,7 @@
             total = None
             for n in range(groups):
                 at = table_ref[1 + (m * groups + n) * pairs + w2]
-                block = jnp.concatenate([own[at], far[at]], axis=1)
+                block = jnp.concatenate([own[at, :rows], far[at, :rows]], axis=1)
                 part = mm(normed_ref[:, n * rows : (n + 1) * rows], block)
                 total = part if total is None else total + part
             total = total.astype(BF)
@@ -244,8 +260,9 @@
             jax.ShapeDtypeStruct((head_count, length, length), F32),
             jax.ShapeDtypeStruct((2 * pairs, length, LANES), BF),
         ],
-        compiler_params=params(),
+        compiler_params=params(14),
         name="attend",
+        cost_estimate=cost(16),
     )(table, tokens, gain.reshape(1, features), bias_table, *owns, *fars)
 
 
@@ -288,20 +305,35 @@
         in_specs=[smem()] + [vmem()] * 3,
         out_specs=[vmem()] * 2,
         out_shape=[jax.ShapeDtypeStruct((experts, cap // 2, features + LANES), BF)] * 2,
-        compiler_params=params(),
+        compiler_params=params(8),
         name="upstream_rows",
+        cost_estimate=cost(3),
     )(row_table, upstream, row_ids, other_ids)
 
 
+def projection_block(halves, table_ref, n, w2, groups, pairs, depth, cuts):
+    sides = []
+    for refs in halves:
+        parts = []
+        for i in range(3):
+            at = table_ref[1 + (i * groups + n) * pairs + w2]
+            first = depth if refs[i].shape[1] > depth else 0
+            parts.append(refs[i][at, first : first + cuts[i + 1] - cuts[i]])
+        sides.append(jnp.concatenate(parts, axis=0))
+    return jnp.concatenate(sides, axis=1)
+
+
 def post_body(
-    table_ref, slots_ref, tokens_ref, attended_ref, own, far, gain_ref, ids_ref,
+    table_ref, slots_ref, tokens_ref, attended_ref,
+    own_q, own_k, own_v, far_q, far_k, far_v, gain_ref, ids_ref,
     x1_ref, normed_ref, send_a, send_b,
-    *, groups, experts, cap,
+    *, groups, experts, cap, cuts,
 ):
     length, features = tokens_ref.shape
     pairs = features // (2 * LANES)
     per_group = 2 * pairs // groups
     depth = features // groups
+    halves = ((own_q, own_k, own_v), (far_q, far_k, far_v))
     core = table_ref[0]
     rows = [
         jnp.concatenate([attended_ref[n * per_group + i] for i in range(per_group)], axis=1)
@@ -310,8 +342,7 @@
     for w2 in range(pairs):
         total = None
         for n in range(groups):
-            at = table_ref[1 + (3 * groups + n) * pairs + w2]
-            block = jnp.concatenate([own[at, :depth], far[at, :depth]], axis=1)
+            block = projection_block(halves, table_ref, n, w2, groups, pairs, depth, cuts)
             part = mm(rows[n], block)
             total = part if total is None else total + part
         for j in range(2):
@@ -326,11 +357,14 @@
     spread_rows(normed, ids_ref, slots_ref, (send_a, send_b), experts, cap)
 
 
-def post_call(table, row_table, tokens, attended, out_halves, gain, row_ids, groups, experts, cap):
+def post_call(table, row_table, tokens, attended, gathered, gain, row_ids, groups, experts, cap):
     length, features = tokens.shape
+    owns = [g[0] for g in gathered]
+    fars = [g[1] for g in gathered]
+    cuts = row_cuts(features // groups)
     return pl.pallas_call(
-        functools.partial(post_body, groups=groups, experts=experts, cap=cap),
-        in_specs=[smem()] * 2 + [vmem()] * 6,
+        functools.partial(post_body, groups=groups, experts=experts, cap=cap, cuts=cuts),
+        in_specs=[smem()] * 2 + [vmem()] * 10,
         out_specs=[vmem()] * 4,
         out_shape=[
             jax.ShapeDtypeStruct((length, features), F32),
@@ -338,22 +372,27 @@
             jax.ShapeDtypeStruct((experts, cap // 2, features), BF),
             jax.ShapeDtypeStruct((experts, cap // 2, features), BF),
         ],
-        compiler_params=params(),
+        compiler_params=params(12),
         name="post",
-    )(table, row_table, tokens, attended, *out_halves, gain.reshape(1, features), row_ids)
+        cost_estimate=cost(3),
+    )(
+        table, row_table, tokens, attended, *owns, *fars, gain.reshape(1, features), row_ids
+    )
 
 
 def mid_body(
     table_ref, slots_ref, x1_ref, gain_ref, normed_ref, upstream_ref, back_a, back_b,
-    ids_ref, choice_ref, router_ref, attended_ref, own, far,
+    ids_ref, choice_ref, router_ref, attended_ref,
+    own_q, own_k, own_v, far_q, far_k, far_v,
     x1_grad_ref, gates_ref, gain_out_ref, router_out_ref, keep_ref, send_ref, att_grad_ref,
-    *, groups, experts, cap,
+    *, groups, experts, cap, cuts,
 ):
     length, features = x1_ref.shape
     pairs = features // (2 * LANES)
     per_group = 2 * pairs // groups
     rows = features // groups
     half = cap // 2
+    halves = ((own_q, own_k, own_v), (far_q, far_k, far_v))
     core = table_ref[0]
     dmoe = jnp.zeros((length, features), F32)
     dots = [jnp.zeros((length, LANES), F32)] * 2
@@ -383,7 +422,7 @@
         picks[1], gates[1] * (dgates[1] - inner), 0.0
     )
     dlogits = dlogits.astype(BF)
-    router_out_ref[...] = mm(normed, dlogits, TN)
+    router_out_ref[...] = mm(dlogits, normed, TN)
     dmoe = dmoe + mm(dlogits, router_ref[...], NT)
     x1 = x1_ref[...]
     factor = lax.rsqrt(jnp.mean(x1 * x1, axis=-1, keepdims=True) + NORM_EPS)
@@ -405,11 +444,13 @@
         )
         total = None
         for w2 in range(pairs):
-            at = table_ref[1 + (3 * groups + n) * pairs + w2]
             block = mm(att, branches[w2], TN)
-            keep_ref[at] = block[:, :LANES]
-            send_ref[at] = block[:, LANES:].astype(BF)
-            block = jnp.concatenate([own[at, :rows], far[at, :rows]], axis=1)
+            for i in range(3):
+                at = table_ref[1 + (i * groups + n) * pairs + w2]
+                keep_ref[at, cuts[i] : cuts[i + 1]] = block[cuts[i] : cuts[i + 1], :LANES]
+                send = block[cuts[i] : cuts[i + 1], LANES:].astype(BF)
+                send_ref[at, cuts[i] : cuts[i + 1]] = send
+            block = projection_block(halves, table_ref, n, w2, groups, pairs, rows, cuts)
             part = mm(branches[w2], block, NT)
             total = part if total is None else total + part
         for i in range(per_group):
@@ -418,29 +459,34 @@
 
 def mid_call(
     table, row_table, x1, gain, normed, upstream, backs, row_ids, choices, router, attended,
-    out_halves, groups, experts, cap,
+    gathered, groups, experts, cap,
 ):
     length, features = x1.shape
     pairs = features // (2 * LANES)
     rows = features // groups
+    owns = [g[0] for g in gathered]
+    fars = [g[1] for g in gathered]
     return pl.pallas_call(
-        functools.partial(mid_body, groups=groups, experts=experts, cap=cap),
-        in_specs=[smem()] * 2 + [vmem()] * 12,
+        functools.partial(
+            mid_body, groups=groups, experts=experts, cap=cap, cuts=row_cuts(rows)
+        ),
+        in_specs=[smem()] * 2 + [vmem()] * 16,
         out_specs=[vmem()] * 7,
         out_shape=[
             jax.ShapeDtypeStruct((length, features), F32),
             jax.ShapeDtypeStruct((length, LANES), F32),
             jax.ShapeDtypeStruct((1, features), F32),
-            jax.ShapeDtypeStruct((features, LANES), F32),
+            jax.ShapeDtypeStruct((LANES, features), F32),
             jax.ShapeDtypeStruct((groups * pairs, rows, LANES), F32),
             jax.ShapeDtypeStruct((groups * pairs, rows, LANES), BF),
             jax.ShapeDtypeStruct((2 * pairs, length, LANES), BF),
         ],
-        compiler_params=params(),
+        compiler_params=params(16),
         name="mid",
+        cost_estimate=cost(7),
     )(
         table, row_table, x1, gain.reshape(1, features), normed, upstream, *backs,
-        row_ids, choices, router, attended, *out_halves,
+        row_ids, choices, router, attended, *owns, *fars,
     )
 
 
@@ -468,18 +514,23 @@
         in_specs=[smem()] + [vmem()] * 5,
         out_specs=vmem(),
         out_shape=jax.ShapeDtypeStruct(x1.shape, BF),
-        compiler_params=params(),
+        compiler_params=params(8),
         name="block_out",
+        cost_estimate=cost(7),
     )(row_table, x1, gates, *backs, row_ids)
 
 
 def attend_back_body(
-    table_ref, normed_ref, heads_ref, probs_ref, grad_ref,
-    keep_ref, send_ref, dheads_ref, diag_ref,
-    *, groups, pairs, head_dim,
+    table_ref, normed_ref, heads_ref, probs_ref, grad_ref, out_keep_ref, out_send_ref,
+    keep_q, keep_k, keep_v, send_q, send_k, send_v, dheads_ref, diag_ref,
+    *, groups, pairs, head_dim, cuts,
 ):
     length, features = normed_ref.shape
     rows = features // groups
+    keeps, sends = (keep_q, keep_k, keep_v), (send_q, send_k, send_v)
+    for i in range(3):
+        keeps[i][:, rows:] = out_keep_ref[:, cuts[i] : cuts[i + 1]]
+        sends[i][:, rows:] = out_send_ref[:, cuts[i] : cuts[i + 1]]
     masks = lane_masks(head_dim)
     scale = head_dim**-0.5
 
@@ -518,32 +569,39 @@
             for n in range(groups):
                 at = table_ref[1 + (m * groups + n) * pairs + w2]
                 block = mm(normed_ref[:, n * rows : (n + 1) * rows], both, TN)
-                keep_ref[m, at] = block[:, :LANES]
-                send_ref[m, at] = block[:, LANES:].astype(BF)
+                keeps[m][at, :rows] = block[:, :LANES]
+                sends[m][at, :rows] = block[:, LANES:].astype(BF)
         return carry
 
     lax.fori_loop(0, pairs, weigh, 0)
 
 
-def attend_back_call(table, normed, heads, probs, attended_grad, groups, head_dim):
+def attend_back_call(
+    table, normed, heads, probs, attended_grad, out_keep, out_send, groups, head_dim
+):
     length, features = normed.shape
     pairs = features // (2 * LANES)
     head_count = features // head_dim
     rows = features // groups
-    body = functools.partial(attend_back_body, groups=groups, pairs=pairs, head_dim=head_dim)
+    cuts = row_cuts(rows)
+    body = functools.partial(
+        attend_back_body, groups=groups, pairs=pairs, head_dim=head_dim, cuts=cuts
+    )
+    shapes = [(groups * pairs, rows + b - a, LANES) for a, b in zip(cuts[:-1], cuts[1:])]
     return pl.pallas_call(
         body,
-        in_specs=[smem()] + [vmem()] * 4,
-        out_specs=[vmem()] * 4,
-        out_shape=[
-            jax.ShapeDtypeStruct((3, groups * pairs, rows, LANES), F32),
-            jax.ShapeDtypeStruct((3, groups * pairs, rows, LANES), BF),
+        in_specs=[smem()] + [vmem()] * 6,
+        out_specs=[vmem()] * 8,
+        out_shape=[jax.ShapeDtypeStruct(shape, F32) for shape in shapes]
+        + [jax.ShapeDtypeStruct(shape, BF) for shape in shapes]
+        + [
             jax.ShapeDtypeStruct((3, 2 * pairs, length, LANES), BF),
             jax.ShapeDtypeStruct((head_count, 8, 2 * length), F32),
         ],
-        compiler_params=params(),
+        compiler_params=params(22),
         name="attend_back",
-    )(table, normed, heads, probs, attended_grad)
+        cost_estimate=cost(12),
+    )(table, normed, heads, probs, attended_grad, out_keep, out_send)
 
 
 def tokens_back_body(
@@ -563,7 +621,8 @@
                 both = jnp.concatenate(
                     [dheads_ref[m, 2 * w2 + core], dheads_ref[m, 2 * w2 + 1 - core]], axis=1
                 )
-                total = total + mm(both, jnp.concatenate([own[at], far[at]], axis=1), NT)
+                block = jnp.concatenate([own[at, :rows], far[at, :rows]], axis=1)
+                total = total + mm(both, block, NT)
             return total
 
         total = lax.fori_loop(0, pairs, step, jnp.zeros((length, rows), F32))
@@ -592,8 +651,9 @@
             jax.ShapeDtypeStruct((1, features), F32),
         ],
         scratch_shapes=[pltpu.VMEM((length, features), F32)],
-        compiler_params=params(),
+        compiler_params=params(14),
         name="tokens_back",
+        cost_estimate=cost(10),
     )(table, tokens, gain.reshape(1, features), x1_grad, dheads, *owns, *fars)
 
 
@@ -625,30 +685,23 @@
     grad = up[:, :features].astype(F32)
     dy = (gate * grad).astype(BF)
     dy_ref[...] = dy
-    y, dx = None, None
     step = 2 * LANES
     width = gate_w.shape[0]
     for f in range(0, width, step):
         chunk = slice(f, min(f + step, width))
-        gate_f, up_f, down_f = gate_w[chunk, :], up_w[chunk, :], down_w[chunk, :]
-        g = mm(x, gate_f, NT)
-        u = mm(x, up_f, NT)
-        dh = mm(dy, down_f, NT)
-        t = jnp.tanh(g * (GELU_C + (GELU_C * GELU_A) * (g * g)))
+        g = mm(x, gate_w[chunk, :], NT)
+        u = mm(x, up_w[chunk, :], NT)
+        dh = mm(dy, down_w[chunk, :], NT)
+        square = g * g
+        t = jnp.tanh(g * (GELU_C + (GELU_C * GELU_A) * square))
         half_t = 0.5 + 0.5 * t
         act = g * half_t
-        hidden = (act * u).astype(BF)
-        slope = half_t + act * (1.0 - t) * (GELU_C + (3.0 * GELU_C * GELU_A) * (g * g))
-        dg = (dh * u * slope).astype(BF)
-        du = (dh * act).astype(BF)
-        hidden_ref[:, chunk] = hidden
-        dgate_ref[:, chunk] = dg
-        dup_ref[:, chunk] = du
-        y_f = mm(hidden, down_f)
-        dx_f = mm(dg, gate_f) + mm(du, up_f)
-        y = y_f if y is None else y + y_f
-        dx = dx_f if dx is None else dx + dx_f
-    y = y.astype(BF)
+        slope = half_t + act * ((1.0 - t) * (GELU_C + (3.0 * GELU_C * GELU_A) * square))
+        hidden_ref[:, chunk] = (act * u).astype(BF)
+        dgate_ref[:, chunk] = (dh * u * slope).astype(BF)
+        dup_ref[:, chunk] = (dh * act).astype(BF)
+    y = mm(hidden_ref[...], down_w[...]).astype(BF)
+    dx = mm(dgate_ref[...], gate_w[...]) + mm(dup_ref[...], up_w[...])
     dot = jnp.sum(grad * y.astype(F32), axis=1, keepdims=True)
     dx = dx.astype(BF)
     dot = jnp.broadcast_to(dot, (x.shape[0], LANES)).astype(BF)
@@ -667,7 +720,7 @@
     count = len(xs)
 
     def whole(arr):
-        return pl.BlockSpec(arr.shape, lambda i, e: (0, 0))
+        return pl.BlockSpec(arr.shape, lambda i, e: (0, 0), pipeline_mode=pl.Buffered(1))
 
     def kept_spec(cols):
         return pl.BlockSpec((rows, cols), lambda i, e: (first + i, 0))
@@ -692,8 +745,9 @@
         input_output_aliases={
             1 + len(inputs) + i: 2 * count + i for i in range(len(kept_in))
         },
-        compiler_params=params(),
+        compiler_params=params(48),
         name="expert",
+        cost_estimate=cost(6 * count),
     )(expert, *inputs, *kept_in)
     return out[:count], out[count : 2 * count], out[2 * count :]
 
@@ -715,85 +769,128 @@
         ],
         out_specs=pl.BlockSpec((width, size), lambda i: (0, i)),
         out_shape=jax.ShapeDtypeStruct((width, features), F32),
-        compiler_params=params(),
+        compiler_params=params(30),
         name="expert_grad",
+        cost_estimate=cost(9),
     )(left, right)
 
 
-def finish_body(table_ref, place_ref, *refs, groups, pairs, count, first, update, subtract):
-    owns, fars, refs = refs[:count], refs[count : 2 * count], refs[2 * count :]
+def finish_body(
+    table_ref, place_ref, own_q, own_k, own_v, far_q, far_k, far_v, *refs,
+    groups, pairs, cuts, update,
+):
     if update:
         mine_ref, weight_ref, refs = refs[0], refs[1], refs[2:]
-    grads_ref, rows_ref, cols_ref = refs[:3]
-    new_ref = refs[3] if update else None
+    qkv_ref, out_ref, rows_ref, cols_ref = refs[:4]
+    new_ref = refs[4] if update else None
     acc_ref, line_ref = refs[-2:]
+    features = acc_ref.shape[0]
+    rows = features // groups
     core = table_ref[0]
-    rows = owns[0].shape[1]
-    features = acc_ref.shape[0]
-    for m in range(count):
-        acc_ref[...] = jnp.zeros_like(acc_ref)
-
-        def column(w2, carry, m=m):
-            for j, source in enumerate((owns[m], fars[m])):
+    chunk = 32
+
+    def fill(grads_ref, source_of, n, start, stop, cols):
+        def step(c, cols):
+            first = pl.multiple_of(c * chunk, chunk)
+            total = jnp.zeros((chunk, LANES), F32)
+            grown = []
+            for index in range(2 * pairs):
+                w2, j = index // 2, index % 2
+                block = source_of(n, w2, j, first).astype(F32)
                 w = 2 * w2 + (core if j == 0 else 1 - core)
                 place = pl.multiple_of(w * LANES, LANES)
-                total = jnp.zeros((1, LANES), F32)
-                for n in range(groups):
-                    at = table_ref[1 + ((first + m) * groups + n) * pairs + w2]
-                    block = source[at].astype(F32)
-                    grads_ref[m, n * rows : (n + 1) * rows, pl.ds(place, LANES)] = block
-                    square = block * block
-                    total = total + jnp.sum(square, axis=0, keepdims=True)
-                    acc_ref[n * rows : (n + 1) * rows, :] += square
-                cols_ref[m, w] = total / features + STAT_EPS
-            return carry
-
-        lax.fori_loop(0, pairs, column, 0)
+                grads_ref[pl.ds(n * rows + first, chunk), pl.ds(place, LANES)] = block
+                square = block * block
+                total = total + square
+                grown.append(cols[index] + jnp.sum(square.reshape(-1, 8, LANES), axis=0))
+            acc_ref[pl.ds(n * rows + first, chunk), :] = total
+            return tuple(grown)
+
+        return lax.fori_loop(start // chunk, stop // chunk, step, cols)
+
+    def matrix(m, grads_ref, pieces):
+        cols = tuple(jnp.zeros((8, LANES), F32) for _ in range(2 * pairs))
+        for n in range(groups):
+            for chain, start, stop, shift, own, far in pieces:
+
+                def source_of(n, w2, j, first, chain=chain, shift=shift, own=own, far=far):
+                    at = table_ref[1 + (chain * groups + n) * pairs + w2]
+                    ref = own if j == 0 else far
+                    return ref[at, pl.ds(pl.multiple_of(first + shift, 16), chunk), :]
+
+                cols = fill(grads_ref, source_of, n, start, stop, cols)
+        for index in range(2 * pairs):
+            w = 2 * (index // 2) + (core if index % 2 == 0 else 1 - core)
+            total = jnp.sum(cols[index], axis=0, keepdims=True)
+            cols_ref[0, w] = total / features + STAT_EPS
         squares = acc_ref[...]
         sums = lax.dot_general(
             jnp.ones((8, LANES), F32), squares, NT,
             precision=lax.Precision.HIGHEST, preferred_element_type=F32,
         )
-        rows_ref[m] = sums / features + STAT_EPS
+        rows_ref[0] = sums / features + STAT_EPS
         if update:
             line = jnp.sum(squares, axis=1, keepdims=True) / features + STAT_EPS
             line_ref[...] = jnp.broadcast_to(line, line_ref.shape)
             mean = jnp.sum(line, axis=0, keepdims=True) / features
             my_rows = line_ref[pl.ds(pl.multiple_of(place_ref[0] * rows, rows), rows), :]
-            my_cols = cols_ref[m, place_ref[1]]
-            step = STEP_RATE * mine_ref[m] / jnp.sqrt(my_rows * my_cols / mean)
-            new_ref[m] = weight_ref[m] - step if subtract else step
-
-
-def finish_call(table, place, gathered, first, groups, features, mine, weights, subtract):
+            my_cols = cols_ref[0, place_ref[1]]
+            step = STEP_RATE * mine_ref[0] / jnp.sqrt(my_rows * my_cols / mean)
+            new_ref[0] = weight_ref[0] - step if m < 3 else step
+
+    owns, fars = (own_q, own_k, own_v), (far_q, far_k, far_v)
+    for m in range(4):
+
+        @pl.when(pl.program_id(0) == m)
+        def _(m=m):
+            if m < 3:
+                matrix(m, qkv_ref.at[0], [(m, 0, rows, 0, owns[m], fars[m])])
+            else:
+                pieces = [
+                    (i, cuts[i], cuts[i + 1], rows - cuts[i], owns[i], fars[i]) for i in range(3)
+                ]
+                matrix(m, out_ref, pieces)
+
+
+def finish_call(table, place, gathered, groups, features, mine, weights):
     pairs = features // (2 * LANES)
-    count = len(gathered)
     rows = features // groups
     owns = [g[0] for g in gathered]
     fars = [g[1] for g in gathered]
     update = mine is not None
     extra = [mine, weights] if update else []
+    block = pl.BlockSpec((1, rows, LANES), lambda m: (m, 0, 0))
     shapes = [
-        jax.ShapeDtypeStruct((count, features, features), F32),
-        jax.ShapeDtypeStruct((count, 8, features), F32),
-        jax.ShapeDtypeStruct((count, 2 * pairs, 1, LANES), F32),
+        jax.ShapeDtypeStruct((3, features, features), F32),
+        jax.ShapeDtypeStruct((features, features), F32),
+        jax.ShapeDtypeStruct((4, 8, features), F32),
+        jax.ShapeDtypeStruct((4, 2 * pairs, 1, LANES), F32),
+    ]
+    specs = [
+        pl.BlockSpec((1, features, features), lambda m: (jnp.minimum(m, 2), 0, 0)),
+        pl.BlockSpec((features, features), lambda m: (0, 0)),
+        pl.BlockSpec((1, 8, features), lambda m: (m, 0, 0)),
+        pl.BlockSpec((1, 2 * pairs, 1, LANES), lambda m: (m, 0, 0, 0)),
     ]
     if update:
-        shapes.append(jax.ShapeDtypeStruct((count, rows, LANES), F32))
+        shapes.append(jax.ShapeDtypeStruct((4, rows, LANES), F32))
+        specs.append(block)
+
     out = pl.pallas_call(
         functools.partial(
-            finish_body, groups=groups, pairs=pairs, count=count, first=first,
-            update=update, subtract=subtract,
+            finish_body, groups=groups, pairs=pairs, cuts=row_cuts(rows), update=update
         ),
-        in_specs=[smem()] * 2 + [vmem()] * (2 * count + len(extra)),
-        out_specs=[vmem()] * len(shapes),
+        grid=(4,),
+        in_specs=[smem()] * 2 + [vmem()] * 6 + [block] * len(extra),
+        out_specs=specs,
         out_shape=shapes,
         scratch_shapes=[pltpu.VMEM((features, LANES), F32)] * 2,
-        compiler_params=params(),
+        compiler_params=params(26),
         name="finish",
+        cost_estimate=cost(10),
     )(table, place, *owns, *fars, *extra)
-    stats = (out[0], out[1][:, 0], out[2].reshape(count, features))
-    return stats + (out[3] if update else None,)
+    stats = (out[0], out[1], out[2][:, 0], out[3].reshape(4, features))
+    return stats + (out[4] if update else None,)
 
 
 def on_device(
@@ -838,7 +935,7 @@
         core_entry, tables = my_core, slots
     else:
         core_entry = jnp.int32(0)
-        tables = [jnp.arange(groups * pairs, dtype=jnp.int32)] * 4
+        tables = [jnp.arange(groups * pairs, dtype=jnp.int32)] * 3
     table = jnp.concatenate(
         [jnp.reshape(core_entry, (1,)).astype(jnp.int32)] + [t.reshape(-1) for t in tables]
     )
@@ -848,28 +945,34 @@
         blocks = from_matrix(matrix, groups, pairs)
         return blocks.reshape((groups * pairs,) + blocks.shape[2:])
 
-    def as_halves(owns, fars, first):
+    def as_halves(owns, fars):
         if direct:
             return list(zip(owns, fars))
         out = []
-        for i, halves in enumerate(zip(owns, fars)):
-            both = as_pairs(as_matrix(*halves, slots[first + i], my_core))
+        for own, far, slot in zip(owns, fars, slots):
+            both = as_pairs(as_matrix(own, far, slot, my_core))
             out.append((both[:, 0], both[:, 1]))
         return out
 
-    def halves_of(keep, send, which):
+    def halves_of(keep, send, chain):
         if direct:
             return keep, send
+        rows = keep.shape[1]
         both = jnp.stack([keep, send.astype(F32)], axis=1).reshape(
-            groups, pairs, 2, features // groups, LANES
+            groups, pairs, 2, rows, LANES
         )
-        matrix = jnp.transpose(both, (0, 3, 1, 2, 4)).reshape(features, features)
+        matrix = jnp.transpose(both, (0, 3, 1, 2, 4)).reshape(groups * rows, features)
         parts = from_matrix(matrix, groups, half_wide)
         placed = jnp.zeros((groups * half_wide,) + parts.shape[2:], F32)
-        placed = placed.at[slots[which].reshape(-1)].set(parts.reshape(placed.shape))
+        placed = placed.at[slots[chain].reshape(-1)].set(parts.reshape(placed.shape))
         mine = jnp.where(my_core == 0, placed[:, 0], placed[:, 1])
         theirs = jnp.where(my_core == 0, placed[:, 1], placed[:, 0])
         return mine, theirs.astype(BF)
+
+    def split_rows(values, ends):
+        return [
+            lax.slice_in_dim(values, a, b, axis=1) for a, b in zip([0] + ends[:-1], ends)
+        ]
 
     narrow_hops = [("narrow", b) for b in range(groups.bit_length() - 1)]
     place_hops = [
@@ -883,6 +986,10 @@
     row_table = jnp.concatenate(
         [row_slots(hops, groups, places, split_parts) for hops in chains]
     )
+    back_hops = (chains[0][::-1], chains[0])
+    back_table = jnp.concatenate(
+        [row_slots(hops[::-1], groups, places, split_parts) for hops in back_hops]
+    )
     owner_slot = expert_ids % groups * places + expert_ids // groups
     row_ids = jnp.where(expert_slots >= 0, owner_slot * capacity + expert_slots, -1).T
 
@@ -890,7 +997,10 @@
         return rows.reshape(-1, rows.shape[-1])
 
     def sends(states, step):
-        return [send_step(state, hops[step]) for state, hops in zip(states, chains)]
+        return [row_send(state, hops[step]) for state, hops in zip(states, chains)]
+
+    def joins(states, gots):
+        return [row_join(state, got) for state, got in zip(states, gots)]
 
     def to_core(values):
         return [from_partner(value, core_hop) for value in values]
@@ -904,11 +1014,27 @@
     def homeward(rows):
         return rows.astype(BF).reshape(-1, 1, half_cap, rows.shape[-1])
 
-    def back_step(state, chain, step):
-        return return_step(state, chains[chain][hop_count - 1 - step])
-
-    def slots_first(state):
-        return state.reshape((-1,) + state.shape[2:])
+    def homeward_start(states):
+        return [(state, list(hops)) for state, hops in zip(states, chains)]
+
+    def backs_out(states, step):
+        gots = {}
+        for chain in range(2):
+            at = step - chain
+            if 0 <= at < hop_count:
+                gots[chain] = back_send(*states[chain], back_hops[chain][at])
+        return gots
+
+    def backs_join(states, gots, step):
+        return [
+            back_join(*state, back_hops[chain][step - chain], gots[chain])
+            if chain in gots
+            else state
+            for chain, state in enumerate(states)
+        ]
+
+    def slots_first(states):
+        return [state.reshape((-1,) + state.shape[2:]) for state, _ in states]
 
     router_tail = router.astype(BF).reshape(-1, col_count)
     tail_rows = router_tail.shape[0]
@@ -924,25 +1050,39 @@
     upstream_a, upstream_b = upstream_call(
         row_table, upstream, row_ids, expert_ids.T[::-1].astype(F32), experts, capacity
     )
-    qkv_chains = gather_chains(qkv_low, orders[:3])
-    qkv_far = to_core(qkv_chains)
-    out_chain = gather_chains(out_low[None], orders[3:])
-    out_gathered = (out_chain[0], from_partner(out_chain[0], core_hop))
-    qkv_parts = as_halves(qkv_chains, qkv_far, 0)
-    tails = [half[:, row_count : row_count + tail_rows] for half in out_gathered]
+    shared = shared_hops(orders)
+    stages = range(shared, len(orders[0]) - 1)
+    u_state = [upstream_a[None], upstream_b[None]]
+    cuts = row_cuts(row_count)
+    low_cuts = cuts[:3] + [out_low.shape[0]]
+    pieces, ends = [], []
+    for i in range(3):
+        pieces += [qkv_low[i], out_low[low_cuts[i] : low_cuts[i + 1]]]
+        ends.append(sum(piece.shape[0] for piece in pieces))
+    blocks = jnp.concatenate(pieces, axis=0)[None]
+    for hop in orders[0][:shared]:
+        blocks = grow(blocks, from_partner(blocks, hop))
+    u_state, blocks = together(u_state, blocks)
+    u_got = sends(u_state, 0)
+    dense = split_rows(blocks, ends)
+    for count, stage in enumerate(stages):
+        got = [from_partner(c, order[stage]) for c, order in zip(dense, orders)]
+        if count == 1:
+            u_got, got = together(u_got, got)
+            u_state = joins(u_state, u_got)
+            u_got = sends(u_state, 1)
+        dense = [grow(c, g) for c, g in zip(dense, got)]
+    dense_far = to_core(dense)
+    weight_parts = as_halves(dense, dense_far)
+    tails = [half[:, -(out_low.shape[0] - row_count) :][:, :tail_rows] for half in (dense[2], dense_far[2])]
     full_router = jnp.transpose(
-        as_matrix(*tails, slots[3], my_core)
+        as_matrix(*tails, slots[2], my_core)
         .reshape(groups, tail_rows, wide_count, col_count)
         .transpose(0, 2, 1, 3)
         .reshape(groups, wide_count, row_count, router.shape[1]),
         (0, 2, 1, 3),
     ).reshape(features, experts)
     router_wide = jnp.pad(full_router, ((0, 0), (0, -experts % LANES)))
-    out_halves = out_gathered
-    if not direct:
-        out_halves = [half[:, :row_count] for half in out_gathered]
-        both = as_pairs(as_matrix(*out_halves, slots[3], my_core))
-        out_halves = [both[:, 0], both[:, 1]]
     gate_low = gate_weight[0, 0].T.astype(BF)
     up_low = up_weight[0, 0].T.astype(BF)
     down_low = down_weight[0, 0].astype(BF)
@@ -951,34 +1091,37 @@
         == jnp.arange(bucket_count, dtype=jnp.int32)[None, :]
     ).astype(F32)
     bias_table = jnp.dot(table_hot, rel_bias, precision=lax.Precision.HIGHEST).T
-    (upstream_a, upstream_b), qkv_chains = together((upstream_a, upstream_b), qkv_chains)
-    u_state = sends([upstream_a[None], upstream_b[None]], 0)
     normed_in, heads, probs, attended = attend_call(
-        table, tokens, attn_gain, bias_table, qkv_parts, groups, head_dim
-    )
-    u_state, attended = together(u_state, attended)
-    u_state = sends(u_state, 1)
+        table, tokens, attn_gain, bias_table, weight_parts, groups, head_dim
+    )
+    u_got, attended = together(u_got, attended)
+    for step in range(2, hop_count):
+        u_state = joins(u_state, u_got)
+        u_got = sends(u_state, step)
     hidden_x1, moe_input, send_a, send_b = post_call(
-        table, row_table, tokens, attended, out_halves, moe_gain, row_ids, groups, experts,
+        table, row_table, tokens, attended, weight_parts, moe_gain, row_ids, groups, experts,
         capacity,
     )
-    u_state, send_a, send_b = together(u_state, send_a, send_b)
+    u_got, send_a, send_b = together(u_got, send_a, send_b)
+    u_own = [flat(state) for state in joins(u_state, u_got)]
+    u_core, u_part = to_core(u_own), to_part(u_own[:1])
     x_state = [send_a[None], send_b[None]]
     for step in range(hop_count):
-        x_state = sends(x_state, step)
-        if step + 2 < hop_count:
-            u_state = sends(u_state, step + 2)
-        elif step + 2 == hop_count:
-            u_own = [flat(state) for state in u_state]
-            u_core, u_part = to_core(u_own), to_part(u_own)
-            x_state, u_core = together(x_state, u_core)
-            continue
-        if step + 1 < hop_count:
-            x_state, u_state = together(x_state, u_state)
-    x_state, u_part = together(x_state, u_part)
+        x_got = sends(x_state, step)
+        if step == 0:
+            x_got, u_core, u_part[0], router_wide = together(
+                x_got, u_core, u_part[0], router_wide
+            )
+        else:
+            x_got = together(*x_got)
+        x_state = joins(x_state, x_got)
+    late_parts, _ = together(weight_parts, send_a)
+    projection_parts = [tuple(half[:, row_count:] for half in part) for part in late_parts]
+    projection_parts, x_state = together(projection_parts, x_state)
     x_own = [flat(state) for state in x_state]
     x_core, x_part = to_core(x_own), to_part(x_own)
-    u_part_core = to_core(u_part)
+    late_u, _ = together(u_own[1], x_own)
+    u_part.append(from_partner(late_u, part_hop))
 
     my_expert = (my_narrow + groups * (my_wide // split_parts)).reshape(1).astype(jnp.int32)
     row_total = 8 * x_own[0].shape[0]
@@ -989,59 +1132,67 @@
         )
 
     y_near, dx_near, kept = run_expert(x_own + x_core, u_own + u_core, 0, None)
-    x_part, u_part_core, dx_near = together(x_part, u_part_core, dx_near)
-    x_part_core = to_core(x_part)
+    x_part[0], u_part[0], dx_near = together(x_part[0], u_part[0], dx_near)
     dx_near_got = to_core(dx_near[2:])
-    y_far, parts_back, far_sums = [], [], []
+    y_far, parts_back = [], []
     for chain in range(2):
-        xs = [x_part[chain], x_part_core[chain]]
-        us = [u_part[chain], u_part_core[chain]]
         if chain:
-            xs, far_sums = together(xs, far_sums)
+            x_part[1], u_part[1], y_far = together(x_part[1], u_part[1], y_far)
+        xs = [x_part[chain], from_partner(x_part[chain], core_hop)]
+        us = [u_part[chain], from_partner(u_part[chain], core_hop)]
         y_two, dx_two, kept = run_expert(xs, us, 4 + 2 * chain, kept)
+        if chain:
+            y_two, dx_two, kept, parts_back[0] = together(y_two, dx_two, kept, parts_back[0])
         y_far.append(y_two)
-        far_sums.append(add(dx_two[0], from_partner(dx_two[1], core_hop)).astype(BF))
-        parts_back.append(from_partner(far_sums[chain], part_hop))
-    near_sums = [add(mine, got) for mine, got in zip(dx_near[:2], dx_near_got)]
-    near_sums, far_sums[1], kept = together(near_sums, far_sums[1], kept)
+        far_got = from_partner(dx_two[1], core_hop)
+        far_sum = add(dx_two[0], far_got).astype(BF)
+        if not chain:
+            kept, far_sum = together(kept, far_sum)
+        parts_back.append(from_partner(far_sum, part_hop))
+    kept, far_sum = together(kept, far_sum)
     y_near_got = to_core(y_near[2:])
     y_far_got = to_core([two[1] for two in y_far])
 
+    def home_sum(chain, part):
+        near = add(dx_near[chain], dx_near_got[chain])
+        return homeward(near + part.astype(F32))
+
     x_all, dy_all, hidden_all, dgate_all, dup_all = kept
-    backs = [homeward(add(near_sums[0], parts_back[0])), None]
+    states = homeward_start([home_sum(0, parts_back[0]), None])
     for step in range(hop_count + 1):
-        if step < hop_count:
-            backs[0] = back_step(backs[0], 0, step)
-        if step == 1:
-            backs[1] = homeward(add(near_sums[1], parts_back[1]))
-        if step >= 1:
-            backs[1] = back_step(backs[1], 1, step - 1)
+        gots = backs_out(states, step)
         if step == 0:
             gate_local = expert_grad_call(dgate_all, x_all)
             up_local = expert_grad_call(dup_all, x_all)
-            backs[0], parts_back[1], gate_local, up_local, hidden_all = together(
-                backs[0], parts_back[1], gate_local, up_local, hidden_all
+            gots, part_b, gate_local, up_local, hidden_all = together(
+                gots, parts_back[1], gate_local, up_local, hidden_all
             )
+            states[1] = (home_sum(1, part_b), list(chains[1]))
         elif step == 1:
             down_local = expert_grad_call(hidden_all, dy_all)
-            y_sums = [add(mine, got) for mine, got in zip(y_near[:2], y_near_got)]
+            y_sums = [add(mine, got).astype(BF) for mine, got in zip(y_near[:2], y_near_got)]
             y_far_sums = [
                 add(two[0], got).astype(BF) for two, got in zip(y_far, y_far_got)
             ]
-            y_sums = [value.astype(BF) for value in y_sums]
-            backs, down_local, y_sums, y_far_sums = together(
-                backs, down_local, y_sums, y_far_sums
+            gots, down_local, y_sums, y_far_sums = together(
+                gots, down_local, y_sums, y_far_sums
             )
+            y_part_got = to_part(y_far_sums[:1])
         elif step == 2:
-            y_part_got = to_part(y_far_sums)
             squares = [g * g for g in (gate_local, up_local, down_local)]
             local_sums = jnp.stack([jnp.sum(q, axis=0) for q in squares], axis=0)
             part_stats = jnp.stack([jnp.mean(q, axis=1) for q in squares], axis=0) + STAT_EPS
-            wide_sums = cube_sum(local_sums, [core_hop])
-            backs, wide_sums = together(backs, wide_sums)
+            sums_got = from_partner(local_sums, core_hop)
+            gots, local_sums, y_part_got, sums_got = together(
+                gots, local_sums, y_part_got, sums_got
+            )
         elif step == 3:
-            wide_sums = cube_sum(wide_sums, [part_hop])
-            wide_stats = wide_sums / (part_width * split_parts) + STAT_EPS
+            sums_got, y_far_sums = together(sums_got, y_far_sums)
+            local_sums = local_sums + sums_got
+            sums_got = from_partner(local_sums, part_hop)
+            sums_got, y_far_sums = together(sums_got, y_far_sums)
+            y_part_got = y_part_got + to_part(y_far_sums[1:])
+            wide_stats = (local_sums + sums_got) / (part_width * split_parts) + STAT_EPS
             gate_new = factored(
                 gate_weight[0, 0].T, gate_local, part_stats[0], wide_stats[0],
                 jnp.mean(wide_stats[0]),
@@ -1054,145 +1205,179 @@
                 down_weight[0, 0], down_local, part_stats[2], wide_stats[2],
                 jnp.mean(wide_stats[2]),
             )
-            backs, gate_new, up_new, down_new = together(backs, gate_new, up_new, down_new)
-    inputs_back = [slots_first(state) for state in backs]
+            gots, gate_new, up_new, down_new, wide_stats = together(
+                gots, gate_new, up_new, down_new, wide_stats
+            )
+        else:
+            gots = together(gots)[0]
+        states = backs_join(states, gots, step)
+    inputs_back = slots_first(states)
+    y_home = homeward(add(y_sums[0], y_part_got[0]))
+    inputs_back, y_home = together(inputs_back, y_home)
+    y_states = homeward_start([y_home, None])
+    y_gots = backs_out(y_states, 0)
 
     x1_grad, gates, moe_gain_local, router_local, out_keep, out_send, attended_grad = mid_call(
-        table, row_table, hidden_x1, moe_gain, moe_input, upstream, inputs_back, row_ids,
-        expert_ids, router_wide, attended, out_halves, groups, experts, capacity,
-    )
-    y_part_got, attended_grad, out_send = together(y_part_got, attended_grad, out_send)
-    y_backs = [homeward(add(near, got)) for near, got in zip(y_sums, y_part_got)]
-    y_backs = [back_step(state, chain, 0) for chain, state in enumerate(y_backs)]
-    out_keep, out_send = halves_of(out_keep, out_send, 3)
-    out_half = core_sum(out_keep, out_send, orders[3])
-
-    keeps, qkv_sends, dheads, diag = attend_back_call(
-        table, normed_in, heads, probs, attended_grad, groups, head_dim
-    )
-    y_backs, out_half, qkv_sends = together(y_backs, out_half, qkv_sends)
-    if direct:
-        summed = core_sum(keeps, qkv_sends, orders[0])
-        summed = [summed[m] for m in range(3)]
-    else:
-        summed = [
-            core_sum(*halves_of(keeps[m], qkv_sends[m], m), orders[m]) for m in range(3)
-        ]
-    summed = summed + [out_half]
-    y_backs = [back_step(state, chain, 1) for chain, state in enumerate(y_backs)]
-    summed, y_backs = together(summed, y_backs)
-
-    shared = shared_hops(orders)
-    stages = range(shared, len(orders[0]) - 1)
-    y_step = 2
+        table, back_table, hidden_x1, moe_gain, moe_input, upstream, inputs_back, row_ids,
+        expert_ids, router_wide, attended, projection_parts, groups, experts, capacity,
+    )
+    y_part_got, y_gots, attended_grad, out_send = together(
+        y_part_got, y_gots, attended_grad, out_send
+    )
+    y_states = backs_join(y_states, y_gots, 0)
+    y_states[1] = (homeward(add(y_sums[1], y_part_got[1])), list(chains[1]))
+    y_gots = backs_out(y_states, 1)
+
+    *grads, dheads, diag = attend_back_call(
+        table, normed_in, heads, probs, attended_grad, out_keep, out_send, groups, head_dim
+    )
+    halves = [halves_of(grads[i], grads[3 + i], i) for i in range(3)]
+    addends = [[keep, from_partner(send, core_hop)] for keep, send in halves]
+    ends, size = [], 0
+    for value, _ in addends:
+        size += value.shape[1]
+        ends.append(size)
+    y_gots, addends = together(y_gots, addends)
+    y_step = 1
+    router_local, moe_gain_local, dheads, x1_grad, diag, _ = together(
+        router_local, moe_gain_local, dheads, x1_grad, diag, addends
+    )
+
+    def halve(values, hop):
+        half = values[0].shape[0] // 2
+        send = sum(value[half:].astype(F32) for value in values).astype(BF)
+        return [value[:half] for value in values], from_partner(send, hop)
+
+    def more_outputs():
+        joined = backs_join(y_states, y_gots, y_step)
+        return joined, backs_out(joined, y_step + 1), y_step + 1
+
+    small_hops = list(orders[0])
+    y_states, y_gots, y_step = more_outputs()
     for count, stage in enumerate(stages[::-1]):
-        summed = [halve(total, order[stage]) for total, order in zip(summed, orders)]
-        if y_step < hop_count:
-            y_backs = [back_step(state, c, y_step) for c, state in enumerate(y_backs)]
-            y_step += 1
+        halved = [halve(values, order[stage]) for values, order in zip(addends, orders)]
+        gots = [got for _, got in halved]
         if count == 0:
             tokens_grad, attn_gain_local = tokens_back_call(
-                table, tokens, attn_gain, x1_grad, dheads, qkv_parts, groups
+                table, tokens, attn_gain, x1_grad, dheads, weight_parts, groups
             )
             tail = jnp.pad(diag, ((0, 0), (0, 0), (0, 8)))
             line = sum(tail[:, i, i : i + 2 * length] for i in range(8))
-            bias_local = jnp.dot(line, table_hot, precision=lax.Precision.HIGHEST).T
+            bias_local = jnp.dot(line, table_hot, precision=lax.Precision.HIGHEST)
             small = jnp.concatenate(
                 [
                     attn_gain_local.reshape(-1),
                     moe_gain_local.reshape(-1),
                     bias_local.reshape(-1),
-                    router_local[:, :experts].reshape(-1),
+                    router_local[:experts].reshape(-1),
                 ]
             ).reshape(-1, LANES)
-        summed, y_backs, small = together(summed, y_backs, small)
-    while y_step < hop_count:
-        y_backs = [back_step(state, c, y_step) for c, state in enumerate(y_backs)]
-        y_step += 1
+            gots, small, y_gots = together(gots, small, y_gots)
+            y_states, y_gots, y_step = more_outputs()
+        else:
+            small_got = from_partner(small, small_hops.pop(0))
+            if y_gots:
+                gots, small_got, y_gots = together(gots, small_got, y_gots)
+                y_states, y_gots, y_step = more_outputs()
+            else:
+                gots, small_got = together(gots, small_got)
+            small = small + small_got
+        addends = [kept + [got] for (kept, _), got in zip(halved, gots)]
+    summed = [sum(value.astype(F32) for value in values) for values in addends]
+    while y_gots:
+        y_states, y_gots, y_step = more_outputs()
     block_out = block_out_call(
-        row_table, hidden_x1, gates, [slots_first(state) for state in y_backs], row_ids,
-        experts, capacity,
-    )
-    small_hops = list(orders[0])
-
-    def small_step(value):
-        return cube_sum(value, [small_hops.pop(0)]) if small_hops else value
-
-    total = jnp.stack(summed)
+        back_table, hidden_x1, gates, slots_first(y_states), row_ids, experts, capacity
+    )
+
+    def small_beside(value, others):
+        if not small_hops:
+            return value, together(*others)
+        got = from_partner(value, small_hops.pop(0))
+        out = together(got, *others)
+        return value + out[0], out[1:]
+
+    total = jnp.concatenate(summed, axis=1)
     for hop in orders[0][:shared][::-1]:
-        total = halve(total, hop, 1)
-        small = small_step(small)
-        total, small, block_out = together(total, small, block_out)
-    dense_mine = total[:, 0]
+        got = halve_send(total, hop)
+        small, (got, block_out) = small_beside(small, (got, block_out))
+        total = halve_add(total, got)
     blocks = total.astype(BF)
     for hop in orders[0][:shared]:
-        blocks = grow(blocks, hop, 1)
-        small = small_step(small)
-        blocks, small = together(blocks, small)
-    dense = [blocks[i] for i in range(4)]
-    for stage in stages:
-        dense = [grow(chain, order[stage]) for chain, order in zip(dense, orders)]
-        small = small_step(small)
-        dense, small = together(dense, small)
-    small = cube_sum(small, small_hops).reshape(-1)
-    dense_parts = as_halves(dense, to_core(dense), 0)
-    gain_a_total = small[:features]
-    gain_m_total = small[features : 2 * features]
-    bias_size = bucket_count * head_count
-    bias_total = small[2 * features : 2 * features + bias_size].reshape(bucket_count, head_count)
-    router_total = small[2 * features + bias_size :].reshape(features, experts)
-
-    def finish(parts, first, mine, weights, subtract):
-        mine_in = mine if direct else None
-        grads, rows, cols, new = finish_call(
-            table, place, parts, first, groups, features, mine_in, weights, subtract
-        )
-        if not direct:
-            rows_mine = lax.dynamic_slice_in_dim(rows, my_narrow * row_count, row_count, 1)
-            cols_mine = lax.dynamic_slice_in_dim(cols, my_wide * col_count, col_count, 1)
-            step = adafactor_step(mine, rows_mine, cols_mine, jnp.mean(rows, axis=1))
-            new = weights - step if subtract else step
-        return grads, rows, cols, new
-
-    out_total, out_rows, out_cols, out_step = finish(
-        dense_parts[3:], 3, dense_mine[3:], out_weight[None], False
-    )
-    qkv_total, qkv_rows, qkv_cols, qkv_new = finish(
-        dense_parts[:3], 0, dense_mine[:3], qkv_weights, True
-    )
-    qkv_stats = jnp.stack([qkv_rows, qkv_cols], axis=0)
-    out_stats = jnp.concatenate([out_rows, out_cols], axis=0)
-    router_sq = router_total * router_total
-    router_rows = jnp.mean(router_sq, axis=1) + STAT_EPS
-    router_cols = jnp.mean(router_sq, axis=0) + STAT_EPS
-    router_row_count, router_col_count = router.shape
-    router_row_first = my_narrow * router_row_count
-    router_col_first = my_wide * router_col_count
-    router_block = lax.dynamic_slice(
-        router_total, (router_row_first, router_col_first), (router_row_count, router_col_count)
-    )
-    router_new = factored(
-        router,
-        router_block,
-        lax.dynamic_slice_in_dim(router_rows, router_row_first, router_row_count, 0),
-        lax.dynamic_slice_in_dim(router_cols, router_col_first, router_col_count, 0),
-        jnp.mean(router_rows),
-    )
+        got = from_partner(blocks, hop)
+        small, (got, total) = small_beside(small, (got, total))
+        blocks = grow(blocks, got)
+    pieces = split_rows(total, ends)
+    dense_mine = jnp.concatenate(
+        [piece[:, :row_count] for piece in pieces]
+        + [jnp.concatenate([piece[:, row_count:] for piece in pieces], axis=1)],
+        axis=0,
+    )
+    dense_weights = jnp.concatenate([qkv_weights, out_weight[None]], axis=0)
+    dense = split_rows(blocks, ends)
+    router_size = features * experts
+    for count, stage in enumerate(stages):
+        gots = [from_partner(chain, order[stage]) for chain, order in zip(dense, orders)]
+        if count == 0:
+            small, (gots,) = small_beside(small, (gots,))
+            small, small_hops = cube_sum(small, small_hops), []
+        elif count == 1:
+            small, (gots, dense_mine, dense_weights) = small_beside(
+                small, (gots, dense_mine, dense_weights)
+            )
+        else:
+            gots, router_out = together(gots, router_out)
+        if count == 0:
+            router_total = small.reshape(-1)[-router_size:].reshape(experts, features)
+            router_sq = router_total * router_total
+            router_rows = jnp.mean(router_sq, axis=0) + STAT_EPS
+            router_cols = jnp.mean(router_sq, axis=1) + STAT_EPS
+            rows_first, cols_first = my_narrow * router.shape[0], my_wide * router.shape[1]
+            router_new = factored(
+                router.T,
+                lax.dynamic_slice(router_total, (cols_first, rows_first), router.T.shape),
+                lax.dynamic_slice_in_dim(router_cols, cols_first, router.shape[1], 0),
+                lax.dynamic_slice_in_dim(router_rows, rows_first, router.shape[0], 0),
+                jnp.mean(router_rows),
+            )
+            small_flat = small.reshape(-1)
+            router_out = (
+                small_flat[:features],
+                small_flat[features : 2 * features],
+                small_flat[2 * features : -router_size].reshape(head_count, bucket_count),
+                router_total, router_new, router_rows, router_cols,
+            )
+        dense = [grow(chain, got) for chain, got in zip(dense, gots)]
+    gain_a_total, gain_m_total, bias_total, router_total, router_new, router_rows, router_cols = (
+        router_out
+    )
+    dense_parts = as_halves(dense, to_core(dense))
+    qkv_total, out_total, rows, cols, dense_new = finish_call(
+        table, place, dense_parts, groups, features, dense_mine if direct else None,
+        dense_weights,
+    )
+    if not direct:
+        rows_mine = lax.dynamic_slice_in_dim(rows, my_narrow * row_count, row_count, 1)
+        cols_mine = lax.dynamic_slice_in_dim(cols, my_wide * col_count, col_count, 1)
+        step = adafactor_step(dense_mine, rows_mine, cols_mine, jnp.mean(rows, axis=1))
+        dense_new = jnp.concatenate([qkv_weights - step[:3], step[3:]], axis=0)
+    qkv_stats = jnp.stack([rows[:3], cols[:3]], axis=0)
+    out_stats = jnp.concatenate([rows[3:], cols[3:]], axis=0)
     return (
         block_out,
         tokens_grad,
         gain_a_total,
         qkv_total,
-        out_total[0],
-        bias_total,
+        out_total,
+        bias_total.T,
         gain_m_total,
-        router_total,
+        router_total.T,
         gate_local.T[None, None],
         up_local.T[None, None],
         down_local[None, None],
-        qkv_new,
-        out_step[0],
-        router_new,
+        dense_new[:3],
+        dense_new[3],
+        router_new.T,
         gate_new.T[None, None],
         up_new.T[None, None],
         down_new[None, None],

time: 604 us -> 529 us (0.88)
  Pallas kernels: 165 us -> 123 us
  waiting for transfers between devices: 230 us -> 196 us
  local copies, waits for them, and re-layouts: 41.3 us -> 51.7 us
  starting transfers between devices: 87.3 us -> 80.2 us
    ppermute x105 -> x94, waiting for transfers between devices: 230 us -> 196 us  [from_partner(): return lax.ppermute(value, axis, pairs)]
    unnamed x148 -> x250, local copies, waits for them, and re-layouts: 13.3 us -> 28.2 us
    concatenate x39 -> x32, other arithmetic: 9.06 us -> 21.3 us  [the longest x21 15.8 us: grow(): return jnp.concatenate([blocks, got], axis=axis)]
    ppermute x105 -> x94, starting transfers between devices: 87.3 us -> 80.2 us  [from_partner(): return lax.ppermute(value, axis, pairs)]
    pallas_call x3, Pallas kernels: 27.2 us -> 20.9 us  [expert_grad_call(): pl.pallas_call(expert_grad_body, grid=(features // size,), in_specs=[pl.B...]
    pallas_call x1, Pallas kernels: 17.2 us -> 11 us  [attend_back_call(): pl.pallas_call(body, in_specs=[smem()] + [vmem()] * 6, out_specs=[vmem()]...]
    another operation x11 -> x13, other arithmetic: 9.61 us -> 3.48 us  [the longest x12 2.85 us: back_join(): jnp.stack([kept, got], axis=1).reshape((got.shape[0], -1) + state.shape[2:])]
    pallas_call x2 -> x1, Pallas kernels: 16.8 us -> 10.7 us  [finish_call(): pl.pallas_call(functools.partial(finish_body, groups=groups, pairs=pairs,...]
  transfers between devices with their start and end apart: 105 -> 94, of which waited for: 49 -> 41; matrix products, arithmetic and copies ran while one was open for 13% -> 11% of each run, Pallas kernels for 26% -> 19%
where the time goes in v3:
time: 529 us; the launch traced here: 521 us
  waiting for transfers between devices  196 us (37%)
  Pallas kernels  123 us (23%)
  starting transfers between devices  80.2 us (15%)
  other arithmetic  63.4 us (12%)
  local copies, waits for them, and re-layouts  51.7 us (10%)
  between operations  5.59 us (1%)
    ppermute x94, waiting for transfers between devices, from_partner(): return lax.ppermute(value, axis, pairs)  196 us
    ppermute x94, starting transfers between devices, from_partner(): return lax.ppermute(value, axis, pairs)  80.2 us
    pallas_call x3, Pallas kernels, expert_call(): pl.pallas_call(functools.partial(expert_body, count=count), grid_spec=plt...  46.5 us
    unnamed x250, local copies, waits for them, and re-layouts  28.2 us
    pallas_call x3, Pallas kernels, expert_grad_call(): pl.pallas_call(expert_grad_body, grid=(features // size,), in_specs=[pl.B...  20.9 us
    concatenate x21, other arithmetic, grow(): return jnp.concatenate([blocks, got], axis=axis)  15.8 us
    pallas_call x1, Pallas kernels, attend_call(): pl.pallas_call(body, in_specs=[smem()] + [vmem()] * 9, out_specs=[vmem()]...  11.1 us
    pallas_call x1, Pallas kernels, attend_back_call(): pl.pallas_call(body, in_specs=[smem()] + [vmem()] * 6, out_specs=[vmem()]...  11 us
  transfers between devices with their start and end apart: 94, of which 41 were waited for; matrix products, arithmetic and copies ran while one was open for 11% of the time, Pallas kernels for 19%

profile of v3, /device:TPU:0, one launch (start us, length us, event | category | flops | bytes accessed | tf_op | source)
XLA Modules:
  0.0 521.0 jit_solution(17864800593185644202)
XLA Ops:
  3.6 4.1 collective-permute-start
  11.6 8.2 %collective-permute-done = bf16[1,1040,128]{2,1,0:T(8,128)(2,1)S(1)} collective-permute-done((bf16[1,1040,128]{2,1,0:T(8,128)(2,1)S(1)}, bf16[1,1040,128]{2,1,0:T(8,128)(2,1)S(1)}, u32[]{:S(2)}, u32[]{:S(2)}) %collective-permute-start) | collective-permute-done | bytes 266272 | tf_op jit(solution)/shard_map/ppermute | solution.py:31
  32.0 4.9 collective-permute-done.2
  36.9 8.0 %collective-permute-done.3 = bf16[1,4,40,1152]{3,2,1,0:T(8,128)(2,1)S(1)} collective-permute-done((bf16[1,4,40,1152]{3,2,1,0:T(8,128)(2,1)S(1)}, bf16[1,4,40,1152]{3,2,1,0:T(8,128)(2,1)S(1)}, u32[]{:S(2)}, u32[]{:S(2)}) %collective-permute-start.3) | collective-permute-done | bytes 368672 | tf_op jit(solution)/shard_map/ppermute | solution.py:31
  51.4 11.7 %collective-permute-done.9 = bf16[8,352,128]{2,1,0:T(8,128)(2,1)} collective-permute-done((bf16[8,352,128]{2,1,0:T(8,128)(2,1)S(1)}, bf16[8,352,128]{2,1,0:T(8,128)(2,1)}, u32[]{:S(2)}, u32[]{:S(2)}) %collective-permute-start.9) | collective-permute-done | bytes 720928 | tf_op jit(solution)/shard_map/ppermute | solution.py:31
  71.8 11.1 %attend.1 = (bf16[256,1024]{1,0:T(8,128)(2,1)S(1)}, bf16[3,8,256,128]{3,2,1,0:T(8,128)(2,1)S(1)}, f32[16,256,256]{2,1,0:T(8,128)S(1)}, bf16[8,256,128]{2,1,0:T(8,128)(2,1)S(1)}) custom-call(s32[49]{0:T(128)S(1)} %pad_add_fusion.1.table_ref, bf16[256,1024]{1,0:T(8,128)(2,1)S(1)} %copy-done.31, f32[1,1024]{1,0:T(1,128)S(1)} %bitcast.279, ...), custom_call_target="tpu_custom_call" | custom-call | flops 18447998976 | bytes 59040000 | tf_op jit(solution)/shard_map/attend/pallas_call | solution.py:253
  93.5 6.2 %collective-permute-done.18 = bf16[4,1,40,1152]{3,2,0,1:T(8,128)(2,1)S(1)} collective-permute-done((bf16[4,1,40,1152]{3,2,0,1:T(8,128)(2,1)S(1)}, bf16[4,1,40,1152]{3,2,0,1:T(8,128)(2,1)S(1)}, u32[]{:S(2)}, u32[]{:S(2)}) %collective-permute-start.18) | collective-permute-done | bytes 368672 | tf_op jit(solution)/shard_map/ppermute | solution.py:31
  110.7 13.1 %collective-permute-done.20 = bf16[1,4,40,1024]{3,2,1,0:T(8,128)(2,1)} collective-permute-done((bf16[1,4,40,1024]{3,2,1,0:T(8,128)(2,1)}, bf16[1,4,40,1024]{3,2,1,0:T(8,128)(2,1)}, u32[]{:S(2)}, u32[]{:S(2)}) %collective-permute-start.20) | collective-permute-done | bytes 327712 | tf_op jit(solution)/shard_map/ppermute | solution.py:31
  130.2 12.2 %collective-permute-done.24 = bf16[2,2,40,1024]{3,2,0,1:T(8,128)(2,1)S(1)} collective-permute-done((bf16[2,2,40,1024]{3,2,0,1:T(8,128)(2,1)S(1)}, bf16[2,2,40,1024]{3,2,0,1:T(8,128)(2,1)S(1)}, u32[]{:S(2)}, u32[]{:S(2)}) %collective-permute-start.24) | collective-permute-done | bytes 327712 | tf_op jit(solution)/shard_map/ppermute | solution.py:31
  160.5 22.9 %expert.3 = (bf16[320,1024]{1,0:T(8,128)(2,1)S(1)}, bf16[320,1024]{1,0:T(8,128)(2,1)S(1)}, bf16[320,1024]{1,0:T(8,128)(2,1)}, bf16[320,1024]{1,0:T(8,128)(2,1)},...) custom-call(s32[1]{0:T(128)} %bitcast.61.expert_ref, ...), custom_call_target="tpu_custom_call" | custom-call | flops 27672000512 | bytes 88560000 | tf_op jit(solution)/shard_map/expert/pallas_call | solution.py:731
  187.1 12.0 %expert.4 = (bf16[320,1024]{1,0:T(8,128)(2,1)S(1)}, bf16[320,1024]{1,0:T(8,128)(2,1)}, bf16[320,1152]{1,0:T(8,128)(2,1)S(1)}, bf16[320,1152]{1,0:T(8,128)(2,1)S(...) custom-call(s32[1]{0:T(128)} %bitcast.61.expert_ref, ...), custom_call_target="tpu_custom_call", output_to_operand_aliasing={{4}: (9, {}), {5}: (10, {}), {6}: (11, {}), {7}: (12, {}), ... | custom-call | flops 13836000256 | bytes 44280000 | tf_op jit(solution)/shard_map/expert/pallas_call | solution.py:731
  201.5 15.3 %collective-permute-done.33.refs_2_ = bf16[320,1152]{1,0:T(8,128)(2,1)S(1)} collective-permute-done((bf16[320,1152]{1,0:T(8,128)(2,1)}, bf16[320,1152]{1,0:T(8,128)(2,1)S(1)}, u32[]{:S(2)}, u32[]{:S(2)}) %collective-permute-start.33) | collective-permute-done | bytes 737312 | tf_op jit(solution)/shard_map/ppermute | solution.py:31
  227.1 11.7 %expert.5 = (bf16[320,1024]{1,0:T(8,128)(2,1)S(1)}, bf16[320,1024]{1,0:T(8,128)(2,1)S(1)}, bf16[320,1152]{1,0:T(8,128)(2,1)S(1)}, bf16[320,1152]{1,0:T(8,128)(2,...) custom-call(s32[1]{0:T(128)} %bitcast.61.expert_ref, ...), custom_call_target="tpu_custom_call", output_to_operand_aliasing={{4}: (9, {}), {5}: (10, {}), {6}: (11, {}), {7}: (12, {}), ... | custom-call | flops 13836000256 | bytes 44280000 | tf_op jit(solution)/shard_map/expert/pallas_call | solution.py:731
  238.8 5.2 %collective-permute-done.39 = bf16[320,1152]{1,0:T(8,128)(2,1)S(1)} collective-permute-done((bf16[320,1152]{1,0:T(8,128)(2,1)S(1)}, bf16[320,1152]{1,0:T(8,128)(2,1)S(1)}, u32[]{:S(2)}, u32[]{:S(2)}) %collective-permute-start.39) | collective-permute-done | bytes 737312 | tf_op jit(solution)/shard_map/ppermute | solution.py:31
  251.5 6.9 %expert_grad.3 = f32[704,1024]{1,0:T(8,128)} custom-call(bf16[2560,704]{1,0:T(8,128)(2,1)S(1)} %copy-done.46, bf16[2560,1024]{1,0:T(8,128)(2,1)S(1)} %copy-done.44), custom_call_target="tpu_custom_call" | custom-call | flops 10376999936 | bytes 33210000 | tf_op jit(solution)/shard_map/expert_grad/pallas_call | solution.py:763
  258.4 6.9 %expert_grad.4 = f32[704,1024]{1,0:T(8,128)} custom-call(bf16[2560,704]{1,0:T(8,128)(2,1)S(1)} %copy-done.47, bf16[2560,1024]{1,0:T(8,128)(2,1)S(1)} %copy-done.44), custom_call_target="tpu_custom_call" | custom-call | flops 10376999936 | bytes 33210000 | tf_op jit(solution)/shard_map/expert_grad/pallas_call | solution.py:763
  272.5 7.1 %expert_grad.5 = f32[704,1024]{1,0:T(8,128)} custom-call(bf16[2560,704]{1,0:T(8,128)(2,1)S(1)} %copy-done.45, bf16[2560,1024]{1,0:T(8,128)(2,1)S(1)} %bitcast.282), custom_call_target="tpu_custom_call" | custom-call | flops 10376999936 | bytes 33210000 | tf_op jit(solution)/shard_map/expert_grad/pallas_call | solution.py:763
  280.0 8.7 %collective-permute-done.43 = bf16[2,2,40,1152]{3,2,1,0:T(8,128)(2,1)S(1)} collective-permute-done((bf16[2,2,40,1152]{3,2,1,0:T(8,128)(2,1)S(1)}, bf16[2,2,40,1152]{3,2,1,0:T(8,128)(2,1)S(1)}, u32[]{:S(2)}, u32[]{:S(2)}) %collective-permute-start.43) | collective-permute-done | bytes 368672 | tf_op jit(solution)/shard_map/ppermute | solution.py:31
  295.8 15.1 %collective-permute-done.51 = bf16[2,2,40,1152]{3,2,1,0:T(8,128)(2,1)S(1)} collective-permute-done((bf16[2,2,40,1152]{3,2,1,0:T(8,128)(2,1)S(1)}, bf16[2,2,40,1152]{3,2,1,0:T(8,128)(2,1)S(1)}, u32[]{:S(2)}, u32[]{:S(2)}) %collective-permute-start.51) | collective-permute-done | bytes 368672 | tf_op jit(solution)/shard_map/ppermute | solution.py:31
  321.2 5.1 bitcast_subtract_fusion
  334.8 6.0 %mid.1 = (f32[256,1024]{1,0:T(8,128)S(1)}, f32[256,128]{1,0:T(8,128)S(1)}, f32[1,1024]{1,0:T(1,128)S(1)}, f32[128,1024]{1,0:T(8,128)S(1)}, f32[16,256,128]{2,1,0...) custom-call(s32[49]{0:T(128)S(1)} %pad_add_fusion.1.table_ref, s32[16]{0:T(128)S(1)} %copy-done.23, ...), custom_call_target="tpu_custom_call" | custom-call | flops 8071000064 | bytes 25830000 | tf_op jit(solution)/shard_map/mid/pallas_call | solution.py:469
  342.5 11.0 %attend_back.1 = (f32[16,352,128]{2,1,0:T(8,128)S(1)}, f32[16,352,128]{2,1,0:T(8,128)S(1)}, f32[16,320,128]{2,1,0:T(8,128)S(1)}, bf16[16,352,128]{2,1,0:T(8,128)...) custom-call(s32[49]{0:T(128)S(1)} %pad_add_fusion.1.table_ref, ...), custom_call_target="tpu_custom_call" | custom-call | flops 13836000256 | bytes 44280000 | tf_op jit(solution)/shard_map/attend_back/pallas_call | solution.py:591
  358.2 15.0 %collective-permute-done.58 = bf16[2,2,40,1024]{3,2,1,0:T(8,128)(2,1)S(1)} collective-permute-done((bf16[2,2,40,1024]{3,2,1,0:T(8,128)(2,1)S(1)}, bf16[2,2,40,1024]{3,2,1,0:T(8,128)(2,1)S(1)}, u32[]{:S(2)}, u32[]{:S(2)}) %collective-permute-start.58) | collective-permute-done | bytes 327712 | tf_op jit(solution)/shard_map/ppermute | solution.py:31
  398.9 7.1 %tokens_back.1 = (bf16[256,1024]{1,0:T(8,128)(2,1)}, f32[1,1024]{1,0:T(1,128)S(1)}) custom-call(s32[49]{0:T(128)S(1)} %pad_add_fusion.1.table_ref, bf16[256,1024]{1,0:T(8,128)(2,1)S(1)} %copy-done.32, f32[1,1024]{1,0:T(1,128)S(1)} %bitcast.280, f32[256,1024]{1,0:T(8,128)S(1)} %copy-done.51, bf16[3,8,256,128]{3,2,1,0:T(8,128)(2,1)S(1)} %copy-done.53, ...), custom_call_target="tpu_custom_call" | custom-call | flops 11530000384 | bytes 36900000 | tf_op jit(solution)/shard_map/tokens_back/pallas_call | solution.py:645
  420.3 6.9 %collective-permute-done.72 = bf16[1,4,40,1024]{3,2,1,0:T(8,128)(2,1)S(1)} collective-permute-done((bf16[1,4,40,1024]{3,2,1,0:T(8,128)(2,1)S(1)}, bf16[1,4,40,1024]{3,2,1,0:T(8,128)(2,1)S(1)}, u32[]{:S(2)}, u32[]{:S(2)}) %collective-permute-start.72) | collective-permute-done | bytes 327712 | tf_op jit(solution)/shard_map/ppermute | solution.py:31
  438.3 5.9 %block_out.1 = bf16[256,1024]{1,0:T(8,128)(2,1)} custom-call(s32[16]{0:T(128)S(1)} %copy-done.23, f32[256,1024]{1,0:T(8,128)S(1)} %copy-done.39, f32[256,128]{1,0:T(8,128)S(1)} %copy-done.59, bf16[8,40,1024]{2,1,0:T(8,128)(2,1)S(1)} %bitcast.268, bf16[8,40,1024]{2,1,0:T(8,128)(2,1)S(1)} %bitcast.269, s32[2,256]{1,0:T(2,128)S(1)} %fusion.41.ids_ref), custom_call_target="tpu_custom_call" | custom-call | flops 8071000064 | bytes 25830000 | tf_op jit(solution)/shard_map/block_out/pallas_call | solution.py:512
  444.3 7.9 %collective-permute-done.78 = bf16[1,1024,128]{2,1,0:T(8,128)(2,1)S(1)} collective-permute-done((bf16[1,1024,128]{2,1,0:T(8,128)(2,1)S(1)}, bf16[1,1024,128]{2,1,0:T(8,128)(2,1)S(1)}, u32[]{:S(2)}, u32[]{:S(2)}) %collective-permute-start.78) | collective-permute-done | bytes 262176 | tf_op jit(solution)/shard_map/ppermute | solution.py:31
  453.9 4.7 collective-permute-done.79
  474.4 4.8 collective-permute-done.87
  489.7 4.2 collective-permute-done.90
  503.1 4.0 collective-permute-done.93.far_v
  507.1 10.7 %finish.1 = (f32[3,1024,1024]{2,1,0:T(8,128)}, f32[1024,1024]{1,0:T(8,128)}, f32[4,8,1024]{2,1,0:T(8,128)S(1)}, f32[4,8,1,128]{3,2,1,0:T(1,128)S(1)}, f32[4,256,128]{2,1,0:T(8,128)S(1)}) custom-call(s32[49]{0:T(128)S(1)} %pad_add_fusion.1.table_ref, s32[2]{0:T(128)S(1)} %pad_add_fusion.3.place_ref, bf16[16,352,128]{2,1,0:T(8,128)(2,1)S(1)} %pad_maximum_fusion.2.own_q, ...), custom_call_target="tpu_custom_call" | custom-call | flops 11530000384 | bytes 36900000 | tf_op jit(solution)/shard_map/finish/pallas_call | solution.py:879
  (616 shorter events, 230.9 us)
Async XLA Ops:
  25.9 19.0 %collective-permute-start.3 = (bf16[1,4,40,1152]{3,2,1,0:T(8,128)(2,1)S(1)}, bf16[1,4,40,1152]{3,2,1,0:T(8,128)(2,1)S(1)}, u32[]{:S(2)}, u32[]{:S(2)}) collective-permute-start(bf16[1,4,40,1152]{3,2,1,0:T(8,128)(2,1)S(1)} %get-tuple-element.500), channel_id=1, source_target_pairs={{0,4},{1,5},{2,6},{3,7},{4,0},{5,1},{6,2},{7,3},{8,12},{9,13},{10,... | collective-permute-start | bytes 1105928 | tf_op jit(solution)/shard_map/ppermute | solution.py:31
  29.3 18.0 %collective-permute-start.6 = (bf16[4,352,128]{2,1,0:T(8,128)(2,1)S(1)}, bf16[4,352,128]{2,1,0:T(8,128)(2,1)S(1)}, u32[]{:S(2)}, u32[]{:S(2)}) collective-permute-start(bf16[4,352,128]{2,1,0:T(8,128)(2,1)S(1)} %pad_maximum_fusion.32), channel_id=1, source_target_pairs={{0,8},{8,0},{16,24},{24,16},{1,9},{9,1},{17,25},{25,17},{2,10},{10... | collective-permute-start | bytes 1081352 | tf_op jit(solution)/shard_map/ppermute | solution.py:31
  69.2 19.9 %collective-permute-start.15 = (bf16[2,2,40,1152]{3,2,0,1:T(8,128)(2,1)S(1)}, bf16[2,2,40,1152]{3,2,0,1:T(8,128)(2,1)S(1)}, u32[]{:S(2)}, u32[]{:S(2)}) collective-permute-start(bf16[2,2,40,1152]{3,2,0,1:T(8,128)(2,1)S(1)} %get-tuple-element.498), channel_id=1, source_target_pairs={{0,4},{1,5},{2,6},{3,7},{4,0},{5,1},{6,2},{7,3},{8,12},{9,13},{10,... | collective-permute-start | bytes 1105928 | tf_op jit(solution)/shard_map/ppermute | solution.py:31
  70.2 18.8 %collective-permute-start.16 = (bf16[2,2,40,1152]{3,2,0,1:T(8,128)(2,1)S(1)}, bf16[2,2,40,1152]{3,2,0,1:T(8,128)(2,1)S(1)}, u32[]{:S(2)}, u32[]{:S(2)}) collective-permute-start(bf16[2,2,40,1152]{3,2,0,1:T(8,128)(2,1)S(1)} %get-tuple-element.496), channel_id=1, source_target_pairs={{0,16},{8,24},{16,0},{24,8},{1,17},{9,25},{17,1},{25,9},{2,18},{10... | collective-permute-start | bytes 1105928 | tf_op jit(solution)/shard_map/ppermute | solution.py:31
  101.8 24.3 %collective-permute-start.23 = (bf16[320,1152]{1,0:T(8,128)(2,1)}, bf16[320,1152]{1,0:T(8,128)(2,1)}, u32[]{:S(2)}, u32[]{:S(2)}) collective-permute-start(bf16[320,1152]{1,0:T(8,128)(2,1)} %bitcast.34.refs_4_), channel_id=1, source_target_pairs={{0,2},{1,3},{2,0},{3,1},{4,6},{5,7},{6,4},{7,5},{8,10},{9,11},{10,... | collective-permute-start | bytes 2211848 | tf_op jit(solution)/shard_map/ppermute | solution.py:31
  101.8 24.3 %collective-permute-start.21 = (bf16[320,1152]{1,0:T(8,128)(2,1)}, bf16[320,1152]{1,0:T(8,128)(2,1)}, u32[]{:S(2)}, u32[]{:S(2)}) collective-permute-start(bf16[320,1152]{1,0:T(8,128)(2,1)} %bitcast.34.refs_4_), channel_id=1, source_target_pairs={{0,1},{1,0},{2,3},{3,2},{4,5},{5,4},{6,7},{7,6},{8,9},{9,8},{10,11... | collective-permute-start | bytes 2211848 | tf_op jit(solution)/shard_map/ppermute | solution.py:31
  102.7 21.1 %collective-permute-start.22 = (bf16[320,1152]{1,0:T(8,128)(2,1)}, bf16[320,1152]{1,0:T(8,128)(2,1)}, u32[]{:S(2)}, u32[]{:S(2)}) collective-permute-start(bf16[320,1152]{1,0:T(8,128)(2,1)} %bitcast.36.refs_5_), channel_id=1, source_target_pairs={{0,1},{1,0},{2,3},{3,2},{4,5},{5,4},{6,7},{7,6},{8,9},{9,8},{10,11... | collective-permute-start | bytes 2211848 | tf_op jit(solution)/shard_map/ppermute | solution.py:31
  104.0 19.8 %collective-permute-start.20 = (bf16[1,4,40,1024]{3,2,1,0:T(8,128)(2,1)}, bf16[1,4,40,1024]{3,2,1,0:T(8,128)(2,1)}, u32[]{:S(2)}, u32[]{:S(2)}) collective-permute-start(bf16[1,4,40,1024]{3,2,1,0:T(8,128)(2,1)} %get-tuple-element.524), channel_id=1, source_target_pairs={{0,4},{1,5},{2,6},{3,7},{4,0},{5,1},{6,2},{7,3},{8,12},{9,13},{10,... | collective-permute-start | bytes 983048 | tf_op jit(solution)/shard_map/ppermute | solution.py:31
  160.1 23.3 %collective-permute-start.28 = (bf16[320,1024]{1,0:T(8,128)(2,1)S(1)}, bf16[320,1024]{1,0:T(8,128)(2,1)S(1)}, u32[]{:S(2)}, u32[]{:S(2)}) collective-permute-start(bf16[320,1024]{1,0:T(8,128)(2,1)S(1)} %bitcast.271), channel_id=1, source_target_pairs={{0,2},{1,3},{2,0},{3,1},{4,6},{5,7},{6,4},{7,5},{8,10},{9,11},{10,... | collective-permute-start | bytes 1966088 | tf_op jit(solution)/shard_map/ppermute | solution.py:31
  184.0 17.5 %collective-permute-start.32 = (bf16[320,1024]{1,0:T(8,128)(2,1)S(1)}, bf16[320,1024]{1,0:T(8,128)(2,1)S(1)}, u32[]{:S(2)}, u32[]{:S(2)}) collective-permute-start(bf16[320,1024]{1,0:T(8,128)(2,1)S(1)} %bitcast.267), channel_id=1, source_target_pairs={{0,2},{1,3},{2,0},{3,1},{4,6},{5,7},{6,4},{7,5},{8,10},{9,11},{10,... | collective-permute-start | bytes 1966088 | tf_op jit(solution)/shard_map/ppermute | solution.py:31
  185.5 31.3 %collective-permute-start.33 = (bf16[320,1152]{1,0:T(8,128)(2,1)}, bf16[320,1152]{1,0:T(8,128)(2,1)S(1)}, u32[]{:S(2)}, u32[]{:S(2)}) collective-permute-start(bf16[320,1152]{1,0:T(8,128)(2,1)} %bitcast.36.refs_5_), channel_id=1, source_target_pairs={{0,2},{1,3},{2,0},{3,1},{4,6},{5,7},{6,4},{7,5},{8,10},{9,11},{10,... | collective-permute-start | bytes 2211848 | tf_op jit(solution)/shard_map/ppermute | solution.py:31
  186.0 32.5 %collective-permute-start.46 = (bf16[320,1024]{1,0:T(8,128)(2,1)}, bf16[320,1024]{1,0:T(8,128)(2,1)}, u32[]{:S(2)}, u32[]{:S(2)}) collective-permute-start(bf16[320,1024]{1,0:T(8,128)(2,1)} %get-tuple-element.340), channel_id=1, source_target_pairs={{0,1},{1,0},{2,3},{3,2},{4,5},{5,4},{6,7},{7,6},{8,9},{9,8},{10,11... | collective-permute-start | bytes 1966088 | tf_op jit(solution)/shard_map/ppermute | solution.py:31
  186.7 33.6 %collective-permute-start.47 = (bf16[320,1024]{1,0:T(8,128)(2,1)}, bf16[320,1024]{1,0:T(8,128)(2,1)}, u32[]{:S(2)}, u32[]{:S(2)}) collective-permute-start(bf16[320,1024]{1,0:T(8,128)(2,1)} %get-tuple-element.342), channel_id=1, source_target_pairs={{0,1},{1,0},{2,3},{3,2},{4,5},{5,4},{6,7},{7,6},{8,9},{9,8},{10,11... | collective-permute-start | bytes 1966088 | tf_op jit(solution)/shard_map/ppermute | solution.py:31
  217.9 26.7 %collective-permute-start.31 = (bf16[320,1152]{1,0:T(8,128)(2,1)}, bf16[320,1152]{1,0:T(8,128)(2,1)S(1)}, u32[]{:S(2)}, u32[]{:S(2)}) collective-permute-start(bf16[320,1152]{1,0:T(8,128)(2,1)} %get-tuple-element.286), channel_id=1, source_target_pairs={{0,1},{1,0},{2,3},{3,2},{4,5},{5,4},{6,7},{7,6},{8,9},{9,8},{10,11... | collective-permute-start | bytes 2211848 | tf_op jit(solution)/shard_map/ppermute | solution.py:31
  218.4 47.6 %collective-permute-start.44 = (bf16[320,1152]{1,0:T(8,128)(2,1)}, bf16[320,1152]{1,0:T(8,128)(2,1)}, u32[]{:S(2)}, u32[]{:S(2)}) collective-permute-start(bf16[320,1152]{1,0:T(8,128)(2,1)} %get-tuple-element.335), channel_id=1, source_target_pairs={{0,1},{1,0},{2,3},{3,2},{4,5},{5,4},{6,7},{7,6},{8,9},{9,8},{10,11... | collective-permute-start | bytes 2211848 | tf_op jit(solution)/shard_map/ppermute | solution.py:31
  225.5 18.5 %collective-permute-start.39 = (bf16[320,1152]{1,0:T(8,128)(2,1)S(1)}, bf16[320,1152]{1,0:T(8,128)(2,1)S(1)}, u32[]{:S(2)}, u32[]{:S(2)}) collective-permute-start(bf16[320,1152]{1,0:T(8,128)(2,1)S(1)} %add_convert_fusion.3), channel_id=1, source_target_pairs={{0,2},{1,3},{2,0},{3,1},{4,6},{5,7},{6,4},{7,5},{8,10},{9,11},{10,... | collective-permute-start | bytes 2211848 | tf_op jit(solution)/shard_map/ppermute | solution.py:31
  244.9 20.4 %collective-permute-start.40 = (bf16[4,1,40,1152]{3,2,0,1:T(8,128)(2,1)S(1)}, bf16[4,1,40,1152]{3,2,0,1:T(8,128)(2,1)S(1)}, u32[]{:S(2)}, u32[]{:S(2)}) collective-permute-start(bf16[4,1,40,1152]{3,2,0,1:T(8,128)(2,1)S(1)} %get-tuple-element.490), channel_id=1, source_target_pairs={{0,16},{8,24},{16,0},{24,8},{1,17},{9,25},{17,1},{25,9},{2,18},{10... | collective-permute-start | bytes 1105928 | tf_op jit(solution)/shard_map/ppermute | solution.py:31
  247.6 18.4 %collective-permute-start.42 = (bf16[320,1152]{1,0:T(8,128)(2,1)S(1)}, bf16[320,1152]{1,0:T(8,128)(2,1)S(1)}, u32[]{:S(2)}, u32[]{:S(2)}) collective-permute-start(bf16[320,1152]{1,0:T(8,128)(2,1)S(1)} %add_convert_fusion.1), channel_id=1, source_target_pairs={{0,2},{1,3},{2,0},{3,1},{4,6},{5,7},{6,4},{7,5},{8,10},{9,11},{10,... | collective-permute-start | bytes 2211848 | tf_op jit(solution)/shard_map/ppermute | solution.py:31
  270.3 18.4 %collective-permute-start.43 = (bf16[2,2,40,1152]{3,2,1,0:T(8,128)(2,1)S(1)}, bf16[2,2,40,1152]{3,2,1,0:T(8,128)(2,1)S(1)}, u32[]{:S(2)}, u32[]{:S(2)}) collective-permute-start(bf16[2,2,40,1152]{3,2,1,0:T(8,128)(2,1)S(1)} %get-tuple-element.488), channel_id=1, source_target_pairs={{0,4},{1,5},{2,6},{3,7},{4,0},{5,1},{6,2},{7,3},{8,12},{9,13},{10,... | collective-permute-start | bytes 1105928 | tf_op jit(solution)/shard_map/ppermute | solution.py:31
  289.8 23.3 %collective-permute-start.52 = (bf16[320,1024]{1,0:T(8,128)(2,1)S(1)}, bf16[320,1024]{1,0:T(8,128)(2,1)S(1)}, u32[]{:S(2)}, u32[]{:S(2)}) collective-permute-start(bf16[320,1024]{1,0:T(8,128)(2,1)S(1)} %copy-done.95), channel_id=1, source_target_pairs={{0,2},{1,3},{2,0},{3,1},{4,6},{5,7},{6,4},{7,5},{8,10},{9,11},{10,... | collective-permute-start | bytes 1966088 | tf_op jit(solution)/shard_map/ppermute | solution.py:31
  291.2 19.7 %collective-permute-start.51 = (bf16[2,2,40,1152]{3,2,1,0:T(8,128)(2,1)S(1)}, bf16[2,2,40,1152]{3,2,1,0:T(8,128)(2,1)S(1)}, u32[]{:S(2)}, u32[]{:S(2)}) collective-permute-start(bf16[2,2,40,1152]{3,2,1,0:T(8,128)(2,1)S(1)} %bitcast.317), channel_id=1, source_target_pairs={{0,4},{1,5},{2,6},{3,7},{4,0},{5,1},{6,2},{7,3},{8,12},{9,13},{10,... | collective-permute-start | bytes 1105928 | tf_op jit(solution)/shard_map/ppermute | solution.py:31
  292.8 18.1 %collective-permute-start.50 = (bf16[1,4,40,1152]{3,2,1,0:T(8,128)(2,1)S(1)}, bf16[1,4,40,1152]{3,2,1,0:T(8,128)(2,1)S(1)}, u32[]{:S(2)}, u32[]{:S(2)}) collective-permute-start(bf16[1,4,40,1152]{3,2,1,0:T(8,128)(2,1)S(1)} %get-tuple-element.484), channel_id=1, source_target_pairs={{0,8},{8,0},{16,24},{24,16},{1,9},{9,1},{17,25},{25,17},{2,10},{10... | collective-permute-start | bytes 1105928 | tf_op jit(solution)/shard_map/ppermute | solution.py:31
  320.4 22.0 %collective-permute-start.56 = (bf16[320,1024]{1,0:T(8,128)(2,1)}, bf16[320,1024]{1,0:T(8,128)(2,1)S(1)}, u32[]{:S(2)}, u32[]{:S(2)}) collective-permute-start(bf16[320,1024]{1,0:T(8,128)(2,1)} %add_convert_fusion.9), channel_id=1, source_target_pairs={{0,2},{1,3},{2,0},{3,1},{4,6},{5,7},{6,4},{7,5},{8,10},{9,11},{10,... | collective-permute-start | bytes 1966088 | tf_op jit(solution)/shard_map/ppermute | solution.py:31
  354.6 18.7 %collective-permute-start.60 = (bf16[16,352,128]{2,1,0:T(8,128)(2,1)S(1)}, bf16[16,352,128]{2,1,0:T(8,128)(2,1)S(1)}, u32[]{:S(2)}, u32[]{:S(2)}) collective-permute-start(bf16[16,352,128]{2,1,0:T(8,128)(2,1)S(1)} %get-tuple-element.388), channel_id=1, source_target_pairs={{0,1},{1,0},{2,3},{3,2},{4,5},{5,4},{6,7},{7,6},{8,9},{9,8},{10,11... | collective-permute-start | bytes 4325384 | tf_op jit(solution)/shard_map/ppermute | solution.py:31
  354.6 18.7 %collective-permute-start.61 = (bf16[16,352,128]{2,1,0:T(8,128)(2,1)S(1)}, bf16[16,352,128]{2,1,0:T(8,128)(2,1)S(1)}, u32[]{:S(2)}, u32[]{:S(2)}) collective-permute-start(bf16[16,352,128]{2,1,0:T(8,128)(2,1)S(1)} %get-tuple-element.390), channel_id=1, source_target_pairs={{0,1},{1,0},{2,3},{3,2},{4,5},{5,4},{6,7},{7,6},{8,9},{9,8},{10,11... | collective-permute-start | bytes 4325384 | tf_op jit(solution)/shard_map/ppermute | solution.py:31
  355.1 18.2 %collective-permute-start.62 = (bf16[16,320,128]{2,1,0:T(8,128)(2,1)S(1)}, bf16[16,320,128]{2,1,0:T(8,128)(2,1)S(1)}, u32[]{:S(2)}, u32[]{:S(2)}) collective-permute-start(bf16[16,320,128]{2,1,0:T(8,128)(2,1)S(1)} %get-tuple-element.392), channel_id=1, source_target_pairs={{0,1},{1,0},{2,3},{3,2},{4,5},{5,4},{6,7},{7,6},{8,9},{9,8},{10,11... | collective-permute-start | bytes 3932168 | tf_op jit(solution)/shard_map/ppermute | solution.py:31
  355.2 18.0 %collective-permute-start.58 = (bf16[2,2,40,1024]{3,2,1,0:T(8,128)(2,1)S(1)}, bf16[2,2,40,1024]{3,2,1,0:T(8,128)(2,1)S(1)}, u32[]{:S(2)}, u32[]{:S(2)}) collective-permute-start(bf16[2,2,40,1024]{3,2,1,0:T(8,128)(2,1)S(1)} %get-tuple-element.512), channel_id=1, source_target_pairs={{0,4},{1,5},{2,6},{3,7},{4,0},{5,1},{6,2},{7,3},{8,12},{9,13},{10,... | collective-permute-start | bytes 983048 | tf_op jit(solution)/shard_map/ppermute | solution.py:31
  381.5 24.5 %collective-permute-start.67 = (bf16[2,2,40,1024]{3,2,1,0:T(8,128)(2,1)S(1)}, bf16[2,2,40,1024]{3,2,1,0:T(8,128)(2,1)S(1)}, u32[]{:S(2)}, u32[]{:S(2)}) collective-permute-start(bf16[2,2,40,1024]{3,2,1,0:T(8,128)(2,1)S(1)} %bitcast.325), channel_id=1, source_target_pairs={{0,4},{1,5},{2,6},{3,7},{4,0},{5,1},{6,2},{7,3},{8,12},{9,13},{10,... | collective-permute-start | bytes 983048 | tf_op jit(solution)/shard_map/ppermute | solution.py:31
  381.6 24.4 %collective-permute-start.66 = (bf16[1,4,40,1024]{3,2,1,0:T(8,128)(2,1)}, bf16[1,4,40,1024]{3,2,1,0:T(8,128)(2,1)S(1)}, u32[]{:S(2)}, u32[]{:S(2)}) collective-permute-start(bf16[1,4,40,1024]{3,2,1,0:T(8,128)(2,1)} %get-tuple-element.506), channel_id=1, source_target_pairs={{0,8},{8,0},{16,24},{24,16},{1,9},{9,1},{17,25},{25,17},{2,10},{10... | collective-permute-start | bytes 983048 | tf_op jit(solution)/shard_map/ppermute | solution.py:31
  382.6 23.5 %collective-permute-start.65 = (bf16[8,320,128]{2,1,0:T(8,128)(2,1)}, bf16[8,320,128]{2,1,0:T(8,128)(2,1)S(1)}, u32[]{:S(2)}, u32[]{:S(2)}) collective-permute-start(bf16[8,320,128]{2,1,0:T(8,128)(2,1)} %add_convert_fusion.6), channel_id=1, source_target_pairs={{0,8},{8,0},{16,24},{24,16},{1,9},{9,1},{17,25},{25,17},{2,10},{10... | collective-permute-start | bytes 1966088 | tf_op jit(solution)/shard_map/ppermute | solution.py:31
  383.7 22.4 %collective-permute-start.64 = (bf16[8,352,128]{2,1,0:T(8,128)(2,1)}, bf16[8,352,128]{2,1,0:T(8,128)(2,1)S(1)}, u32[]{:S(2)}, u32[]{:S(2)}) collective-permute-start(bf16[8,352,128]{2,1,0:T(8,128)(2,1)} %add_convert_fusion.4), channel_id=1, source_target_pairs={{0,16},{8,24},{16,0},{24,8},{1,17},{9,25},{17,1},{25,9},{2,18},{10... | collective-permute-start | bytes 2162696 | tf_op jit(solution)/shard_map/ppermute | solution.py:31
  384.6 24.9 %collective-permute-start.63 = (bf16[8,352,128]{2,1,0:T(8,128)(2,1)}, bf16[8,352,128]{2,1,0:T(8,128)(2,1)S(1)}, u32[]{:S(2)}, u32[]{:S(2)}) collective-permute-start(bf16[8,352,128]{2,1,0:T(8,128)(2,1)} %add_convert_fusion.5), channel_id=1, source_target_pairs={{0,2},{1,3},{2,0},{3,1},{4,6},{5,7},{6,4},{7,5},{8,10},{9,11},{10,... | collective-permute-start | bytes 2162696 | tf_op jit(solution)/shard_map/ppermute | solution.py:31
  (181 other events, 1624.4 us)

commit v4 on v3

--- a/solution.py
+++ b/solution.py
@@ -651,7 +651,7 @@
             jax.ShapeDtypeStruct((1, features), F32),
         ],
         scratch_shapes=[pltpu.VMEM((length, features), F32)],
-        compiler_params=params(14),
+        compiler_params=params(30),
         name="tokens_back",
         cost_estimate=cost(10),
     )(table, tokens, gain.reshape(1, features), x1_grad, dheads, *owns, *fars)
@@ -664,16 +664,17 @@
     return value
 
 
-def expert_body(expert_ref, *refs, count):
-    x_refs, up_refs, refs = refs[:count], refs[count : 2 * count], refs[2 * count :]
+def expert_body(expert_ref, *refs, count, apart):
+    x_refs, up_refs, refs = refs[:count], refs[count:apart], refs[apart:]
     router_ref, gate_w, up_w, down_w = refs[:4]
     y_refs, dx_refs = refs[-2 * count - 5 : -count - 5], refs[-count - 5 : -5]
     x_out, dy_ref, hidden_ref, dgate_ref, dup_ref = refs[-5:]
     piece = pl.program_id(0)
+    features = x_out.shape[1]
     x = choose(x_refs, piece)
-    up = choose(up_refs, piece)
+    up = choose(up_refs, piece) if up_refs else x[:, features:]
+    x = x[:, :features]
     x_out[...] = x
-    features = x.shape[1]
     logits = mm(x, router_ref[...])
     lane = lax.broadcasted_iota(jnp.int32, logits.shape, 1)
     other_id = up[:, features : features + 1].astype(jnp.int32)
@@ -715,7 +716,7 @@
 
 
 def expert_call(expert, xs, upstreams, router, gate_w, up_w, down_w, first, total, kept):
-    rows, features = xs[0].shape
+    rows, features = xs[0].shape[0], gate_w.shape[1]
     width = gate_w.shape[0]
     count = len(xs)
 
@@ -729,7 +730,7 @@
     kept_in = [] if kept is None else list(kept)
     inputs = list(xs) + list(upstreams) + [router, gate_w, up_w, down_w]
     out = pl.pallas_call(
-        functools.partial(expert_body, count=count),
+        functools.partial(expert_body, count=count, apart=count + len(upstreams)),
         grid_spec=pltpu.PrefetchScalarGridSpec(
             num_scalar_prefetch=1,
             grid=(count,),
@@ -747,7 +748,7 @@
         },
         compiler_params=params(48),
         name="expert",
-        cost_estimate=cost(6 * count),
+        cost_estimate=cost(20 if count == 4 else 1),
     )(expert, *inputs, *kept_in)
     return out[:count], out[count : 2 * count], out[2 * count :]
 
@@ -1119,9 +1120,8 @@
     projection_parts = [tuple(half[:, row_count:] for half in part) for part in late_parts]
     projection_parts, x_state = together(projection_parts, x_state)
     x_own = [flat(state) for state in x_state]
-    x_core, x_part = to_core(x_own), to_part(x_own)
-    late_u, _ = together(u_own[1], x_own)
-    u_part.append(from_partner(late_u, part_hop))
+    x_core, x_part = to_core(x_own), to_part(x_own[:1])
+    joined_part = from_partner(jnp.concatenate([x_own[1], u_own[1]], axis=1), part_hop)
 
     my_expert = (my_narrow + groups * (my_wide // split_parts)).reshape(1).astype(jnp.int32)
     row_total = 8 * x_own[0].shape[0]
@@ -1137,9 +1137,12 @@
     y_far, parts_back = [], []
     for chain in range(2):
         if chain:
-            x_part[1], u_part[1], y_far = together(x_part[1], u_part[1], y_far)
-        xs = [x_part[chain], from_partner(x_part[chain], core_hop)]
-        us = [u_part[chain], from_partner(u_part[chain], core_hop)]
+            joined_part, y_far = together(joined_part, y_far)
+            xs = [joined_part, from_partner(joined_part, core_hop)]
+            us = []
+        else:
+            xs = [x_part[0], from_partner(x_part[0], core_hop)]
+            us = [u_part[0], from_partner(u_part[0], core_hop)]
         y_two, dx_two, kept = run_expert(xs, us, 4 + 2 * chain, kept)
         if chain:
             y_two, dx_two, kept, parts_back[0] = together(y_two, dx_two, kept, parts_back[0])
@@ -1237,7 +1240,6 @@
     for value, _ in addends:
         size += value.shape[1]
         ends.append(size)
-    y_gots, addends = together(y_gots, addends)
     y_step = 1
     router_local, moe_gain_local, dheads, x1_grad, diag, _ = together(
         router_local, moe_gain_local, dheads, x1_grad, diag, addends
@@ -1253,7 +1255,6 @@
         return joined, backs_out(joined, y_step + 1), y_step + 1
 
     small_hops = list(orders[0])
-    y_states, y_gots, y_step = more_outputs()
     for count, stage in enumerate(stages[::-1]):
         halved = [halve(values, order[stage]) for values, order in zip(addends, orders)]
         gots = [got for _, got in halved]
@@ -1286,10 +1287,6 @@
     summed = [sum(value.astype(F32) for value in values) for values in addends]
     while y_gots:
         y_states, y_gots, y_step = more_outputs()
-    block_out = block_out_call(
-        back_table, hidden_x1, gates, slots_first(y_states), row_ids, experts, capacity
-    )
-
     def small_beside(value, others):
         if not small_hops:
             return value, together(*others)
@@ -1300,12 +1297,15 @@
     total = jnp.concatenate(summed, axis=1)
     for hop in orders[0][:shared][::-1]:
         got = halve_send(total, hop)
-        small, (got, block_out) = small_beside(small, (got, block_out))
+        small, (got, y_states) = small_beside(small, (got, y_states))
         total = halve_add(total, got)
+    block_out = block_out_call(
+        back_table, hidden_x1, gates, slots_first(y_states), row_ids, experts, capacity
+    )
     blocks = total.astype(BF)
     for hop in orders[0][:shared]:
         got = from_partner(blocks, hop)
-        small, (got, total) = small_beside(small, (got, total))
+        small, (got, total, block_out) = small_beside(small, (got, total, block_out))
         blocks = grow(blocks, got)
     pieces = split_rows(total, ends)
     dense_mine = jnp.concatenate(

time: 529 us -> 520 us (0.983)
  waiting for transfers between devices: 196 us -> 179 us
  other arithmetic: 63.4 us -> 76.1 us
  local copies, waits for them, and re-layouts: 51.7 us -> 43.3 us
    ppermute x94 -> x92, waiting for transfers between devices: 196 us -> 179 us  [from_partner(): return lax.ppermute(value, axis, pairs)]
    unnamed x250 -> x274, local copies, waits for them, and re-layouts: 28.2 us -> 16.2 us
    convert_element_type x9, other arithmetic: 3.78 us -> 10.2 us  [halve(): send = sum((value[half:].astype(F32) for value in values)).astype(BF)]
    ppermute x94 -> x92, starting transfers between devices: 80.2 us -> 83.6 us  [from_partner(): return lax.ppermute(value, axis, pairs)]
  transfers between devices with their start and end apart: 94 -> 92, of which waited for: 41 -> 37; matrix products, arithmetic and copies ran while one was open for 11% -> 15% of each run, Pallas kernels for 19% -> 20%
where the time goes in v4:
time: 520 us; the launch traced here: 511 us
  waiting for transfers between devices  179 us (34%)
  Pallas kernels  123 us (24%)
  starting transfers between devices  83.6 us (16%)
  other arithmetic  76.1 us (15%)
  local copies, waits for them, and re-layouts  43.3 us (8%)
  between operations  5.77 us (1%)
    ppermute x92, waiting for transfers between devices, from_partner(): return lax.ppermute(value, axis, pairs)  179 us
    ppermute x92, starting transfers between devices, from_partner(): return lax.ppermute(value, axis, pairs)  83.6 us
    pallas_call x3, Pallas kernels, expert_call(): pl.pallas_call(functools.partial(expert_body, count=count, apart=count +...  46.6 us
    pallas_call x3, Pallas kernels, expert_grad_call(): pl.pallas_call(expert_grad_body, grid=(features // size,), in_specs=[pl.B...  20.9 us
    unnamed x274, local copies, waits for them, and re-layouts  16.2 us
    concatenate x21, other arithmetic, grow(): return jnp.concatenate([blocks, got], axis=axis)  14.1 us
    pallas_call x1, Pallas kernels, attend_call(): pl.pallas_call(body, in_specs=[smem()] + [vmem()] * 9, out_specs=[vmem()]...  11.1 us
    sub x4, other arithmetic, factored(): return weight - adafactor_step(gradient, row_stats, col_stats, mean_rows)  10.8 us
  transfers between devices with their start and end apart: 92, of which 37 were waited for; matrix products, arithmetic and copies ran while one was open for 15% of the time, Pallas kernels for 20%

profile of v4, /device:TPU:0, one launch (start us, length us, event | category | flops | bytes accessed | tf_op | source)
XLA Modules:
  0.0 511.2 jit_solution(373564003235802665)
XLA Ops:
  3.6 4.1 collective-permute-start
  11.6 8.3 %collective-permute-done = bf16[1,1040,128]{2,1,0:T(8,128)(2,1)S(1)} collective-permute-done((bf16[1,1040,128]{2,1,0:T(8,128)(2,1)S(1)}, bf16[1,1040,128]{2,1,0:T(8,128)(2,1)S(1)}, u32[]{:S(2)}, u32[]{:S(2)}) %collective-permute-start) | collective-permute-done | bytes 266272 | tf_op jit(solution)/shard_map/ppermute | solution.py:31
  31.9 7.2 %collective-permute-done.2 = bf16[1,4,40,1152]{3,2,1,0:T(8,128)(2,1)S(1)} collective-permute-done((bf16[1,4,40,1152]{3,2,1,0:T(8,128)(2,1)S(1)}, bf16[1,4,40,1152]{3,2,1,0:T(8,128)(2,1)S(1)}, u32[]{:S(2)}, u32[]{:S(2)}) %collective-permute-start.2) | collective-permute-done | bytes 368672 | tf_op jit(solution)/shard_map/ppermute | solution.py:31
  39.2 5.6 %collective-permute-done.3 = bf16[1,4,40,1152]{3,2,1,0:T(8,128)(2,1)S(1)} collective-permute-done((bf16[1,4,40,1152]{3,2,1,0:T(8,128)(2,1)S(1)}, bf16[1,4,40,1152]{3,2,1,0:T(8,128)(2,1)S(1)}, u32[]{:S(2)}, u32[]{:S(2)}) %collective-permute-start.3) | collective-permute-done | bytes 368672 | tf_op jit(solution)/shard_map/ppermute | solution.py:31
  50.6 12.1 %collective-permute-done.9 = bf16[8,352,128]{2,1,0:T(8,128)(2,1)} collective-permute-done((bf16[8,352,128]{2,1,0:T(8,128)(2,1)S(1)}, bf16[8,352,128]{2,1,0:T(8,128)(2,1)}, u32[]{:S(2)}, u32[]{:S(2)}) %collective-permute-start.9) | collective-permute-done | bytes 720928 | tf_op jit(solution)/shard_map/ppermute | solution.py:31
  72.4 11.1 %attend.1 = (bf16[256,1024]{1,0:T(8,128)(2,1)S(1)}, bf16[3,8,256,128]{3,2,1,0:T(8,128)(2,1)S(1)}, f32[16,256,256]{2,1,0:T(8,128)S(1)}, bf16[8,256,128]{2,1,0:T(8,128)(2,1)S(1)}) custom-call(s32[49]{0:T(128)S(1)} %pad_add_fusion.table_ref, bf16[256,1024]{1,0:T(8,128)(2,1)S(1)} %copy-done.39, f32[1,1024]{1,0:T(1,128)S(1)} %bitcast.283, ...), custom_call_target="tpu_custom_call" | custom-call | flops 18447998976 | bytes 59040000 | tf_op jit(solution)/shard_map/attend/pallas_call | solution.py:253
  93.8 5.7 %collective-permute-done.18 = bf16[4,1,40,1152]{3,2,0,1:T(8,128)(2,1)S(1)} collective-permute-done((bf16[4,1,40,1152]{3,2,0,1:T(8,128)(2,1)S(1)}, bf16[4,1,40,1152]{3,2,0,1:T(8,128)(2,1)S(1)}, u32[]{:S(2)}, u32[]{:S(2)}) %collective-permute-start.18) | collective-permute-done | bytes 368672 | tf_op jit(solution)/shard_map/ppermute | solution.py:31
  111.4 12.4 %collective-permute-done.20 = bf16[1,4,40,1024]{3,2,1,0:T(8,128)(2,1)} collective-permute-done((bf16[1,4,40,1024]{3,2,1,0:T(8,128)(2,1)}, bf16[1,4,40,1024]{3,2,1,0:T(8,128)(2,1)}, u32[]{:S(2)}, u32[]{:S(2)}) %collective-permute-start.20) | collective-permute-done | bytes 327712 | tf_op jit(solution)/shard_map/ppermute | solution.py:31
  130.1 12.4 %collective-permute-done.24 = bf16[2,2,40,1024]{3,2,0,1:T(8,128)(2,1)S(1)} collective-permute-done((bf16[2,2,40,1024]{3,2,0,1:T(8,128)(2,1)S(1)}, bf16[2,2,40,1024]{3,2,0,1:T(8,128)(2,1)S(1)}, u32[]{:S(2)}, u32[]{:S(2)}) %collective-permute-start.24) | collective-permute-done | bytes 327712 | tf_op jit(solution)/shard_map/ppermute | solution.py:31
  160.5 22.6 %expert.3 = (bf16[320,1024]{1,0:T(8,128)(2,1)S(1)}, bf16[320,1024]{1,0:T(8,128)(2,1)S(1)}, bf16[320,1024]{1,0:T(8,128)(2,1)}, bf16[320,1024]{1,0:T(8,128)(2,1)S(...) custom-call(s32[1]{0:T(128)} %bitcast.61.expert_ref, ...), custom_call_target="tpu_custom_call" | custom-call | flops 23060000768 | bytes 73800000 | tf_op jit(solution)/shard_map/expert/pallas_call | solution.py:732
  187.4 12.2 %expert.4 = (bf16[320,1024]{1,0:T(8,128)(2,1)S(1)}, bf16[320,1024]{1,0:T(8,128)(2,1)S(1)}, bf16[320,1152]{1,0:T(8,128)(2,1)S(1)}, bf16[320,1152]{1,0:T(8,128)(2,...) custom-call(s32[1]{0:T(128)} %bitcast.61.expert_ref, ...), custom_call_target="tpu_custom_call", output_to_operand_aliasing={{4}: (9, {}), {5}: (10, {}), {6}: (11, {}), {7}: (12, {}), ... | custom-call | flops 1152999936 | bytes 3690000 | tf_op jit(solution)/shard_map/expert/pallas_call | solution.py:732
  202.6 16.0 %collective-permute-done.32.refs_0_ = bf16[320,2176]{1,0:T(8,128)(2,1)S(1)} collective-permute-done((bf16[320,2176]{1,0:T(8,128)(2,1)S(1)}, bf16[320,2176]{1,0:T(8,128)(2,1)S(1)}, u32[]{:S(2)}, u32[]{:S(2)}) %collective-permute-start.32) | collective-permute-done | bytes 1392672 | tf_op jit(solution)/shard_map/ppermute | solution.py:31
  227.3 11.9 %expert.5 = (bf16[320,1024]{1,0:T(8,128)(2,1)S(1)}, bf16[320,1024]{1,0:T(8,128)(2,1)S(1)}, bf16[320,1152]{1,0:T(8,128)(2,1)S(1)}, bf16[320,1152]{1,0:T(8,128)(2,...) custom-call(s32[1]{0:T(128)} %bitcast.61.expert_ref, ...), custom_call_target="tpu_custom_call", output_to_operand_aliasing={{4}: (7, {}), {5}: (8, {}), {6}: (9, {}), {7}: (10, {}), {8... | custom-call | flops 1152999936 | bytes 3690000 | tf_op jit(solution)/shard_map/expert/pallas_call | solution.py:732
  248.0 6.9 %expert_grad.3 = f32[704,1024]{1,0:T(8,128)} custom-call(bf16[2560,704]{1,0:T(8,128)(2,1)S(1)} %copy-done.4, bf16[2560,1024]{1,0:T(8,128)(2,1)S(1)} %copy-done.2), custom_call_target="tpu_custom_call" | custom-call | flops 10376999936 | bytes 33210000 | tf_op jit(solution)/shard_map/expert_grad/pallas_call | solution.py:764
  254.9 6.9 %expert_grad.4 = f32[704,1024]{1,0:T(8,128)} custom-call(bf16[2560,704]{1,0:T(8,128)(2,1)S(1)} %copy-done.5, bf16[2560,1024]{1,0:T(8,128)(2,1)S(1)} %copy-done.2), custom_call_target="tpu_custom_call" | custom-call | flops 10376999936 | bytes 33210000 | tf_op jit(solution)/shard_map/expert_grad/pallas_call | solution.py:764
  269.7 7.1 %expert_grad.5 = f32[704,1024]{1,0:T(8,128)} custom-call(bf16[2560,704]{1,0:T(8,128)(2,1)S(1)} %copy-done.3, bf16[2560,1024]{1,0:T(8,128)(2,1)S(1)} %bitcast.264), custom_call_target="tpu_custom_call" | custom-call | flops 10376999936 | bytes 33210000 | tf_op jit(solution)/shard_map/expert_grad/pallas_call | solution.py:764
  277.3 8.0 %collective-permute-done.41 = bf16[2,2,40,1152]{3,2,1,0:T(8,128)(2,1)S(1)} collective-permute-done((bf16[2,2,40,1152]{3,2,1,0:T(8,128)(2,1)S(1)}, bf16[2,2,40,1152]{3,2,1,0:T(8,128)(2,1)S(1)}, u32[]{:S(2)}, u32[]{:S(2)}) %collective-permute-start.41) | collective-permute-done | bytes 368672 | tf_op jit(solution)/shard_map/ppermute | solution.py:31
  292.0 16.8 %collective-permute-done.49 = bf16[2,2,40,1152]{3,2,1,0:T(8,128)(2,1)S(1)} collective-permute-done((bf16[2,2,40,1152]{3,2,1,0:T(8,128)(2,1)S(1)}, bf16[2,2,40,1152]{3,2,1,0:T(8,128)(2,1)S(1)}, u32[]{:S(2)}, u32[]{:S(2)}) %collective-permute-start.49) | collective-permute-done | bytes 368672 | tf_op jit(solution)/shard_map/ppermute | solution.py:31
  317.4 5.0 bitcast_subtract_fusion
  331.5 6.0 %mid.1 = (f32[256,1024]{1,0:T(8,128)S(1)}, f32[256,128]{1,0:T(8,128)S(1)}, f32[1,1024]{1,0:T(1,128)S(1)}, f32[128,1024]{1,0:T(8,128)S(1)}, f32[16,256,128]{2,1,0...) custom-call(s32[49]{0:T(128)S(1)} %pad_add_fusion.table_ref, s32[16]{0:T(128)S(1)} %copy-done.34, ...), custom_call_target="tpu_custom_call" | custom-call | flops 8071000064 | bytes 25830000 | tf_op jit(solution)/shard_map/mid/pallas_call | solution.py:469
  338.2 10.8 %attend_back.1 = (f32[16,352,128]{2,1,0:T(8,128)S(1)}, f32[16,352,128]{2,1,0:T(8,128)S(1)}, f32[16,320,128]{2,1,0:T(8,128)S(1)}, bf16[16,352,128]{2,1,0:T(8,128)...) custom-call(s32[49]{0:T(128)S(1)} %pad_add_fusion.table_ref, ...), custom_call_target="tpu_custom_call" | custom-call | flops 13836000256 | bytes 44280000 | tf_op jit(solution)/shard_map/attend_back/pallas_call | solution.py:591
  361.8 7.3 %tokens_back.1 = (bf16[256,1024]{1,0:T(8,128)(2,1)}, f32[1,1024]{1,0:T(1,128)S(1)}) custom-call(s32[49]{0:T(128)S(1)} %pad_add_fusion.table_ref, bf16[256,1024]{1,0:T(8,128)(2,1)S(1)} %copy-done.40, f32[1,1024]{1,0:T(1,128)S(1)} %bitcast.284, f32[256,1024]{1,0:T(8,128)S(1)} %get-tuple-element.387.x1_grad_ref, ...), custom_call_target="tpu_custom_call" | custom-call | flops 11530000384 | bytes 36900000 | tf_op jit(solution)/shard_map/tokens_back/pallas_call | solution.py:645
  370.2 7.0 %collective-permute-done.61 = bf16[8,320,128]{2,1,0:T(8,128)(2,1)} collective-permute-done((bf16[8,320,128]{2,1,0:T(8,128)(2,1)}, bf16[8,320,128]{2,1,0:T(8,128)(2,1)}, u32[]{:S(2)}, u32[]{:S(2)}) %collective-permute-start.61) | collective-permute-done | bytes 655392 | tf_op jit(solution)/shard_map/ppermute | solution.py:31
  377.2 4.8 collective-permute-done.57
  395.2 9.9 %collective-permute-done.66 = bf16[4,320,128]{2,1,0:T(8,128)(2,1)S(1)} collective-permute-done((bf16[4,320,128]{2,1,0:T(8,128)(2,1)S(1)}, bf16[4,320,128]{2,1,0:T(8,128)(2,1)S(1)}, u32[]{:S(2)}, u32[]{:S(2)}) %collective-permute-start.66) | collective-permute-done | bytes 327712 | tf_op jit(solution)/shard_map/ppermute | solution.py:31
  405.0 3.6 collective-permute-done.69
  433.2 8.0 %collective-permute-done.76 = bf16[1,1024,128]{2,1,0:T(8,128)(2,1)} collective-permute-done((bf16[1,1024,128]{2,1,0:T(8,128)(2,1)}, bf16[1,1024,128]{2,1,0:T(8,128)(2,1)}, u32[]{:S(2)}, u32[]{:S(2)}) %collective-permute-start.76) | collective-permute-done | bytes 262176 | tf_op jit(solution)/shard_map/ppermute | solution.py:31
  445.4 5.9 %block_out.1 = bf16[256,1024]{1,0:T(8,128)(2,1)} custom-call(s32[16]{0:T(128)S(1)} %copy-done.34, f32[256,1024]{1,0:T(8,128)S(1)} %copy-done.46, f32[256,128]{1,0:T(8,128)S(1)} %copy-done.58, bf16[8,40,1024]{2,1,0:T(8,128)(2,1)S(1)} %bitcast.276, bf16[8,40,1024]{2,1,0:T(8,128)(2,1)S(1)} %bitcast.278, s32[2,256]{1,0:T(2,128)S(1)} %fusion.41.ids_ref), custom_call_target="tpu_custom_call" | custom-call | flops 8071000064 | bytes 25830000 | tf_op jit(solution)/shard_map/block_out/pallas_call | solution.py:512
  465.8 4.5 collective-permute-done.85
  484.3 3.8 collective-permute-done.87
  493.3 3.9 collective-permute-done.91.far_v
  497.3 10.7 %finish.1 = (f32[3,1024,1024]{2,1,0:T(8,128)}, f32[1024,1024]{1,0:T(8,128)}, f32[4,8,1024]{2,1,0:T(8,128)S(1)}, f32[4,8,1,128]{3,2,1,0:T(1,128)S(1)}, f32[4,256,128]{2,1,0:T(8,128)S(1)}) custom-call(s32[49]{0:T(128)S(1)} %pad_add_fusion.table_ref, s32[2]{0:T(128)S(1)} %pad_add_fusion.3.place_ref, bf16[16,352,128]{2,1,0:T(8,128)(2,1)S(1)} %pad_maximum_fusion.2.own_q, ...), custom_call_target="tpu_custom_call" | custom-call | flops 11530000384 | bytes 36900000 | tf_op jit(solution)/shard_map/finish/pallas_call | solution.py:880
  (638 shorter events, 226.9 us)
Async XLA Ops:
  25.8 19.0 %collective-permute-start.3 = (bf16[1,4,40,1152]{3,2,1,0:T(8,128)(2,1)S(1)}, bf16[1,4,40,1152]{3,2,1,0:T(8,128)(2,1)S(1)}, u32[]{:S(2)}, u32[]{:S(2)}) collective-permute-start(bf16[1,4,40,1152]{3,2,1,0:T(8,128)(2,1)S(1)} %get-tuple-element.488), channel_id=1, source_target_pairs={{0,4},{1,5},{2,6},{3,7},{4,0},{5,1},{6,2},{7,3},{8,12},{9,13},{10,... | collective-permute-start | bytes 1105928 | tf_op jit(solution)/shard_map/ppermute | solution.py:31
  45.6 17.1 %collective-permute-start.9 = (bf16[8,352,128]{2,1,0:T(8,128)(2,1)S(1)}, bf16[8,352,128]{2,1,0:T(8,128)(2,1)}, u32[]{:S(2)}, u32[]{:S(2)}) collective-permute-start(bf16[8,352,128]{2,1,0:T(8,128)(2,1)S(1)} %pad_maximum_fusion.14), channel_id=1, source_target_pairs={{0,2},{1,3},{2,0},{3,1},{4,6},{5,7},{6,4},{7,5},{8,10},{9,11},{10,... | collective-permute-start | bytes 2162696 | tf_op jit(solution)/shard_map/ppermute | solution.py:31
  47.1 17.0 %collective-permute-start.10 = (bf16[8,352,128]{2,1,0:T(8,128)(2,1)}, bf16[8,352,128]{2,1,0:T(8,128)(2,1)}, u32[]{:S(2)}, u32[]{:S(2)}) collective-permute-start(bf16[8,352,128]{2,1,0:T(8,128)(2,1)} %pad_maximum_fusion.15), channel_id=1, source_target_pairs={{0,16},{8,24},{16,0},{24,8},{1,17},{9,25},{17,1},{25,9},{2,18},{10... | collective-permute-start | bytes 2162696 | tf_op jit(solution)/shard_map/ppermute | solution.py:31
  48.6 17.6 %collective-permute-start.11 = (bf16[8,336,128]{2,1,0:T(8,128)(2,1)}, bf16[8,336,128]{2,1,0:T(8,128)(2,1)}, u32[]{:S(2)}, u32[]{:S(2)}) collective-permute-start(bf16[8,336,128]{2,1,0:T(8,128)(2,1)} %pad_maximum_fusion.18), channel_id=1, source_target_pairs={{0,8},{8,0},{16,24},{24,16},{1,9},{9,1},{17,25},{25,17},{2,10},{10... | collective-permute-start | bytes 2064392 | tf_op jit(solution)/shard_map/ppermute | solution.py:31
  68.8 20.0 %collective-permute-start.15 = (bf16[2,2,40,1152]{3,2,0,1:T(8,128)(2,1)S(1)}, bf16[2,2,40,1152]{3,2,0,1:T(8,128)(2,1)S(1)}, u32[]{:S(2)}, u32[]{:S(2)}) collective-permute-start(bf16[2,2,40,1152]{3,2,0,1:T(8,128)(2,1)S(1)} %get-tuple-element.486), channel_id=1, source_target_pairs={{0,4},{1,5},{2,6},{3,7},{4,0},{5,1},{6,2},{7,3},{8,12},{9,13},{10,... | collective-permute-start | bytes 1105928 | tf_op jit(solution)/shard_map/ppermute | solution.py:31
  71.7 17.1 %collective-permute-start.16 = (bf16[2,2,40,1152]{3,2,0,1:T(8,128)(2,1)S(1)}, bf16[2,2,40,1152]{3,2,0,1:T(8,128)(2,1)S(1)}, u32[]{:S(2)}, u32[]{:S(2)}) collective-permute-start(bf16[2,2,40,1152]{3,2,0,1:T(8,128)(2,1)S(1)} %get-tuple-element.484), channel_id=1, source_target_pairs={{0,16},{8,24},{16,0},{24,8},{1,17},{9,25},{17,1},{25,9},{2,18},{10... | collective-permute-start | bytes 1105928 | tf_op jit(solution)/shard_map/ppermute | solution.py:31
  101.6 24.3 %collective-permute-start.23 = (bf16[320,1152]{1,0:T(8,128)(2,1)}, bf16[320,1152]{1,0:T(8,128)(2,1)}, u32[]{:S(2)}, u32[]{:S(2)}) collective-permute-start(bf16[320,1152]{1,0:T(8,128)(2,1)} %bitcast.34.refs_4_), channel_id=1, source_target_pairs={{0,2},{1,3},{2,0},{3,1},{4,6},{5,7},{6,4},{7,5},{8,10},{9,11},{10,... | collective-permute-start | bytes 2211848 | tf_op jit(solution)/shard_map/ppermute | solution.py:31
  101.8 24.2 %collective-permute-start.21 = (bf16[320,1152]{1,0:T(8,128)(2,1)}, bf16[320,1152]{1,0:T(8,128)(2,1)}, u32[]{:S(2)}, u32[]{:S(2)}) collective-permute-start(bf16[320,1152]{1,0:T(8,128)(2,1)} %bitcast.34.refs_4_), channel_id=1, source_target_pairs={{0,1},{1,0},{2,3},{3,2},{4,5},{5,4},{6,7},{7,6},{8,9},{9,8},{10,11... | collective-permute-start | bytes 2211848 | tf_op jit(solution)/shard_map/ppermute | solution.py:31
  102.7 21.1 %collective-permute-start.22 = (bf16[320,1152]{1,0:T(8,128)(2,1)}, bf16[320,1152]{1,0:T(8,128)(2,1)}, u32[]{:S(2)}, u32[]{:S(2)}) collective-permute-start(bf16[320,1152]{1,0:T(8,128)(2,1)} %bitcast.36.refs_5_), channel_id=1, source_target_pairs={{0,1},{1,0},{2,3},{3,2},{4,5},{5,4},{6,7},{7,6},{8,9},{9,8},{10,11... | collective-permute-start | bytes 2211848 | tf_op jit(solution)/shard_map/ppermute | solution.py:31
  104.0 19.8 %collective-permute-start.20 = (bf16[1,4,40,1024]{3,2,1,0:T(8,128)(2,1)}, bf16[1,4,40,1024]{3,2,1,0:T(8,128)(2,1)}, u32[]{:S(2)}, u32[]{:S(2)}) collective-permute-start(bf16[1,4,40,1024]{3,2,1,0:T(8,128)(2,1)} %get-tuple-element.512), channel_id=1, source_target_pairs={{0,4},{1,5},{2,6},{3,7},{4,0},{5,1},{6,2},{7,3},{8,12},{9,13},{10,... | collective-permute-start | bytes 983048 | tf_op jit(solution)/shard_map/ppermute | solution.py:31
  160.1 23.9 %collective-permute-start.28 = (bf16[320,1024]{1,0:T(8,128)(2,1)S(1)}, bf16[320,1024]{1,0:T(8,128)(2,1)S(1)}, u32[]{:S(2)}, u32[]{:S(2)}) collective-permute-start(bf16[320,1024]{1,0:T(8,128)(2,1)S(1)} %bitcast.273), channel_id=1, source_target_pairs={{0,2},{1,3},{2,0},{3,1},{4,6},{5,7},{6,4},{7,5},{8,10},{9,11},{10,... | collective-permute-start | bytes 1966088 | tf_op jit(solution)/shard_map/ppermute | solution.py:31
  185.7 32.9 %collective-permute-start.32 = (bf16[320,2176]{1,0:T(8,128)(2,1)S(1)}, bf16[320,2176]{1,0:T(8,128)(2,1)S(1)}, u32[]{:S(2)}, u32[]{:S(2)}) collective-permute-start(bf16[320,2176]{1,0:T(8,128)(2,1)S(1)} %pad_maximum_fusion.4), channel_id=1, source_target_pairs={{0,2},{1,3},{2,0},{3,1},{4,6},{5,7},{6,4},{7,5},{8,10},{9,11},{10,... | collective-permute-start | bytes 4177928 | tf_op jit(solution)/shard_map/ppermute | solution.py:31
  202.1 17.8 %collective-permute-start.36 = (bf16[320,1152]{1,0:T(8,128)(2,1)}, bf16[320,1152]{1,0:T(8,128)(2,1)}, u32[]{:S(2)}, u32[]{:S(2)}) collective-permute-start(bf16[320,1152]{1,0:T(8,128)(2,1)} %get-tuple-element.300), channel_id=1, source_target_pairs={{0,1},{1,0},{2,3},{3,2},{4,5},{5,4},{6,7},{7,6},{8,9},{9,8},{10,11... | collective-permute-start | bytes 2211848 | tf_op jit(solution)/shard_map/ppermute | solution.py:31
  202.5 19.5 %collective-permute-start.44 = (bf16[320,1024]{1,0:T(8,128)(2,1)}, bf16[320,1024]{1,0:T(8,128)(2,1)}, u32[]{:S(2)}, u32[]{:S(2)}) collective-permute-start(bf16[320,1024]{1,0:T(8,128)(2,1)} %get-tuple-element.335), channel_id=1, source_target_pairs={{0,1},{1,0},{2,3},{3,2},{4,5},{5,4},{6,7},{7,6},{8,9},{9,8},{10,11... | collective-permute-start | bytes 1966088 | tf_op jit(solution)/shard_map/ppermute | solution.py:31
  220.0 21.0 %collective-permute-start.31 = (bf16[320,1152]{1,0:T(8,128)(2,1)}, bf16[320,1152]{1,0:T(8,128)(2,1)S(1)}, u32[]{:S(2)}, u32[]{:S(2)}) collective-permute-start(bf16[320,1152]{1,0:T(8,128)(2,1)} %get-tuple-element.283), channel_id=1, source_target_pairs={{0,1},{1,0},{2,3},{3,2},{4,5},{5,4},{6,7},{7,6},{8,9},{9,8},{10,11... | collective-permute-start | bytes 2211848 | tf_op jit(solution)/shard_map/ppermute | solution.py:31
  222.0 18.5 %collective-permute-start.37 = (bf16[320,1152]{1,0:T(8,128)(2,1)S(1)}, bf16[320,1152]{1,0:T(8,128)(2,1)S(1)}, u32[]{:S(2)}, u32[]{:S(2)}) collective-permute-start(bf16[320,1152]{1,0:T(8,128)(2,1)S(1)} %add_convert_fusion.3), channel_id=1, source_target_pairs={{0,2},{1,3},{2,0},{3,1},{4,6},{5,7},{6,4},{7,5},{8,10},{9,11},{10,... | collective-permute-start | bytes 2211848 | tf_op jit(solution)/shard_map/ppermute | solution.py:31
  225.0 37.4 %collective-permute-start.42 = (bf16[320,1152]{1,0:T(8,128)(2,1)}, bf16[320,1152]{1,0:T(8,128)(2,1)S(1)}, u32[]{:S(2)}, u32[]{:S(2)}) collective-permute-start(bf16[320,1152]{1,0:T(8,128)(2,1)} %get-tuple-element.330), channel_id=1, source_target_pairs={{0,1},{1,0},{2,3},{3,2},{4,5},{5,4},{6,7},{7,6},{8,9},{9,8},{10,11... | collective-permute-start | bytes 2211848 | tf_op jit(solution)/shard_map/ppermute | solution.py:31
  241.3 20.5 %collective-permute-start.38 = (bf16[4,1,40,1152]{3,2,0,1:T(8,128)(2,1)S(1)}, bf16[4,1,40,1152]{3,2,0,1:T(8,128)(2,1)S(1)}, u32[]{:S(2)}, u32[]{:S(2)}) collective-permute-start(bf16[4,1,40,1152]{3,2,0,1:T(8,128)(2,1)S(1)} %get-tuple-element.478), channel_id=1, source_target_pairs={{0,16},{8,24},{16,0},{24,8},{1,17},{9,25},{17,1},{25,9},{2,18},{10... | collective-permute-start | bytes 1105928 | tf_op jit(solution)/shard_map/ppermute | solution.py:31
  244.1 18.4 %collective-permute-start.40 = (bf16[320,1152]{1,0:T(8,128)(2,1)S(1)}, bf16[320,1152]{1,0:T(8,128)(2,1)S(1)}, u32[]{:S(2)}, u32[]{:S(2)}) collective-permute-start(bf16[320,1152]{1,0:T(8,128)(2,1)S(1)} %add_convert_fusion.1), channel_id=1, source_target_pairs={{0,2},{1,3},{2,0},{3,1},{4,6},{5,7},{6,4},{7,5},{8,10},{9,11},{10,... | collective-permute-start | bytes 2211848 | tf_op jit(solution)/shard_map/ppermute | solution.py:31
  266.2 19.0 %collective-permute-start.41 = (bf16[2,2,40,1152]{3,2,1,0:T(8,128)(2,1)S(1)}, bf16[2,2,40,1152]{3,2,1,0:T(8,128)(2,1)S(1)}, u32[]{:S(2)}, u32[]{:S(2)}) collective-permute-start(bf16[2,2,40,1152]{3,2,1,0:T(8,128)(2,1)S(1)} %get-tuple-element.476), channel_id=1, source_target_pairs={{0,4},{1,5},{2,6},{3,7},{4,0},{5,1},{6,2},{7,3},{8,12},{9,13},{10,... | collective-permute-start | bytes 1105928 | tf_op jit(solution)/shard_map/ppermute | solution.py:31
  286.4 24.6 %collective-permute-start.50 = (bf16[320,1024]{1,0:T(8,128)(2,1)S(1)}, bf16[320,1024]{1,0:T(8,128)(2,1)S(1)}, u32[]{:S(2)}, u32[]{:S(2)}) collective-permute-start(bf16[320,1024]{1,0:T(8,128)(2,1)S(1)} %copy-done.95), channel_id=1, source_target_pairs={{0,2},{1,3},{2,0},{3,1},{4,6},{5,7},{6,4},{7,5},{8,10},{9,11},{10,... | collective-permute-start | bytes 1966088 | tf_op jit(solution)/shard_map/ppermute | solution.py:31
  287.8 20.9 %collective-permute-start.49 = (bf16[2,2,40,1152]{3,2,1,0:T(8,128)(2,1)S(1)}, bf16[2,2,40,1152]{3,2,1,0:T(8,128)(2,1)S(1)}, u32[]{:S(2)}, u32[]{:S(2)}) collective-permute-start(bf16[2,2,40,1152]{3,2,1,0:T(8,128)(2,1)S(1)} %bitcast.319), channel_id=1, source_target_pairs={{0,4},{1,5},{2,6},{3,7},{4,0},{5,1},{6,2},{7,3},{8,12},{9,13},{10,... | collective-permute-start | bytes 1105928 | tf_op jit(solution)/shard_map/ppermute | solution.py:31
  290.0 18.7 %collective-permute-start.48 = (bf16[1,4,40,1152]{3,2,1,0:T(8,128)(2,1)S(1)}, bf16[1,4,40,1152]{3,2,1,0:T(8,128)(2,1)S(1)}, u32[]{:S(2)}, u32[]{:S(2)}) collective-permute-start(bf16[1,4,40,1152]{3,2,1,0:T(8,128)(2,1)S(1)} %get-tuple-element.472), channel_id=1, source_target_pairs={{0,8},{8,0},{16,24},{24,16},{1,9},{9,1},{17,25},{25,17},{2,10},{10... | collective-permute-start | bytes 1105928 | tf_op jit(solution)/shard_map/ppermute | solution.py:31
  312.0 16.5 %collective-permute-start.54 = (bf16[1,4,40,1152]{3,2,1,0:T(8,128)(2,1)}, bf16[1,4,40,1152]{3,2,1,0:T(8,128)(2,1)}, u32[]{:S(2)}, u32[]{:S(2)}) collective-permute-start(bf16[1,4,40,1152]{3,2,1,0:T(8,128)(2,1)} %get-tuple-element.468), channel_id=1, source_target_pairs={{0,16},{8,24},{16,0},{24,8},{1,17},{9,25},{17,1},{25,9},{2,18},{10... | collective-permute-start | bytes 1105928 | tf_op jit(solution)/shard_map/ppermute | solution.py:31
  317.3 20.9 %collective-permute-start.53 = (bf16[320,1024]{1,0:T(8,128)(2,1)}, bf16[320,1024]{1,0:T(8,128)(2,1)S(1)}, u32[]{:S(2)}, u32[]{:S(2)}) collective-permute-start(bf16[320,1024]{1,0:T(8,128)(2,1)} %add_convert_fusion.9), channel_id=1, source_target_pairs={{0,2},{1,3},{2,0},{3,1},{4,6},{5,7},{6,4},{7,5},{8,10},{9,11},{10,... | collective-permute-start | bytes 1966088 | tf_op jit(solution)/shard_map/ppermute | solution.py:31
  351.1 19.1 %collective-permute-start.62 = (bf16[2,2,40,1024]{3,2,1,0:T(8,128)(2,1)}, bf16[2,2,40,1024]{3,2,1,0:T(8,128)(2,1)}, u32[]{:S(2)}, u32[]{:S(2)}) collective-permute-start(bf16[2,2,40,1024]{3,2,1,0:T(8,128)(2,1)} %get-tuple-element.500), channel_id=1, source_target_pairs={{0,4},{1,5},{2,6},{3,7},{4,0},{5,1},{6,2},{7,3},{8,12},{9,13},{10,... | collective-permute-start | bytes 983048 | tf_op jit(solution)/shard_map/ppermute | solution.py:31
  353.6 16.7 %collective-permute-start.63 = (bf16[4,1,40,1024]{3,2,0,1:T(8,128)(2,1)}, bf16[4,1,40,1024]{3,2,0,1:T(8,128)(2,1)}, u32[]{:S(2)}, u32[]{:S(2)}) collective-permute-start(bf16[4,1,40,1024]{3,2,0,1:T(8,128)(2,1)} %get-tuple-element.498), channel_id=1, source_target_pairs={{0,8},{8,0},{16,24},{24,16},{1,9},{9,1},{17,25},{25,17},{2,10},{10... | collective-permute-start | bytes 983048 | tf_op jit(solution)/shard_map/ppermute | solution.py:31
  355.3 22.0 %collective-permute-start.61 = (bf16[8,320,128]{2,1,0:T(8,128)(2,1)}, bf16[8,320,128]{2,1,0:T(8,128)(2,1)}, u32[]{:S(2)}, u32[]{:S(2)}) collective-permute-start(bf16[8,320,128]{2,1,0:T(8,128)(2,1)} %add_convert_fusion.7), channel_id=1, source_target_pairs={{0,8},{8,0},{16,24},{24,16},{1,9},{9,1},{17,25},{25,17},{2,10},{10... | collective-permute-start | bytes 1966088 | tf_op jit(solution)/shard_map/ppermute | solution.py:31
  358.0 24.0 %collective-permute-start.57 = (bf16[8,352,128]{2,1,0:T(8,128)(2,1)}, bf16[8,352,128]{2,1,0:T(8,128)(2,1)}, u32[]{:S(2)}, u32[]{:S(2)}) collective-permute-start(bf16[8,352,128]{2,1,0:T(8,128)(2,1)} %add_convert_fusion.5), channel_id=1, source_target_pairs={{0,2},{1,3},{2,0},{3,1},{4,6},{5,7},{6,4},{7,5},{8,10},{9,11},{10,... | collective-permute-start | bytes 2162696 | tf_op jit(solution)/shard_map/ppermute | solution.py:31
  360.6 21.4 %collective-permute-start.59 = (bf16[8,352,128]{2,1,0:T(8,128)(2,1)}, bf16[8,352,128]{2,1,0:T(8,128)(2,1)}, u32[]{:S(2)}, u32[]{:S(2)}) collective-permute-start(bf16[8,352,128]{2,1,0:T(8,128)(2,1)} %add_convert_fusion.4), channel_id=1, source_target_pairs={{0,16},{8,24},{16,0},{24,8},{1,17},{9,25},{17,1},{25,9},{2,18},{10... | collective-permute-start | bytes 2162696 | tf_op jit(solution)/shard_map/ppermute | solution.py:31
  385.7 22.9 %collective-permute-start.65 = (bf16[4,352,128]{2,1,0:T(8,128)(2,1)S(1)}, bf16[4,352,128]{2,1,0:T(8,128)(2,1)S(1)}, u32[]{:S(2)}, u32[]{:S(2)}) collective-permute-start(bf16[4,352,128]{2,1,0:T(8,128)(2,1)S(1)} %add_convert_fusion.13), channel_id=1, source_target_pairs={{0,8},{8,0},{16,24},{24,16},{1,9},{9,1},{17,25},{25,17},{2,10},{10... | collective-permute-start | bytes 1081352 | tf_op jit(solution)/shard_map/ppermute | solution.py:31
  387.6 21.0 %collective-permute-start.64 = (bf16[4,352,128]{2,1,0:T(8,128)(2,1)S(1)}, bf16[4,352,128]{2,1,0:T(8,128)(2,1)S(1)}, u32[]{:S(2)}, u32[]{:S(2)}) collective-permute-start(bf16[4,352,128]{2,1,0:T(8,128)(2,1)S(1)} %add_convert_fusion.14), channel_id=1, source_target_pairs={{0,16},{8,24},{16,0},{24,8},{1,17},{9,25},{17,1},{25,9},{2,18},{10... | collective-permute-start | bytes 1081352 | tf_op jit(solution)/shard_map/ppermute | solution.py:31
  (192 other events, 1618.6 us)

commit v5 on v4

--- a/solution.py
+++ b/solution.py
@@ -657,24 +657,22 @@
     )(table, tokens, gain.reshape(1, features), x1_grad, dheads, *owns, *fars)
 
 
-def choose(refs, which):
-    value = refs[0][...]
-    for i in range(1, len(refs)):
-        value = jnp.where(which == i, refs[i][...], value)
-    return value
-
-
 def expert_body(expert_ref, *refs, count, apart):
     x_refs, up_refs, refs = refs[:count], refs[count:apart], refs[apart:]
     router_ref, gate_w, up_w, down_w = refs[:4]
-    y_refs, dx_refs = refs[-2 * count - 5 : -count - 5], refs[-count - 5 : -5]
-    x_out, dy_ref, hidden_ref, dgate_ref, dup_ref = refs[-5:]
+    y_refs, dx_refs = refs[-2 * count - 6 : -count - 6], refs[-count - 6 : -6]
+    x_out, dy_ref, hidden_ref, dgate_ref, dup_ref, up_scr = refs[-6:]
     piece = pl.program_id(0)
     features = x_out.shape[1]
-    x = choose(x_refs, piece)
-    up = choose(up_refs, piece) if up_refs else x[:, features:]
-    x = x[:, :features]
-    x_out[...] = x
+    for i in range(count):
+
+        @pl.when(piece == i)
+        def _(i=i):
+            x_out[...] = x_refs[i][:, :features]
+            up_ref = up_refs[i] if up_refs else x_refs[i].at[:, features:]
+            up_scr[...] = up_ref[...]
+
+    x, up = x_out[...], up_scr[...]
     logits = mm(x, router_ref[...])
     lane = lax.broadcasted_iota(jnp.int32, logits.shape, 1)
     other_id = up[:, features : features + 1].astype(jnp.int32)
@@ -739,6 +737,7 @@
             out_specs=[pl.BlockSpec((rows, features), lambda i, e: (0, 0))] * count
             + [pl.BlockSpec((rows, features + LANES), lambda i, e: (0, 0))] * count
             + [kept_spec(cols) for cols in kept_cols],
+            scratch_shapes=[pltpu.VMEM((rows, features + LANES), BF)],
         ),
         out_shape=[jax.ShapeDtypeStruct((rows, features), BF)] * count
         + [jax.ShapeDtypeStruct((rows, features + LANES), BF)] * count
@@ -807,7 +806,7 @@
             acc_ref[pl.ds(n * rows + first, chunk), :] = total
             return tuple(grown)
 
-        return lax.fori_loop(start // chunk, stop // chunk, step, cols)
+        return lax.fori_loop(start // chunk, stop // chunk, step, cols, unroll=2)
 
     def matrix(m, grads_ref, pieces):
         cols = tuple(jnp.zeros((8, LANES), F32) for _ in range(2 * pairs))

time: 520 us -> 519 us (level)
  no operation moved by 1% of the time
where the time goes in v5:
time: 519 us; the launch traced here: 510 us
  waiting for transfers between devices  179 us (34%)
  Pallas kernels  123 us (24%)
  starting transfers between devices  83.6 us (16%)
  other arithmetic  76.1 us (15%)
  local copies, waits for them, and re-layouts  43.3 us (8%)
  between operations  5.77 us (1%)
    ppermute x92, waiting for transfers between devices, from_partner(): return lax.ppermute(value, axis, pairs)  179 us
    ppermute x92, starting transfers between devices, from_partner(): return lax.ppermute(value, axis, pairs)  83.6 us
    pallas_call x3, Pallas kernels, expert_call(): pl.pallas_call(functools.partial(expert_body, count=count, apart=count +...  46.4 us
    pallas_call x3, Pallas kernels, expert_grad_call(): pl.pallas_call(expert_grad_body, grid=(features // size,), in_specs=[pl.B...  20.9 us
    unnamed x274, local copies, waits for them, and re-layouts  16.2 us
    concatenate x21, other arithmetic, grow(): return jnp.concatenate([blocks, got], axis=axis)  14.1 us
    pallas_call x1, Pallas kernels, attend_call(): pl.pallas_call(body, in_specs=[smem()] + [vmem()] * 9, out_specs=[vmem()]...  11.1 us
    sub x4, other arithmetic, factored(): return weight - adafactor_step(gradient, row_stats, col_stats, mean_rows)  10.8 us
  transfers between devices with their start and end apart: 92, of which 37 were waited for; matrix products, arithmetic and copies ran while one was open for 15% of the time, Pallas kernels for 20%

profile of v5, /device:TPU:0, one launch (start us, length us, event | category | flops | bytes accessed | tf_op | source)
XLA Modules:
  0.0 510.4 jit_solution(6660154839058783786)
XLA Ops:
  3.6 4.1 collective-permute-start
  11.6 8.3 %collective-permute-done = bf16[1,1040,128]{2,1,0:T(8,128)(2,1)S(1)} collective-permute-done((bf16[1,1040,128]{2,1,0:T(8,128)(2,1)S(1)}, bf16[1,1040,128]{2,1,0:T(8,128)(2,1)S(1)}, u32[]{:S(2)}, u32[]{:S(2)}) %collective-permute-start) | collective-permute-done | bytes 266272 | tf_op jit(solution)/shard_map/ppermute | solution.py:31
  31.9 7.2 %collective-permute-done.2 = bf16[1,4,40,1152]{3,2,1,0:T(8,128)(2,1)S(1)} collective-permute-done((bf16[1,4,40,1152]{3,2,1,0:T(8,128)(2,1)S(1)}, bf16[1,4,40,1152]{3,2,1,0:T(8,128)(2,1)S(1)}, u32[]{:S(2)}, u32[]{:S(2)}) %collective-permute-start.2) | collective-permute-done | bytes 368672 | tf_op jit(solution)/shard_map/ppermute | solution.py:31
  39.2 5.6 %collective-permute-done.3 = bf16[1,4,40,1152]{3,2,1,0:T(8,128)(2,1)S(1)} collective-permute-done((bf16[1,4,40,1152]{3,2,1,0:T(8,128)(2,1)S(1)}, bf16[1,4,40,1152]{3,2,1,0:T(8,128)(2,1)S(1)}, u32[]{:S(2)}, u32[]{:S(2)}) %collective-permute-start.3) | collective-permute-done | bytes 368672 | tf_op jit(solution)/shard_map/ppermute | solution.py:31
  50.6 12.1 %collective-permute-done.9 = bf16[8,352,128]{2,1,0:T(8,128)(2,1)} collective-permute-done((bf16[8,352,128]{2,1,0:T(8,128)(2,1)S(1)}, bf16[8,352,128]{2,1,0:T(8,128)(2,1)}, u32[]{:S(2)}, u32[]{:S(2)}) %collective-permute-start.9) | collective-permute-done | bytes 720928 | tf_op jit(solution)/shard_map/ppermute | solution.py:31
  72.4 11.1 %attend.1 = (bf16[256,1024]{1,0:T(8,128)(2,1)S(1)}, bf16[3,8,256,128]{3,2,1,0:T(8,128)(2,1)S(1)}, f32[16,256,256]{2,1,0:T(8,128)S(1)}, bf16[8,256,128]{2,1,0:T(8,128)(2,1)S(1)}) custom-call(s32[49]{0:T(128)S(1)} %pad_add_fusion.table_ref, bf16[256,1024]{1,0:T(8,128)(2,1)S(1)} %copy-done.39, f32[1,1024]{1,0:T(1,128)S(1)} %bitcast.283, ...), custom_call_target="tpu_custom_call" | custom-call | flops 18447998976 | bytes 59040000 | tf_op jit(solution)/shard_map/attend/pallas_call | solution.py:253
  93.8 5.7 %collective-permute-done.18 = bf16[4,1,40,1152]{3,2,0,1:T(8,128)(2,1)S(1)} collective-permute-done((bf16[4,1,40,1152]{3,2,0,1:T(8,128)(2,1)S(1)}, bf16[4,1,40,1152]{3,2,0,1:T(8,128)(2,1)S(1)}, u32[]{:S(2)}, u32[]{:S(2)}) %collective-permute-start.18) | collective-permute-done | bytes 368672 | tf_op jit(solution)/shard_map/ppermute | solution.py:31
  111.4 12.4 %collective-permute-done.20 = bf16[1,4,40,1024]{3,2,1,0:T(8,128)(2,1)} collective-permute-done((bf16[1,4,40,1024]{3,2,1,0:T(8,128)(2,1)}, bf16[1,4,40,1024]{3,2,1,0:T(8,128)(2,1)}, u32[]{:S(2)}, u32[]{:S(2)}) %collective-permute-start.20) | collective-permute-done | bytes 327712 | tf_op jit(solution)/shard_map/ppermute | solution.py:31
  130.1 12.4 %collective-permute-done.24 = bf16[2,2,40,1024]{3,2,0,1:T(8,128)(2,1)S(1)} collective-permute-done((bf16[2,2,40,1024]{3,2,0,1:T(8,128)(2,1)S(1)}, bf16[2,2,40,1024]{3,2,0,1:T(8,128)(2,1)S(1)}, u32[]{:S(2)}, u32[]{:S(2)}) %collective-permute-start.24) | collective-permute-done | bytes 327712 | tf_op jit(solution)/shard_map/ppermute | solution.py:31
  160.5 22.3 %expert.3 = (bf16[320,1024]{1,0:T(8,128)(2,1)S(1)}, bf16[320,1024]{1,0:T(8,128)(2,1)S(1)}, bf16[320,1024]{1,0:T(8,128)(2,1)}, bf16[320,1024]{1,0:T(8,128)(2,1)S(...) custom-call(s32[1]{0:T(128)} %bitcast.61.expert_ref, ...), custom_call_target="tpu_custom_call" | custom-call | flops 23060000768 | bytes 73800000 | tf_op jit(solution)/shard_map/expert/pallas_call | solution.py:730
  187.1 12.2 %expert.4 = (bf16[320,1024]{1,0:T(8,128)(2,1)S(1)}, bf16[320,1024]{1,0:T(8,128)(2,1)S(1)}, bf16[320,1152]{1,0:T(8,128)(2,1)S(1)}, bf16[320,1152]{1,0:T(8,128)(2,...) custom-call(s32[1]{0:T(128)} %bitcast.61.expert_ref, ...), custom_call_target="tpu_custom_call", output_to_operand_aliasing={{4}: (9, {}), {5}: (10, {}), {6}: (11, {}), {7}: (12, {}), ... | custom-call | flops 1152999936 | bytes 3690000 | tf_op jit(solution)/shard_map/expert/pallas_call | solution.py:730
  202.4 16.0 %collective-permute-done.32.refs_0_ = bf16[320,2176]{1,0:T(8,128)(2,1)S(1)} collective-permute-done((bf16[320,2176]{1,0:T(8,128)(2,1)S(1)}, bf16[320,2176]{1,0:T(8,128)(2,1)S(1)}, u32[]{:S(2)}, u32[]{:S(2)}) %collective-permute-start.32) | collective-permute-done | bytes 1392672 | tf_op jit(solution)/shard_map/ppermute | solution.py:31
  227.0 11.9 %expert.5 = (bf16[320,1024]{1,0:T(8,128)(2,1)S(1)}, bf16[320,1024]{1,0:T(8,128)(2,1)S(1)}, bf16[320,1152]{1,0:T(8,128)(2,1)S(1)}, bf16[320,1152]{1,0:T(8,128)(2,...) custom-call(s32[1]{0:T(128)} %bitcast.61.expert_ref, ...), custom_call_target="tpu_custom_call", output_to_operand_aliasing={{4}: (7, {}), {5}: (8, {}), {6}: (9, {}), {7}: (10, {}), {8... | custom-call | flops 1152999936 | bytes 3690000 | tf_op jit(solution)/shard_map/expert/pallas_call | solution.py:730
  247.7 6.9 %expert_grad.3 = f32[704,1024]{1,0:T(8,128)} custom-call(bf16[2560,704]{1,0:T(8,128)(2,1)S(1)} %copy-done.4, bf16[2560,1024]{1,0:T(8,128)(2,1)S(1)} %copy-done.2), custom_call_target="tpu_custom_call" | custom-call | flops 10376999936 | bytes 33210000 | tf_op jit(solution)/shard_map/expert_grad/pallas_call | solution.py:763
  254.6 6.9 %expert_grad.4 = f32[704,1024]{1,0:T(8,128)} custom-call(bf16[2560,704]{1,0:T(8,128)(2,1)S(1)} %copy-done.5, bf16[2560,1024]{1,0:T(8,128)(2,1)S(1)} %copy-done.2), custom_call_target="tpu_custom_call" | custom-call | flops 10376999936 | bytes 33210000 | tf_op jit(solution)/shard_map/expert_grad/pallas_call | solution.py:763
  269.4 7.1 %expert_grad.5 = f32[704,1024]{1,0:T(8,128)} custom-call(bf16[2560,704]{1,0:T(8,128)(2,1)S(1)} %copy-done.3, bf16[2560,1024]{1,0:T(8,128)(2,1)S(1)} %bitcast.264), custom_call_target="tpu_custom_call" | custom-call | flops 10376999936 | bytes 33210000 | tf_op jit(solution)/shard_map/expert_grad/pallas_call | solution.py:763
  277.0 8.0 %collective-permute-done.41 = bf16[2,2,40,1152]{3,2,1,0:T(8,128)(2,1)S(1)} collective-permute-done((bf16[2,2,40,1152]{3,2,1,0:T(8,128)(2,1)S(1)}, bf16[2,2,40,1152]{3,2,1,0:T(8,128)(2,1)S(1)}, u32[]{:S(2)}, u32[]{:S(2)}) %collective-permute-start.41) | collective-permute-done | bytes 368672 | tf_op jit(solution)/shard_map/ppermute | solution.py:31
  291.7 16.8 %collective-permute-done.49 = bf16[2,2,40,1152]{3,2,1,0:T(8,128)(2,1)S(1)} collective-permute-done((bf16[2,2,40,1152]{3,2,1,0:T(8,128)(2,1)S(1)}, bf16[2,2,40,1152]{3,2,1,0:T(8,128)(2,1)S(1)}, u32[]{:S(2)}, u32[]{:S(2)}) %collective-permute-start.49) | collective-permute-done | bytes 368672 | tf_op jit(solution)/shard_map/ppermute | solution.py:31
  317.2 5.0 bitcast_subtract_fusion
  331.2 6.0 %mid.1 = (f32[256,1024]{1,0:T(8,128)S(1)}, f32[256,128]{1,0:T(8,128)S(1)}, f32[1,1024]{1,0:T(1,128)S(1)}, f32[128,1024]{1,0:T(8,128)S(1)}, f32[16,256,128]{2,1,0...) custom-call(s32[49]{0:T(128)S(1)} %pad_add_fusion.table_ref, s32[16]{0:T(128)S(1)} %copy-done.34, ...), custom_call_target="tpu_custom_call" | custom-call | flops 8071000064 | bytes 25830000 | tf_op jit(solution)/shard_map/mid/pallas_call | solution.py:469
  337.9 10.8 %attend_back.1 = (f32[16,352,128]{2,1,0:T(8,128)S(1)}, f32[16,352,128]{2,1,0:T(8,128)S(1)}, f32[16,320,128]{2,1,0:T(8,128)S(1)}, bf16[16,352,128]{2,1,0:T(8,128)...) custom-call(s32[49]{0:T(128)S(1)} %pad_add_fusion.table_ref, ...), custom_call_target="tpu_custom_call" | custom-call | flops 13836000256 | bytes 44280000 | tf_op jit(solution)/shard_map/attend_back/pallas_call | solution.py:591
  361.5 7.3 %tokens_back.1 = (bf16[256,1024]{1,0:T(8,128)(2,1)}, f32[1,1024]{1,0:T(1,128)S(1)}) custom-call(s32[49]{0:T(128)S(1)} %pad_add_fusion.table_ref, bf16[256,1024]{1,0:T(8,128)(2,1)S(1)} %copy-done.40, f32[1,1024]{1,0:T(1,128)S(1)} %bitcast.284, f32[256,1024]{1,0:T(8,128)S(1)} %get-tuple-element.387.x1_grad_ref, ...), custom_call_target="tpu_custom_call" | custom-call | flops 11530000384 | bytes 36900000 | tf_op jit(solution)/shard_map/tokens_back/pallas_call | solution.py:645
  369.9 7.0 %collective-permute-done.61 = bf16[8,320,128]{2,1,0:T(8,128)(2,1)} collective-permute-done((bf16[8,320,128]{2,1,0:T(8,128)(2,1)}, bf16[8,320,128]{2,1,0:T(8,128)(2,1)}, u32[]{:S(2)}, u32[]{:S(2)}) %collective-permute-start.61) | collective-permute-done | bytes 655392 | tf_op jit(solution)/shard_map/ppermute | solution.py:31
  376.9 4.8 collective-permute-done.57
  394.9 9.8 %collective-permute-done.66 = bf16[4,320,128]{2,1,0:T(8,128)(2,1)S(1)} collective-permute-done((bf16[4,320,128]{2,1,0:T(8,128)(2,1)S(1)}, bf16[4,320,128]{2,1,0:T(8,128)(2,1)S(1)}, u32[]{:S(2)}, u32[]{:S(2)}) %collective-permute-start.66) | collective-permute-done | bytes 327712 | tf_op jit(solution)/shard_map/ppermute | solution.py:31
  404.7 3.6 collective-permute-done.69
  432.9 8.0 %collective-permute-done.76 = bf16[1,1024,128]{2,1,0:T(8,128)(2,1)} collective-permute-done((bf16[1,1024,128]{2,1,0:T(8,128)(2,1)}, bf16[1,1024,128]{2,1,0:T(8,128)(2,1)}, u32[]{:S(2)}, u32[]{:S(2)}) %collective-permute-start.76) | collective-permute-done | bytes 262176 | tf_op jit(solution)/shard_map/ppermute | solution.py:31
  445.2 5.9 %block_out.1 = bf16[256,1024]{1,0:T(8,128)(2,1)} custom-call(s32[16]{0:T(128)S(1)} %copy-done.34, f32[256,1024]{1,0:T(8,128)S(1)} %copy-done.46, f32[256,128]{1,0:T(8,128)S(1)} %copy-done.58, bf16[8,40,1024]{2,1,0:T(8,128)(2,1)S(1)} %bitcast.276, bf16[8,40,1024]{2,1,0:T(8,128)(2,1)S(1)} %bitcast.278, s32[2,256]{1,0:T(2,128)S(1)} %fusion.41.ids_ref), custom_call_target="tpu_custom_call" | custom-call | flops 8071000064 | bytes 25830000 | tf_op jit(solution)/shard_map/block_out/pallas_call | solution.py:512
  465.5 4.5 collective-permute-done.85
  484.1 3.8 collective-permute-done.87
  493.0 3.9 collective-permute-done.91.far_v
  497.0 10.2 %finish.1 = (f32[3,1024,1024]{2,1,0:T(8,128)}, f32[1024,1024]{1,0:T(8,128)}, f32[4,8,1024]{2,1,0:T(8,128)S(1)}, f32[4,8,1,128]{3,2,1,0:T(1,128)S(1)}, f32[4,256,128]{2,1,0:T(8,128)S(1)}) custom-call(s32[49]{0:T(128)S(1)} %pad_add_fusion.table_ref, s32[2]{0:T(128)S(1)} %pad_add_fusion.3.place_ref, bf16[16,352,128]{2,1,0:T(8,128)(2,1)S(1)} %pad_maximum_fusion.2.own_q, ...), custom_call_target="tpu_custom_call" | custom-call | flops 11530000384 | bytes 36900000 | tf_op jit(solution)/shard_map/finish/pallas_call | solution.py:879
  (638 shorter events, 226.9 us)
Async XLA Ops:
  25.8 19.0 %collective-permute-start.3 = (bf16[1,4,40,1152]{3,2,1,0:T(8,128)(2,1)S(1)}, bf16[1,4,40,1152]{3,2,1,0:T(8,128)(2,1)S(1)}, u32[]{:S(2)}, u32[]{:S(2)}) collective-permute-start(bf16[1,4,40,1152]{3,2,1,0:T(8,128)(2,1)S(1)} %get-tuple-element.488), channel_id=1, source_target_pairs={{0,4},{1,5},{2,6},{3,7},{4,0},{5,1},{6,2},{7,3},{8,12},{9,13},{10,... | collective-permute-start | bytes 1105928 | tf_op jit(solution)/shard_map/ppermute | solution.py:31
  45.6 17.1 %collective-permute-start.9 = (bf16[8,352,128]{2,1,0:T(8,128)(2,1)S(1)}, bf16[8,352,128]{2,1,0:T(8,128)(2,1)}, u32[]{:S(2)}, u32[]{:S(2)}) collective-permute-start(bf16[8,352,128]{2,1,0:T(8,128)(2,1)S(1)} %pad_maximum_fusion.14), channel_id=1, source_target_pairs={{0,2},{1,3},{2,0},{3,1},{4,6},{5,7},{6,4},{7,5},{8,10},{9,11},{10,... | collective-permute-start | bytes 2162696 | tf_op jit(solution)/shard_map/ppermute | solution.py:31
  47.1 17.0 %collective-permute-start.10 = (bf16[8,352,128]{2,1,0:T(8,128)(2,1)}, bf16[8,352,128]{2,1,0:T(8,128)(2,1)}, u32[]{:S(2)}, u32[]{:S(2)}) collective-permute-start(bf16[8,352,128]{2,1,0:T(8,128)(2,1)} %pad_maximum_fusion.15), channel_id=1, source_target_pairs={{0,16},{8,24},{16,0},{24,8},{1,17},{9,25},{17,1},{25,9},{2,18},{10... | collective-permute-start | bytes 2162696 | tf_op jit(solution)/shard_map/ppermute | solution.py:31
  48.6 17.6 %collective-permute-start.11 = (bf16[8,336,128]{2,1,0:T(8,128)(2,1)}, bf16[8,336,128]{2,1,0:T(8,128)(2,1)}, u32[]{:S(2)}, u32[]{:S(2)}) collective-permute-start(bf16[8,336,128]{2,1,0:T(8,128)(2,1)} %pad_maximum_fusion.18), channel_id=1, source_target_pairs={{0,8},{8,0},{16,24},{24,16},{1,9},{9,1},{17,25},{25,17},{2,10},{10... | collective-permute-start | bytes 2064392 | tf_op jit(solution)/shard_map/ppermute | solution.py:31
  68.8 20.0 %collective-permute-start.15 = (bf16[2,2,40,1152]{3,2,0,1:T(8,128)(2,1)S(1)}, bf16[2,2,40,1152]{3,2,0,1:T(8,128)(2,1)S(1)}, u32[]{:S(2)}, u32[]{:S(2)}) collective-permute-start(bf16[2,2,40,1152]{3,2,0,1:T(8,128)(2,1)S(1)} %get-tuple-element.486), channel_id=1, source_target_pairs={{0,4},{1,5},{2,6},{3,7},{4,0},{5,1},{6,2},{7,3},{8,12},{9,13},{10,... | collective-permute-start | bytes 1105928 | tf_op jit(solution)/shard_map/ppermute | solution.py:31
  71.7 17.1 %collective-permute-start.16 = (bf16[2,2,40,1152]{3,2,0,1:T(8,128)(2,1)S(1)}, bf16[2,2,40,1152]{3,2,0,1:T(8,128)(2,1)S(1)}, u32[]{:S(2)}, u32[]{:S(2)}) collective-permute-start(bf16[2,2,40,1152]{3,2,0,1:T(8,128)(2,1)S(1)} %get-tuple-element.484), channel_id=1, source_target_pairs={{0,16},{8,24},{16,0},{24,8},{1,17},{9,25},{17,1},{25,9},{2,18},{10... | collective-permute-start | bytes 1105928 | tf_op jit(solution)/shard_map/ppermute | solution.py:31
  101.6 24.3 %collective-permute-start.23 = (bf16[320,1152]{1,0:T(8,128)(2,1)}, bf16[320,1152]{1,0:T(8,128)(2,1)}, u32[]{:S(2)}, u32[]{:S(2)}) collective-permute-start(bf16[320,1152]{1,0:T(8,128)(2,1)} %bitcast.34.refs_4_), channel_id=1, source_target_pairs={{0,2},{1,3},{2,0},{3,1},{4,6},{5,7},{6,4},{7,5},{8,10},{9,11},{10,... | collective-permute-start | bytes 2211848 | tf_op jit(solution)/shard_map/ppermute | solution.py:31
  101.8 24.2 %collective-permute-start.21 = (bf16[320,1152]{1,0:T(8,128)(2,1)}, bf16[320,1152]{1,0:T(8,128)(2,1)}, u32[]{:S(2)}, u32[]{:S(2)}) collective-permute-start(bf16[320,1152]{1,0:T(8,128)(2,1)} %bitcast.34.refs_4_), channel_id=1, source_target_pairs={{0,1},{1,0},{2,3},{3,2},{4,5},{5,4},{6,7},{7,6},{8,9},{9,8},{10,11... | collective-permute-start | bytes 2211848 | tf_op jit(solution)/shard_map/ppermute | solution.py:31
  102.7 21.1 %collective-permute-start.22 = (bf16[320,1152]{1,0:T(8,128)(2,1)}, bf16[320,1152]{1,0:T(8,128)(2,1)}, u32[]{:S(2)}, u32[]{:S(2)}) collective-permute-start(bf16[320,1152]{1,0:T(8,128)(2,1)} %bitcast.36.refs_5_), channel_id=1, source_target_pairs={{0,1},{1,0},{2,3},{3,2},{4,5},{5,4},{6,7},{7,6},{8,9},{9,8},{10,11... | collective-permute-start | bytes 2211848 | tf_op jit(solution)/shard_map/ppermute | solution.py:31
  104.0 19.8 %collective-permute-start.20 = (bf16[1,4,40,1024]{3,2,1,0:T(8,128)(2,1)}, bf16[1,4,40,1024]{3,2,1,0:T(8,128)(2,1)}, u32[]{:S(2)}, u32[]{:S(2)}) collective-permute-start(bf16[1,4,40,1024]{3,2,1,0:T(8,128)(2,1)} %get-tuple-element.512), channel_id=1, source_target_pairs={{0,4},{1,5},{2,6},{3,7},{4,0},{5,1},{6,2},{7,3},{8,12},{9,13},{10,... | collective-permute-start | bytes 983048 | tf_op jit(solution)/shard_map/ppermute | solution.py:31
  160.1 23.6 %collective-permute-start.28 = (bf16[320,1024]{1,0:T(8,128)(2,1)S(1)}, bf16[320,1024]{1,0:T(8,128)(2,1)S(1)}, u32[]{:S(2)}, u32[]{:S(2)}) collective-permute-start(bf16[320,1024]{1,0:T(8,128)(2,1)S(1)} %bitcast.273), channel_id=1, source_target_pairs={{0,2},{1,3},{2,0},{3,1},{4,6},{5,7},{6,4},{7,5},{8,10},{9,11},{10,... | collective-permute-start | bytes 1966088 | tf_op jit(solution)/shard_map/ppermute | solution.py:31
  185.4 32.9 %collective-permute-start.32 = (bf16[320,2176]{1,0:T(8,128)(2,1)S(1)}, bf16[320,2176]{1,0:T(8,128)(2,1)S(1)}, u32[]{:S(2)}, u32[]{:S(2)}) collective-permute-start(bf16[320,2176]{1,0:T(8,128)(2,1)S(1)} %pad_maximum_fusion.4), channel_id=1, source_target_pairs={{0,2},{1,3},{2,0},{3,1},{4,6},{5,7},{6,4},{7,5},{8,10},{9,11},{10,... | collective-permute-start | bytes 4177928 | tf_op jit(solution)/shard_map/ppermute | solution.py:31
  201.8 17.8 %collective-permute-start.36 = (bf16[320,1152]{1,0:T(8,128)(2,1)}, bf16[320,1152]{1,0:T(8,128)(2,1)}, u32[]{:S(2)}, u32[]{:S(2)}) collective-permute-start(bf16[320,1152]{1,0:T(8,128)(2,1)} %get-tuple-element.300), channel_id=1, source_target_pairs={{0,1},{1,0},{2,3},{3,2},{4,5},{5,4},{6,7},{7,6},{8,9},{9,8},{10,11... | collective-permute-start | bytes 2211848 | tf_op jit(solution)/shard_map/ppermute | solution.py:31
  202.2 19.5 %collective-permute-start.44 = (bf16[320,1024]{1,0:T(8,128)(2,1)}, bf16[320,1024]{1,0:T(8,128)(2,1)}, u32[]{:S(2)}, u32[]{:S(2)}) collective-permute-start(bf16[320,1024]{1,0:T(8,128)(2,1)} %get-tuple-element.335), channel_id=1, source_target_pairs={{0,1},{1,0},{2,3},{3,2},{4,5},{5,4},{6,7},{7,6},{8,9},{9,8},{10,11... | collective-permute-start | bytes 1966088 | tf_op jit(solution)/shard_map/ppermute | solution.py:31
  219.7 21.0 %collective-permute-start.31 = (bf16[320,1152]{1,0:T(8,128)(2,1)}, bf16[320,1152]{1,0:T(8,128)(2,1)S(1)}, u32[]{:S(2)}, u32[]{:S(2)}) collective-permute-start(bf16[320,1152]{1,0:T(8,128)(2,1)} %get-tuple-element.283), channel_id=1, source_target_pairs={{0,1},{1,0},{2,3},{3,2},{4,5},{5,4},{6,7},{7,6},{8,9},{9,8},{10,11... | collective-permute-start | bytes 2211848 | tf_op jit(solution)/shard_map/ppermute | solution.py:31
  221.7 18.5 %collective-permute-start.37 = (bf16[320,1152]{1,0:T(8,128)(2,1)S(1)}, bf16[320,1152]{1,0:T(8,128)(2,1)S(1)}, u32[]{:S(2)}, u32[]{:S(2)}) collective-permute-start(bf16[320,1152]{1,0:T(8,128)(2,1)S(1)} %add_convert_fusion.3), channel_id=1, source_target_pairs={{0,2},{1,3},{2,0},{3,1},{4,6},{5,7},{6,4},{7,5},{8,10},{9,11},{10,... | collective-permute-start | bytes 2211848 | tf_op jit(solution)/shard_map/ppermute | solution.py:31
  224.7 37.4 %collective-permute-start.42 = (bf16[320,1152]{1,0:T(8,128)(2,1)}, bf16[320,1152]{1,0:T(8,128)(2,1)S(1)}, u32[]{:S(2)}, u32[]{:S(2)}) collective-permute-start(bf16[320,1152]{1,0:T(8,128)(2,1)} %get-tuple-element.330), channel_id=1, source_target_pairs={{0,1},{1,0},{2,3},{3,2},{4,5},{5,4},{6,7},{7,6},{8,9},{9,8},{10,11... | collective-permute-start | bytes 2211848 | tf_op jit(solution)/shard_map/ppermute | solution.py:31
  241.0 20.5 %collective-permute-start.38 = (bf16[4,1,40,1152]{3,2,0,1:T(8,128)(2,1)S(1)}, bf16[4,1,40,1152]{3,2,0,1:T(8,128)(2,1)S(1)}, u32[]{:S(2)}, u32[]{:S(2)}) collective-permute-start(bf16[4,1,40,1152]{3,2,0,1:T(8,128)(2,1)S(1)} %get-tuple-element.478), channel_id=1, source_target_pairs={{0,16},{8,24},{16,0},{24,8},{1,17},{9,25},{17,1},{25,9},{2,18},{10... | collective-permute-start | bytes 1105928 | tf_op jit(solution)/shard_map/ppermute | solution.py:31
  243.8 18.4 %collective-permute-start.40 = (bf16[320,1152]{1,0:T(8,128)(2,1)S(1)}, bf16[320,1152]{1,0:T(8,128)(2,1)S(1)}, u32[]{:S(2)}, u32[]{:S(2)}) collective-permute-start(bf16[320,1152]{1,0:T(8,128)(2,1)S(1)} %add_convert_fusion.1), channel_id=1, source_target_pairs={{0,2},{1,3},{2,0},{3,1},{4,6},{5,7},{6,4},{7,5},{8,10},{9,11},{10,... | collective-permute-start | bytes 2211848 | tf_op jit(solution)/shard_map/ppermute | solution.py:31
  265.9 19.0 %collective-permute-start.41 = (bf16[2,2,40,1152]{3,2,1,0:T(8,128)(2,1)S(1)}, bf16[2,2,40,1152]{3,2,1,0:T(8,128)(2,1)S(1)}, u32[]{:S(2)}, u32[]{:S(2)}) collective-permute-start(bf16[2,2,40,1152]{3,2,1,0:T(8,128)(2,1)S(1)} %get-tuple-element.476), channel_id=1, source_target_pairs={{0,4},{1,5},{2,6},{3,7},{4,0},{5,1},{6,2},{7,3},{8,12},{9,13},{10,... | collective-permute-start | bytes 1105928 | tf_op jit(solution)/shard_map/ppermute | solution.py:31
  286.1 24.6 %collective-permute-start.50 = (bf16[320,1024]{1,0:T(8,128)(2,1)S(1)}, bf16[320,1024]{1,0:T(8,128)(2,1)S(1)}, u32[]{:S(2)}, u32[]{:S(2)}) collective-permute-start(bf16[320,1024]{1,0:T(8,128)(2,1)S(1)} %copy-done.95), channel_id=1, source_target_pairs={{0,2},{1,3},{2,0},{3,1},{4,6},{5,7},{6,4},{7,5},{8,10},{9,11},{10,... | collective-permute-start | bytes 1966088 | tf_op jit(solution)/shard_map/ppermute | solution.py:31
  287.5 20.9 %collective-permute-start.49 = (bf16[2,2,40,1152]{3,2,1,0:T(8,128)(2,1)S(1)}, bf16[2,2,40,1152]{3,2,1,0:T(8,128)(2,1)S(1)}, u32[]{:S(2)}, u32[]{:S(2)}) collective-permute-start(bf16[2,2,40,1152]{3,2,1,0:T(8,128)(2,1)S(1)} %bitcast.319), channel_id=1, source_target_pairs={{0,4},{1,5},{2,6},{3,7},{4,0},{5,1},{6,2},{7,3},{8,12},{9,13},{10,... | collective-permute-start | bytes 1105928 | tf_op jit(solution)/shard_map/ppermute | solution.py:31
  289.7 18.7 %collective-permute-start.48 = (bf16[1,4,40,1152]{3,2,1,0:T(8,128)(2,1)S(1)}, bf16[1,4,40,1152]{3,2,1,0:T(8,128)(2,1)S(1)}, u32[]{:S(2)}, u32[]{:S(2)}) collective-permute-start(bf16[1,4,40,1152]{3,2,1,0:T(8,128)(2,1)S(1)} %get-tuple-element.472), channel_id=1, source_target_pairs={{0,8},{8,0},{16,24},{24,16},{1,9},{9,1},{17,25},{25,17},{2,10},{10... | collective-permute-start | bytes 1105928 | tf_op jit(solution)/shard_map/ppermute | solution.py:31
  311.7 16.5 %collective-permute-start.54 = (bf16[1,4,40,1152]{3,2,1,0:T(8,128)(2,1)}, bf16[1,4,40,1152]{3,2,1,0:T(8,128)(2,1)}, u32[]{:S(2)}, u32[]{:S(2)}) collective-permute-start(bf16[1,4,40,1152]{3,2,1,0:T(8,128)(2,1)} %get-tuple-element.468), channel_id=1, source_target_pairs={{0,16},{8,24},{16,0},{24,8},{1,17},{9,25},{17,1},{25,9},{2,18},{10... | collective-permute-start | bytes 1105928 | tf_op jit(solution)/shard_map/ppermute | solution.py:31
  317.0 20.9 %collective-permute-start.53 = (bf16[320,1024]{1,0:T(8,128)(2,1)}, bf16[320,1024]{1,0:T(8,128)(2,1)S(1)}, u32[]{:S(2)}, u32[]{:S(2)}) collective-permute-start(bf16[320,1024]{1,0:T(8,128)(2,1)} %add_convert_fusion.9), channel_id=1, source_target_pairs={{0,2},{1,3},{2,0},{3,1},{4,6},{5,7},{6,4},{7,5},{8,10},{9,11},{10,... | collective-permute-start | bytes 1966088 | tf_op jit(solution)/shard_map/ppermute | solution.py:31
  350.8 19.1 %collective-permute-start.62 = (bf16[2,2,40,1024]{3,2,1,0:T(8,128)(2,1)}, bf16[2,2,40,1024]{3,2,1,0:T(8,128)(2,1)}, u32[]{:S(2)}, u32[]{:S(2)}) collective-permute-start(bf16[2,2,40,1024]{3,2,1,0:T(8,128)(2,1)} %get-tuple-element.500), channel_id=1, source_target_pairs={{0,4},{1,5},{2,6},{3,7},{4,0},{5,1},{6,2},{7,3},{8,12},{9,13},{10,... | collective-permute-start | bytes 983048 | tf_op jit(solution)/shard_map/ppermute | solution.py:31
  353.3 16.7 %collective-permute-start.63 = (bf16[4,1,40,1024]{3,2,0,1:T(8,128)(2,1)}, bf16[4,1,40,1024]{3,2,0,1:T(8,128)(2,1)}, u32[]{:S(2)}, u32[]{:S(2)}) collective-permute-start(bf16[4,1,40,1024]{3,2,0,1:T(8,128)(2,1)} %get-tuple-element.498), channel_id=1, source_target_pairs={{0,8},{8,0},{16,24},{24,16},{1,9},{9,1},{17,25},{25,17},{2,10},{10... | collective-permute-start | bytes 983048 | tf_op jit(solution)/shard_map/ppermute | solution.py:31
  355.0 22.0 %collective-permute-start.61 = (bf16[8,320,128]{2,1,0:T(8,128)(2,1)}, bf16[8,320,128]{2,1,0:T(8,128)(2,1)}, u32[]{:S(2)}, u32[]{:S(2)}) collective-permute-start(bf16[8,320,128]{2,1,0:T(8,128)(2,1)} %add_convert_fusion.7), channel_id=1, source_target_pairs={{0,8},{8,0},{16,24},{24,16},{1,9},{9,1},{17,25},{25,17},{2,10},{10... | collective-permute-start | bytes 1966088 | tf_op jit(solution)/shard_map/ppermute | solution.py:31
  357.7 24.0 %collective-permute-start.57 = (bf16[8,352,128]{2,1,0:T(8,128)(2,1)}, bf16[8,352,128]{2,1,0:T(8,128)(2,1)}, u32[]{:S(2)}, u32[]{:S(2)}) collective-permute-start(bf16[8,352,128]{2,1,0:T(8,128)(2,1)} %add_convert_fusion.5), channel_id=1, source_target_pairs={{0,2},{1,3},{2,0},{3,1},{4,6},{5,7},{6,4},{7,5},{8,10},{9,11},{10,... | collective-permute-start | bytes 2162696 | tf_op jit(solution)/shard_map/ppermute | solution.py:31
  360.3 21.4 %collective-permute-start.59 = (bf16[8,352,128]{2,1,0:T(8,128)(2,1)}, bf16[8,352,128]{2,1,0:T(8,128)(2,1)}, u32[]{:S(2)}, u32[]{:S(2)}) collective-permute-start(bf16[8,352,128]{2,1,0:T(8,128)(2,1)} %add_convert_fusion.4), channel_id=1, source_target_pairs={{0,16},{8,24},{16,0},{24,8},{1,17},{9,25},{17,1},{25,9},{2,18},{10... | collective-permute-start | bytes 2162696 | tf_op jit(solution)/shard_map/ppermute | solution.py:31
  385.4 22.9 %collective-permute-start.65 = (bf16[4,352,128]{2,1,0:T(8,128)(2,1)S(1)}, bf16[4,352,128]{2,1,0:T(8,128)(2,1)S(1)}, u32[]{:S(2)}, u32[]{:S(2)}) collective-permute-start(bf16[4,352,128]{2,1,0:T(8,128)(2,1)S(1)} %add_convert_fusion.13), channel_id=1, source_target_pairs={{0,8},{8,0},{16,24},{24,16},{1,9},{9,1},{17,25},{25,17},{2,10},{10... | collective-permute-start | bytes 1081352 | tf_op jit(solution)/shard_map/ppermute | solution.py:31
  387.3 21.0 %collective-permute-start.64 = (bf16[4,352,128]{2,1,0:T(8,128)(2,1)S(1)}, bf16[4,352,128]{2,1,0:T(8,128)(2,1)S(1)}, u32[]{:S(2)}, u32[]{:S(2)}) collective-permute-start(bf16[4,352,128]{2,1,0:T(8,128)(2,1)S(1)} %add_convert_fusion.14), channel_id=1, source_target_pairs={{0,16},{8,24},{16,0},{24,8},{1,17},{9,25},{17,1},{25,9},{2,18},{10... | collective-permute-start | bytes 1081352 | tf_op jit(solution)/shard_map/ppermute | solution.py:31
  (192 other events, 1618.4 us)
